TPU v7x, 32 devices: a whole 2x2x4 slice. The times are simulated.
32 devices in a mesh: shots: 2 (over x), depth: 8 (over z, y), freq: 2 (over core).
Axes of the slice: x: 2, y: 2, z: 4, core: 2. Of those that a mesh axis runs over, the one named last changes fastest.
Arguments:
- surface: float32 [2, 4, 2, 128, 256], P('shots', 'freq'), parts along dimension 0, may hold values from -2.1 to 2.1
- bins: int32 [8, 128, 128], P('depth'), may hold values from 0 to 7
- stencil: float32 [4, 8, 5], P('freq'), may hold values from 0.25 to 1
- phase_step: float32 [4, 8], P('freq'), may hold values from 0.3 to 1.4
- phase_shift: float32 [4, 8], P('freq'), may hold values from -3.140625 to 3.140625
- lags: int32 [4], replicated, may hold values from 0 to 7, as said below
Outputs:
- image: float32 [8, 8, 16384], P('depth', 'shots', 'freq'), parts along dimension 1
There are 2 independent parts, one for each index of `shots`. A program takes and returns all parts, laid end to end along the dimension named above; an argument that names none is the same for every part. Nothing has to cross between parts.
Inputs may be any that keep to these rules, and one draw needn't show every extreme that they name: `lags`: 4 distinct half-offsets in cells; one of them is 7.
All inputs are finite; a program needn't handle non-finite values.
Results may differ from a plain program's by a relative error of at most 0.0003.
Values sent between devices are 32-bit elements; how exact they have to be, the bound alone decides.
No kernel may reach another device: no remote copies, remote signals or barrier semaphores. Data moves between devices by JAX's collectives and lax.ppermute only.
A program may use at most 64 MiB of HBM per device.

v0:
```python
import math

import jax
import jax.numpy as jnp
from jax import lax
from jax.sharding import PartitionSpec as P

KERNELS = 8
TAPS = 13
HALF = 6
LAGS = 4
HMAX = 7


column_tile = 16


def from_behind(value, axis, steps):
    count = lax.axis_size(axis)
    initial, last = (max(0, -steps), min(count, count - steps))
    return lax.ppermute(value, axis, [(source, source + steps) for source in range(initial, last)])


def kernel_taps(stencil, phase_step, phase_shift):
    center = stencil[..., 0]
    along_x = stencil[..., 1]
    along_y = stencil[..., 2]
    diag_main = stencil[..., 3]
    diag_anti = stencil[..., 4]
    row_above = jnp.stack([diag_main, along_y, diag_anti], -1)
    row_middle = jnp.stack([along_x, center, along_x], -1)
    row_below = jnp.stack([diag_anti, along_y, diag_main], -1)
    stencil_grid = jnp.stack([row_above, row_middle, row_below], -2)
    weight_sum = center + 2.0 * (along_x + along_y + diag_main + diag_anti)
    stencil_grid = stencil_grid * (phase_step / weight_sum)[..., None, None]
    lead = stencil.shape[:-1]
    tap_rows = lax.broadcasted_iota(jnp.int32, (TAPS, TAPS), 0)
    tap_cols = lax.broadcasted_iota(jnp.int32, (TAPS, TAPS), 1)
    unit_tap = ((tap_rows == HALF) & (tap_cols == HALF)).astype(jnp.float32)
    power = jnp.broadcast_to(unit_tap, lead + (TAPS, TAPS))
    real_sum = power
    imag_sum = jnp.zeros(lead + (TAPS, TAPS), jnp.float32)
    pad_spec = [(0, 0)] * len(lead) + [(1, 1), (1, 1)]
    for order in range(1, HALF + 1):
        padded = jnp.pad(power, pad_spec)
        grown = jnp.zeros(lead + (TAPS, TAPS), jnp.float32)
        for row_off in range(3):
            for col_off in range(3):
                piece = padded[
                    ..., 2 - row_off : 2 - row_off + TAPS, 2 - col_off : 2 - col_off + TAPS
                ]
                grown = grown + stencil_grid[..., row_off, col_off, None, None] * piece
        power = grown
        weighted = power * (1.0 / math.factorial(order))
        if order % 4 == 1:
            imag_sum = imag_sum + weighted
        elif order % 4 == 2:
            real_sum = real_sum - weighted
        elif order % 4 == 3:
            imag_sum = imag_sum - weighted
        else:
            real_sum = real_sum + weighted
    cosine = jnp.cos(phase_shift)[..., None, None]
    sine = jnp.sin(phase_shift)[..., None, None]
    return (cosine * real_sum - sine * imag_sum, sine * real_sum + cosine * imag_sum)


def advance_level(fields, weights, selector):
    field_count = fields.shape[0]
    grid_width = fields.shape[1]
    tiles = grid_width // column_tile
    parts = fields.reshape(field_count, grid_width, 2, grid_width)
    padded = jnp.pad(parts, ((0, 0), (HALF, HALF), (0, 0), (HALF, column_tile - HALF)))
    main = padded[..., :grid_width].reshape(
        field_count, grid_width + 2 * HALF, 2, tiles, column_tile
    )
    after = padded[..., column_tile : grid_width + column_tile].reshape(
        field_count, grid_width + 2 * HALF, 2, tiles, column_tile
    )
    windows = jnp.concatenate([main, after[..., : 2 * HALF]], -1)
    windows = jnp.transpose(windows, (0, 1, 3, 2, 4))
    patches = jnp.stack(
        [windows[:, row_tap : row_tap + grid_width] for row_tap in range(TAPS)], axis=3
    )
    patches = patches.reshape(field_count * grid_width * tiles, TAPS * 2 * (column_tile + 2 * HALF))
    result = jnp.dot(
        patches, weights, precision=lax.Precision.HIGHEST, preferred_element_type=jnp.float32
    )
    result = result.reshape(field_count, grid_width, tiles, KERNELS, 2, column_tile)
    chosen = jnp.sum(result * selector[None], axis=3)
    return jnp.transpose(chosen, (0, 1, 3, 2, 4)).reshape(field_count, grid_width, 2 * grid_width)


def image_terms(source, receiver, lags):
    grid_width = source.shape[0]
    source_parts = jnp.pad(
        source.reshape(grid_width, 2, grid_width), ((0, 0), (0, 0), (HMAX, HMAX))
    )
    receiver_parts = jnp.pad(
        receiver.reshape(grid_width, 2, grid_width), ((0, 0), (0, 0), (HMAX, HMAX))
    )
    lag_terms = []
    for lag_index in range(LAGS):
        offset = lags[lag_index]
        shifted_source = lax.dynamic_slice_in_dim(source_parts, HMAX - offset, grid_width, 2)
        shifted_receiver = lax.dynamic_slice_in_dim(receiver_parts, HMAX + offset, grid_width, 2)
        lag_terms.append(jnp.sum(shifted_source * shifted_receiver, axis=1))
    return jnp.stack(lag_terms)


def body(surface, bins, stencil, phase_step, phase_shift, lags):
    shot_count = surface.shape[0]
    freq_count = surface.shape[1]
    grid_width = surface.shape[3]
    slab_steps = bins.shape[0]
    tiles = grid_width // column_tile
    window_width = column_tile + 2 * HALF
    depth_count = lax.axis_size("depth")
    depth_index = lax.axis_index("depth")
    kern_real, kern_imag = kernel_taps(stencil, phase_step, phase_shift)
    mixing = jnp.stack(
        [jnp.stack([kern_real, kern_imag], 1), jnp.stack([-kern_imag, kern_real], 1)], 1
    )
    window_ids = lax.broadcasted_iota(jnp.int32, (window_width, column_tile, TAPS), 0)
    out_ids = lax.broadcasted_iota(jnp.int32, (window_width, column_tile, TAPS), 1)
    tap_ids = lax.broadcasted_iota(jnp.int32, (window_width, column_tile, TAPS), 2)
    shift_table = (window_ids == out_ids + tap_ids).astype(jnp.float32)
    all_weights = jnp.einsum(
        "fpqkab,cwb->fapckqw", mixing, shift_table, precision=lax.Precision.HIGHEST
    )
    all_weights = all_weights.reshape(
        freq_count, TAPS * 2 * window_width, KERNELS * 2 * column_tile
    )
    kernel_ids = lax.broadcasted_iota(jnp.int32, (1, 1, 1, KERNELS, 1, 1), 3)
    selectors = (
        bins.reshape(slab_steps, grid_width, tiles, 1, 1, column_tile) == kernel_ids
    ).astype(jnp.float32)
    image_part = jnp.zeros((slab_steps, LAGS, grid_width, grid_width), jnp.float32)
    front_count = shot_count * freq_count

    def advance_turn(step_index, carry):
        sent, image_now = carry
        received = from_behind(sent, "depth", 1)
        front_index = step_index - depth_index
        active = (front_index >= 0) & (front_index < front_count)
        clipped = jnp.clip(front_index, 0, front_count - 1)
        shot_index = clipped // freq_count
        freq_index = clipped % freq_count
        shot_fields = lax.dynamic_index_in_dim(surface, shot_index, 0, keepdims=False)
        surface_front = lax.dynamic_index_in_dim(shot_fields, freq_index, 0, keepdims=False)
        incoming = jnp.where(depth_index == 0, surface_front, received)
        weights_front = lax.dynamic_index_in_dim(all_weights, freq_index, 0, keepdims=False)

        def compute_front(state):
            fields, image_held = state
            fields = advance_level(fields, weights_front, selectors[0])
            level_terms = [image_terms(fields[0], fields[1], lags)]
            return (fields, image_held + jnp.stack(level_terms))

        def keep_state(state):
            return state

        return lax.cond(active, compute_front, keep_state, (incoming, image_now))

    start = (jnp.zeros((2, grid_width, 2 * grid_width), jnp.float32), image_part)
    final_sent, image_part = lax.fori_loop(0, depth_count + front_count - 1, advance_turn, start)
    image_part = image_part.reshape(slab_steps, LAGS, grid_width * grid_width)
    return lax.psum_scatter(image_part, "freq", scatter_dimension=2, tiled=True)


def solution(mesh):
    return jax.shard_map(
        body,
        mesh=mesh,
        in_specs=(
            P("shots", "freq", None, None, None),
            P("depth", None, None),
            P("freq", None, None),
            P("freq", None),
            P("freq", None),
            P(),
        ),
        out_specs=P("depth", "shots", "freq"),
        check_vma=False,
    )
```

profile of v0, /device:TPU:1, one launch (start us, length us, event | category | flops | bytes accessed | tf_op | source)
XLA Modules:
  0.0 383.3 jit_solution(565116637435025677)
XLA Ops:
  6.5 0.7 fusion.78
  7.3 0.7 fusion.79
  8.0 0.8 bitcast_divide_fusion
  8.9 0.4 fusion.39
  9.3 0.4 multiply_add_fusion.5
  9.7 0.4 multiply_add_fusion.4
  10.2 0.4 multiply_add_fusion.3
  10.6 0.4 multiply_add_fusion.2
  11.0 0.7 fusion.80
  11.8 1.1 fusion.74
  13.0 5.6 %convolution_bitcast_fusion = f32[2,13,2,28,8,2,16]{3,1,4,5,2,0,6:T(8,128)} fusion(f32[2,1,2,8,13,13]{5,4,3,2,1,0:T(8,128)S(1)} %get-tuple-element.337, f32[2,1,2,8,13,13]{5,4,3,2,1,0:T(8,128)S(1)} %get-tuple-element.336), kind=kOutput, calls=%fused_computation.56 | convolution fusion | flops 58169280 | bytes 1534208 | tf_op jit(solution)/shard_map/fpqkab,cwb->fapckqw/dot_general | solution.py:128
  18.6 11.5 %copy.36 = f32[2,13,2,28,8,2,16]{3,2,1,6,5,4,0:T(2,128)} copy(f32[2,13,2,28,8,2,16]{3,1,4,5,2,0,6:T(8,128)} %convolution_bitcast_fusion) | data formatting | bytes 2981888 | tf_op jit(solution)/shard_map/fpqkab,cwb->fapckqw/transpose | solution.py:128
  30.1 6.1 %reshape.91 = f32[2,728,256]{1,2,0:T(8,128)S(1)} reshape(f32[2,13,2,28,8,2,16]{3,2,1,6,5,4,0:T(2,128)} %copy.36) | data formatting | bytes 2981888 | tf_op jit(solution)/shard_map/reshape | solution.py:131
  36.4 199.5 %while.18 = (s32[]{:T(128)}, f32[2,128,256]{1,2,0:T(8,128)S(1)}, f32[1,4,128,128]{2,3,1,0:T(8,128)S(1)}, s32[]{:T(128)}, pred[]{:T(512)}, /*index=5*/f32[1,2,2,1...) while((s32[]{:T(128)}, f32[2,128,256]{1,2,0:T(8,128)S(1)}, ...), condition=%wide.region_8.9_spmd.clone, body=%wide.region_0.8_spmd.clone.sunk | while | flops 4582074880 | bytes 42677048 | solution.py:166
  36.6 4.0 %collective-permute-start = (f32[2,128,256]{1,2,0:T(8,128)S(1)}, f32[2,128,256]{1,2,0:T(8,128)S(1)}, u32[]{:S(2)}, u32[]{:S(2)}) collective-permute-start(f32[2,128,256]{1,2,0:T(8,128)S(1)} %get-tuple-element.434), channel_id=1, source_target_pairs={{0,2},{2,4},{4,6},{6,8},{8,10},{10,12},{12,14},{1,3},{3,5},{5,7},{... | collective-permute-start | bytes 786440 | tf_op jit(solution)/shard_map/while/body/eval_jaxpr/ppermute | solution.py:21
  40.9 4.7 %collective-permute-done = f32[2,128,256]{1,2,0:T(8,128)S(1)} collective-permute-done((f32[2,128,256]{1,2,0:T(8,128)S(1)}, f32[2,128,256]{1,2,0:T(8,128)S(1)}, u32[]{:S(2)}, u32[]{:S(2)}) %collective-permute-start) | collective-permute-done | bytes 262176 | tf_op jit(solution)/shard_map/while/body/eval_jaxpr/ppermute | solution.py:21
  45.6 26.1 %conditional.3 = ((f32[2,128,256]{1,2,0:T(8,128)S(1)}, f32[1,4,128,128]{2,3,1,0:T(8,128)S(1)})) conditional(s32[]{:T(128)} %convert_element_type.53, (f32[2,128,256]{1,2,0:T(8,128)S(1)}, f32[1,4,128,128]{2,3,1,0:T(8,128)S(1)}) %tuple.81, (f32[2,128,256]{1,2,0:T(8,128)S(1)}, f32[2,728,256]{1,2,0:T(8,128)S(1)}, s32[]{:T(128)}, ...), branch_computations={%region_1.1_spmd, %region_2.7_spmd} | conditional | flops 4581747200 | bytes 39203260 | solution.py:163
  45.6 0.3 pad_slice_fusion.1
  46.3 0.2 fusion.16
  46.5 0.2 fusion.15
  46.7 0.2 fusion.14
  46.9 0.2 fusion.13
  47.1 0.2 fusion.12
  47.3 0.2 fusion.11
  47.5 0.2 fusion.10
  47.7 0.2 fusion.9
  48.0 0.2 fusion.8
  48.2 0.2 fusion.7
  48.4 0.2 fusion.6
  48.6 5.7 %copy.29 = f32[2,128,8,13,2,28]{1,2,5,4,3,0:T(8,128)S(1)} copy(f32[2,128,8,13,2,28]{1,5,2,4,0,3:T(8,128)S(1)} %fusion.6) | data formatting | bytes 11927552 | tf_op jit(solution)/shard_map/while/body/eval_jaxpr/cond/branch_1_fun/stack | solution.py:82
  54.3 6.3 %multiply_reduce_fusion = f32[2,128,8,2,16]{1,4,3,2,0:T(8,128)S(1)} fusion(f32[8,2,16,728,1,1]{3,2,1,0,5,4:T(8,128)S(1)} %bitcast.171, f32[2,128,8,728,1,1]{1,2,3,0,5,4:T(8,128)S(1)} %bitcast.165, f32[128,8,8,16]{0,3,2,1:T(8,128)S(1)} %bitcast.172), kind=kOutput, calls=%fused_computation.3 | convolution fusion | flops 4581163008 | bytes 7495680 | tf_op jit(solution)/shard_map/while/body/eval_jaxpr/cond/branch_1_fun/dot_general | solution.py:86
  60.7 0.7 fusion.77
  71.7 1.3 collective-permute-start
  73.3 4.1 %collective-permute-done = f32[2,128,256]{1,2,0:T(8,128)S(1)} collective-permute-done((f32[2,128,256]{1,2,0:T(8,128)S(1)}, f32[2,128,256]{1,2,0:T(8,128)S(1)}, u32[]{:S(2)}, u32[]{:S(2)}) %collective-permute-start) | collective-permute-done | bytes 262176 | tf_op jit(solution)/shard_map/while/body/eval_jaxpr/ppermute | solution.py:21
  77.4 26.1 %conditional.3 = ((f32[2,128,256]{1,2,0:T(8,128)S(1)}, f32[1,4,128,128]{2,3,1,0:T(8,128)S(1)})) conditional(s32[]{:T(128)} %convert_element_type.53, (f32[2,128,256]{1,2,0:T(8,128)S(1)}, f32[1,4,128,128]{2,3,1,0:T(8,128)S(1)}) %tuple.81, (f32[2,128,256]{1,2,0:T(8,128)S(1)}, f32[2,728,256]{1,2,0:T(8,128)S(1)}, s32[]{:T(128)}, ...), branch_computations={%region_1.1_spmd, %region_2.7_spmd} | conditional | flops 4581747200 | bytes 39203260 | solution.py:163
  77.4 0.3 pad_slice_fusion.1
  78.1 0.2 fusion.16
  78.3 0.2 fusion.15
  78.5 0.2 fusion.14
  78.7 0.2 fusion.13
  78.9 0.2 fusion.12
  79.2 0.2 fusion.11
  79.4 0.2 fusion.10
  80.2 0.2 fusion.6
  80.4 5.7 %copy.29 = f32[2,128,8,13,2,28]{1,2,5,4,3,0:T(8,128)S(1)} copy(f32[2,128,8,13,2,28]{1,5,2,4,0,3:T(8,128)S(1)} %fusion.6) | data formatting | bytes 11927552 | tf_op jit(solution)/shard_map/while/body/eval_jaxpr/cond/branch_1_fun/stack | solution.py:82
  86.1 6.3 %multiply_reduce_fusion = f32[2,128,8,2,16]{1,4,3,2,0:T(8,128)S(1)} fusion(f32[8,2,16,728,1,1]{3,2,1,0,5,4:T(8,128)S(1)} %bitcast.171, f32[2,128,8,728,1,1]{1,2,3,0,5,4:T(8,128)S(1)} %bitcast.165, f32[128,8,8,16]{0,3,2,1:T(8,128)S(1)} %bitcast.172), kind=kOutput, calls=%fused_computation.3 | convolution fusion | flops 4581163008 | bytes 7495680 | tf_op jit(solution)/shard_map/while/body/eval_jaxpr/cond/branch_1_fun/dot_general | solution.py:86
  92.5 0.7 fusion.77
  103.5 4.1 %collective-permute-start = (f32[2,128,256]{1,2,0:T(8,128)S(1)}, f32[2,128,256]{1,2,0:T(8,128)S(1)}, u32[]{:S(2)}, u32[]{:S(2)}) collective-permute-start(f32[2,128,256]{1,2,0:T(8,128)S(1)} %get-tuple-element.434), channel_id=1, source_target_pairs={{0,2},{2,4},{4,6},{6,8},{8,10},{10,12},{12,14},{1,3},{3,5},{5,7},{... | collective-permute-start | bytes 786440 | tf_op jit(solution)/shard_map/while/body/eval_jaxpr/ppermute | solution.py:21
  107.9 3.3 collective-permute-done
  111.2 30.2 %collective-permute-start = (f32[2,128,256]{1,2,0:T(8,128)S(1)}, f32[2,128,256]{1,2,0:T(8,128)S(1)}, u32[]{:S(2)}, u32[]{:S(2)}) collective-permute-start(f32[2,128,256]{1,2,0:T(8,128)S(1)} %get-tuple-element.434), channel_id=1, source_target_pairs={{0,2},{2,4},{4,6},{6,8},{8,10},{10,12},{12,14},{1,3},{3,5},{5,7},{... | collective-permute-start | bytes 786440 | tf_op jit(solution)/shard_map/while/body/eval_jaxpr/ppermute | solution.py:21
  141.7 3.0 collective-permute-done
  144.8 3.8 collective-permute-start
  148.9 3.0 collective-permute-done
  152.0 30.1 %collective-permute-start = (f32[2,128,256]{1,2,0:T(8,128)S(1)}, f32[2,128,256]{1,2,0:T(8,128)S(1)}, u32[]{:S(2)}, u32[]{:S(2)}) collective-permute-start(f32[2,128,256]{1,2,0:T(8,128)S(1)} %get-tuple-element.434), channel_id=1, source_target_pairs={{0,2},{2,4},{4,6},{6,8},{8,10},{10,12},{12,14},{1,3},{3,5},{5,7},{... | collective-permute-start | bytes 786440 | tf_op jit(solution)/shard_map/while/body/eval_jaxpr/ppermute | solution.py:21
  182.3 3.0 collective-permute-done
  185.4 4.7 %collective-permute-start = (f32[2,128,256]{1,2,0:T(8,128)S(1)}, f32[2,128,256]{1,2,0:T(8,128)S(1)}, u32[]{:S(2)}, u32[]{:S(2)}) collective-permute-start(f32[2,128,256]{1,2,0:T(8,128)S(1)} %get-tuple-element.434), channel_id=1, source_target_pairs={{0,2},{2,4},{4,6},{6,8},{8,10},{10,12},{12,14},{1,3},{3,5},{5,7},{... | collective-permute-start | bytes 786440 | tf_op jit(solution)/shard_map/while/body/eval_jaxpr/ppermute | solution.py:21
  190.4 3.0 collective-permute-done
  193.5 27.1 %collective-permute-start = (f32[2,128,256]{1,2,0:T(8,128)S(1)}, f32[2,128,256]{1,2,0:T(8,128)S(1)}, u32[]{:S(2)}, u32[]{:S(2)}) collective-permute-start(f32[2,128,256]{1,2,0:T(8,128)S(1)} %get-tuple-element.434), channel_id=1, source_target_pairs={{0,2},{2,4},{4,6},{6,8},{8,10},{10,12},{12,14},{1,3},{3,5},{5,7},{... | collective-permute-start | bytes 786440 | tf_op jit(solution)/shard_map/while/body/eval_jaxpr/ppermute | solution.py:21
  220.8 3.0 collective-permute-done
  224.0 6.3 %collective-permute-start = (f32[2,128,256]{1,2,0:T(8,128)S(1)}, f32[2,128,256]{1,2,0:T(8,128)S(1)}, u32[]{:S(2)}, u32[]{:S(2)}) collective-permute-start(f32[2,128,256]{1,2,0:T(8,128)S(1)} %get-tuple-element.434), channel_id=1, source_target_pairs={{0,2},{2,4},{4,6},{6,8},{8,10},{10,12},{12,14},{1,3},{3,5},{5,7},{... | collective-permute-start | bytes 786440 | tf_op jit(solution)/shard_map/while/body/eval_jaxpr/ppermute | solution.py:21
  230.5 5.4 %collective-permute-done = f32[2,128,256]{1,2,0:T(8,128)S(1)} collective-permute-done((f32[2,128,256]{1,2,0:T(8,128)S(1)}, f32[2,128,256]{1,2,0:T(8,128)S(1)}, u32[]{:S(2)}, u32[]{:S(2)}) %collective-permute-start) | collective-permute-done | bytes 262176 | tf_op jit(solution)/shard_map/while/body/eval_jaxpr/ppermute | solution.py:21
  236.0 7.7 %copy.47 = f32[1,4,128,128]{1,3,2,0:T(8,128)} copy(f32[1,4,128,128]{2,3,1,0:T(8,128)S(1)} %get-tuple-element.259) | data formatting | bytes 524288
  243.6 124.1 %reduce-scatter.4.cloned.1.call-done = f32[8192,4]{1,0:T(8,128)} async-done(((f32[16384,4]{1,0:T(8,128)}), f32[8192,4]{1,0:T(8,128)}) %reduce-scatter.4.cloned.1.call-update) | async-done | bytes 131088
  367.8 8.6 %copy.46 = f32[1,4,8192]{2,1,0:T(4,128)} copy(f32[1,4,8192]{1,0,2:T(1,128)} %bitcast.181) | data formatting | bytes 262144
  (85 shorter events, 4.4 us)
Async XLA Ops:
  6.5 361.2 %reduce-scatter.4.cloned.1.call-start = ((), (), s32[]{:S(2)}) async-start(), calls=%async_computation.1 | async-start | bytes 12582912
  30.1 6.1 %copy-start.2 = (s32[1,128,128]{2,1,0:T(8,128)S(1)}, s32[1,128,128]{2,1,0:T(8,128)}, u32[]{:S(2)}) copy-start(s32[1,128,128]{2,1,0:T(8,128)} %param.11) | copy-start | bytes 196612
  30.1 6.3 %copy-start = (f32[1,2,2,128,256]{4,3,2,1,0:T(8,128)S(1)}, f32[1,2,2,128,256]{4,3,2,1,0:T(8,128)}, u32[]{:S(2)}) copy-start(f32[1,2,2,128,256]{4,3,2,1,0:T(8,128)} %param.10) | copy-start | bytes 1572868
  30.1 6.3 %copy-start.1 = (s32[4]{0:T(128)S(1)}, s32[4]{0:T(128)}, u32[]{:S(2)}) copy-start(s32[4]{0:T(128)} %param.15) | copy-start | bytes 52
  36.6 8.9 %collective-permute-start = (f32[2,128,256]{1,2,0:T(8,128)S(1)}, f32[2,128,256]{1,2,0:T(8,128)S(1)}, u32[]{:S(2)}, u32[]{:S(2)}) collective-permute-start(f32[2,128,256]{1,2,0:T(8,128)S(1)} %get-tuple-element.434), channel_id=1, source_target_pairs={{0,2},{2,4},{4,6},{6,8},{8,10},{10,12},{12,14},{1,3},{3,5},{5,7},{... | collective-permute-start | bytes 786440 | tf_op jit(solution)/shard_map/while/body/eval_jaxpr/ppermute | solution.py:21
  71.7 5.7 %collective-permute-start = (f32[2,128,256]{1,2,0:T(8,128)S(1)}, f32[2,128,256]{1,2,0:T(8,128)S(1)}, u32[]{:S(2)}, u32[]{:S(2)}) collective-permute-start(f32[2,128,256]{1,2,0:T(8,128)S(1)} %get-tuple-element.434), channel_id=1, source_target_pairs={{0,2},{2,4},{4,6},{6,8},{8,10},{10,12},{12,14},{1,3},{3,5},{5,7},{... | collective-permute-start | bytes 786440 | tf_op jit(solution)/shard_map/while/body/eval_jaxpr/ppermute | solution.py:21
  103.5 7.6 %collective-permute-start = (f32[2,128,256]{1,2,0:T(8,128)S(1)}, f32[2,128,256]{1,2,0:T(8,128)S(1)}, u32[]{:S(2)}, u32[]{:S(2)}) collective-permute-start(f32[2,128,256]{1,2,0:T(8,128)S(1)} %get-tuple-element.434), channel_id=1, source_target_pairs={{0,2},{2,4},{4,6},{6,8},{8,10},{10,12},{12,14},{1,3},{3,5},{5,7},{... | collective-permute-start | bytes 786440 | tf_op jit(solution)/shard_map/while/body/eval_jaxpr/ppermute | solution.py:21
  111.2 33.5 %collective-permute-start = (f32[2,128,256]{1,2,0:T(8,128)S(1)}, f32[2,128,256]{1,2,0:T(8,128)S(1)}, u32[]{:S(2)}, u32[]{:S(2)}) collective-permute-start(f32[2,128,256]{1,2,0:T(8,128)S(1)} %get-tuple-element.434), channel_id=1, source_target_pairs={{0,2},{2,4},{4,6},{6,8},{8,10},{10,12},{12,14},{1,3},{3,5},{5,7},{... | collective-permute-start | bytes 786440 | tf_op jit(solution)/shard_map/while/body/eval_jaxpr/ppermute | solution.py:21
  144.8 7.1 %collective-permute-start = (f32[2,128,256]{1,2,0:T(8,128)S(1)}, f32[2,128,256]{1,2,0:T(8,128)S(1)}, u32[]{:S(2)}, u32[]{:S(2)}) collective-permute-start(f32[2,128,256]{1,2,0:T(8,128)S(1)} %get-tuple-element.434), channel_id=1, source_target_pairs={{0,2},{2,4},{4,6},{6,8},{8,10},{10,12},{12,14},{1,3},{3,5},{5,7},{... | collective-permute-start | bytes 786440 | tf_op jit(solution)/shard_map/while/body/eval_jaxpr/ppermute | solution.py:21
  152.0 33.4 %collective-permute-start = (f32[2,128,256]{1,2,0:T(8,128)S(1)}, f32[2,128,256]{1,2,0:T(8,128)S(1)}, u32[]{:S(2)}, u32[]{:S(2)}) collective-permute-start(f32[2,128,256]{1,2,0:T(8,128)S(1)} %get-tuple-element.434), channel_id=1, source_target_pairs={{0,2},{2,4},{4,6},{6,8},{8,10},{10,12},{12,14},{1,3},{3,5},{5,7},{... | collective-permute-start | bytes 786440 | tf_op jit(solution)/shard_map/while/body/eval_jaxpr/ppermute | solution.py:21
  185.4 8.0 %collective-permute-start = (f32[2,128,256]{1,2,0:T(8,128)S(1)}, f32[2,128,256]{1,2,0:T(8,128)S(1)}, u32[]{:S(2)}, u32[]{:S(2)}) collective-permute-start(f32[2,128,256]{1,2,0:T(8,128)S(1)} %get-tuple-element.434), channel_id=1, source_target_pairs={{0,2},{2,4},{4,6},{6,8},{8,10},{10,12},{12,14},{1,3},{3,5},{5,7},{... | collective-permute-start | bytes 786440 | tf_op jit(solution)/shard_map/while/body/eval_jaxpr/ppermute | solution.py:21
  193.5 30.4 %collective-permute-start = (f32[2,128,256]{1,2,0:T(8,128)S(1)}, f32[2,128,256]{1,2,0:T(8,128)S(1)}, u32[]{:S(2)}, u32[]{:S(2)}) collective-permute-start(f32[2,128,256]{1,2,0:T(8,128)S(1)} %get-tuple-element.434), channel_id=1, source_target_pairs={{0,2},{2,4},{4,6},{6,8},{8,10},{10,12},{12,14},{1,3},{3,5},{5,7},{... | collective-permute-start | bytes 786440 | tf_op jit(solution)/shard_map/while/body/eval_jaxpr/ppermute | solution.py:21
  224.0 11.9 %collective-permute-start = (f32[2,128,256]{1,2,0:T(8,128)S(1)}, f32[2,128,256]{1,2,0:T(8,128)S(1)}, u32[]{:S(2)}, u32[]{:S(2)}) collective-permute-start(f32[2,128,256]{1,2,0:T(8,128)S(1)} %get-tuple-element.434), channel_id=1, source_target_pairs={{0,2},{2,4},{4,6},{6,8},{8,10},{10,12},{12,14},{1,3},{3,5},{5,7},{... | collective-permute-start | bytes 786440 | tf_op jit(solution)/shard_map/while/body/eval_jaxpr/ppermute | solution.py:21
Sparse Core Ops, SparseCore 0:
  243.8 123.9 reduce-scatter.3
where the time goes:
time: 384 us; the launch traced here: 383 us
  waiting for transfers between devices  157 us (41%)
  starting transfers between devices  112 us (29%)
  local copies, waits for them, and re-layouts  56.1 us (15%)
  loops' own time  21.4 us (6%)
  matrix products  18.2 us (5%)
  between operations  13.5 us (4%)
  other arithmetic  5.48 us (1%)
    unnamed x2, waiting for transfers between devices  124 us
    ppermute x9, starting transfers between devices, from_behind(): lax.ppermute(value, axis, [(source, source + steps) for source in range(i...  112 us
    ppermute x9, waiting for transfers between devices, from_behind(): lax.ppermute(value, axis, [(source, source + steps) for source in range(i...  32.8 us
    another operation x9, loops' own time, advance_turn(): return lax.cond(active, compute_front, keep_state, (incoming, image_now))  20.5 us
    unnamed x9, local copies, waits for them, and re-layouts  16.4 us
    dot_general x2, matrix products, advance_level(): jnp.dot(patches, weights, precision=lax.Precision.HIGHEST, preferred_elem...  12.6 us
    another operation x4, local copies, waits for them, and re-layouts, advance_level(): jnp.stack([windows[:, row_tap:row_tap + grid_width] for row_tap in range(...  11.8 us
    transpose x1, local copies, waits for them, and re-layouts, body(): jnp.einsum('fpqkab,cwb->fapckqw', mixing, shift_table, precision=lax.Prec...  11.5 us
  transfers between devices with their start and end apart: 10, of which 10 were waited for; matrix products, arithmetic and copies ran while one was open for 0% of the time, Pallas kernels for 0%

commit v1 on v0

--- a/solution.py
+++ b/solution.py
@@ -1,15 +1,198 @@
+import functools
 import math
 
 import jax
 import jax.numpy as jnp
 from jax import lax
+from jax.experimental import pallas as pl
+from jax.experimental.pallas import tpu as pltpu
 from jax.sharding import PartitionSpec as P
 
 KERNELS = 8
+LAGS = 4
+HMAX = 7
+
 TAPS = 13
 HALF = 6
-LAGS = 4
-HMAX = 7
+TILE = 16
+WIN = 32
+LANES = 128
+BF = jnp.bfloat16
+F32 = jnp.float32
+
+
+def column(row):
+    n = row.shape[1]
+    eye = lax.broadcasted_iota(jnp.int32, (n, n), 0) == lax.broadcasted_iota(jnp.int32, (n, n), 1)
+    return jnp.sum(jnp.where(eye, jnp.broadcast_to(row, (n, n)), 0.0), axis=1, keepdims=True)
+
+
+def lane_taps(stencil, step, shift):
+    kernels = stencil.shape[0]
+    lanes = 512
+    weight = [stencil[:, i : i + 1] for i in range(5)]
+    total = weight[0] + 2.0 * (weight[1] + weight[2] + weight[3] + weight[4])
+    scale = step / total
+    weight = [w * scale for w in weight]
+    lane = lax.broadcasted_iota(jnp.int32, (kernels, lanes), 1)
+    power = (lane == HALF * WIN + HALF).astype(F32)
+    real, imag = power, jnp.zeros((kernels, lanes), F32)
+
+    def both(value, distance):
+        return pltpu.roll(value, distance, 1) + pltpu.roll(value, lanes - distance, 1)
+
+    for order in range(1, HALF + 1):
+        power = (
+            weight[0] * power
+            + weight[1] * both(power, WIN)
+            + weight[2] * both(power, 1)
+            + weight[3] * both(power, WIN + 1)
+            + weight[4] * both(power, WIN - 1)
+        )
+        term = power * (1.0 / math.factorial(order))
+        if order % 4 == 1:
+            imag = imag + term
+        elif order % 4 == 2:
+            real = real - term
+        elif order % 4 == 3:
+            imag = imag - term
+        else:
+            real = real + term
+    cosine, sine = jnp.cos(shift), jnp.sin(shift)
+    return cosine * real - sine * imag, sine * real + cosine * imag
+
+
+def split(value):
+    high = value.astype(BF)
+    return high, (value - high.astype(F32)).astype(BF)
+
+
+def levels_kernel(dims, place, lags, surface, bins, stencil, step, shift, image,
+                  weights, wide, grid_pad, bins_pad, high, low, state):
+    levels, kernels, strip, grid, lag_count = dims
+    halo = HALF * levels
+    freq, first = place[0], place[1]
+    real, imag = lane_taps(stencil[freq], column(step[pl.ds(freq, 1), :]), column(shift[pl.ds(freq, 1), :]))
+    for which, taps in enumerate((real, real + imag, imag - real)):
+        for row in range(TILE):
+            moved = pltpu.roll(taps, row, 1) if row else taps
+            for chunk in range(4):
+                wide[chunk, pl.ds(row, kernels, stride=TILE), :] = moved[:, chunk * LANES : (chunk + 1) * LANES]
+        for chunk in range(4):
+            w_high, w_low = split(wide[chunk])
+            weights[which, : kernels * TILE, chunk * LANES : (chunk + 1) * LANES] = w_high
+            weights[which, kernels * TILE :, chunk * LANES : (chunk + 1) * LANES] = w_low
+    bins_pad[...] = jnp.full(bins_pad.shape, kernels, jnp.int32)
+    for slot in range(levels):
+        bins_pad[lax.rem(place[2] - slot + levels, levels), halo : halo + grid, :] = bins[slot]
+    grid_pad[...] = jnp.zeros(grid_pad.shape, F32)
+    for field in range(2):
+        for part in range(2):
+            grid_pad[2 * field + part, halo : halo + grid, :] = surface[freq, field, :, part * LANES : (part + 1) * LANES]
+    lane = lax.broadcasted_iota(jnp.int32, (TILE, LANES), 1)
+
+    def spread(slot, row, planes):
+        for tap in range(TAPS):
+            reach = tap - HALF
+            moved = []
+            for plane in planes:
+                if reach:
+                    plane = pltpu.roll(plane, (-reach) % LANES, 1)
+                    inside = lane < LANES - reach if reach > 0 else lane >= -reach
+                    plane = jnp.where(inside, plane, 0.0)
+                moved.append(plane)
+            for field in range(2):
+                re, im = moved[2 * field], moved[2 * field + 1]
+                for which, value in enumerate((re + im, im, re)):
+                    v_high, v_low = split(value)
+                    high[slot, which, tap, pl.ds(row, TILE), field * LANES : (field + 1) * LANES] = v_high
+                    low[slot, which, tap, pl.ds(row, TILE), field * LANES : (field + 1) * LANES] = v_low
+
+    base = first + halo - halo
+
+    def fill(index, carry):
+        row = pl.multiple_of(index * TILE, TILE)
+        spread(0, row, [grid_pad[plane, pl.ds(base + row, TILE), :] for plane in range(4)])
+        return carry
+
+    most = strip + 2 * halo
+    lax.fori_loop(0, (most - 2 * HALF + TILE - 1) // TILE + 1, fill, 0)
+
+    def level(index, carry):
+        slot = index % 2
+        needed = strip + 2 * HALF * (levels - 1 - index)
+        bins_base = base + HALF * (index + 1)
+
+        def tile(number, inner):
+            row = pl.multiple_of(number * TILE, TILE)
+            cell_bins = bins_pad[index, pl.ds(bins_base + row, TILE), :]
+            sums = []
+            for which in range(3):
+                rhs = high[slot, which, :, pl.ds(row, WIN), :].reshape(TAPS * WIN, 2 * LANES)
+                rhs_low = low[slot, which, :, pl.ds(row, WIN), :].reshape(TAPS * WIN, 2 * LANES)
+                out = jnp.dot(weights[which, :, : TAPS * WIN], rhs, preferred_element_type=F32)
+                out_low = jnp.dot(weights[which, : kernels * TILE, : TAPS * WIN], rhs_low, preferred_element_type=F32)
+                out = out[: kernels * TILE] + out[kernels * TILE :] + out_low
+                for field in range(2):
+                    chosen = jnp.zeros((TILE, LANES), F32)
+                    for k in range(kernels):
+                        chosen = jnp.where(cell_bins == k, out[k * TILE : (k + 1) * TILE, field * LANES : (field + 1) * LANES], chosen)
+                    sums.append(chosen)
+            planes = []
+            for field in range(2):
+                planes.append(sums[field] - sums[2 + field])
+                planes.append(sums[field] + sums[4 + field])
+            for plane in range(4):
+                state[plane, pl.ds(row, TILE), :] = planes[plane]
+            spread(1 - slot, row, planes)
+            return inner
+
+        lax.fori_loop(0, (needed + TILE - 1) // TILE, tile, 0)
+        start = halo - HALF * (index + 1)
+        planes = [state[plane, pl.ds(start, strip), :] for plane in range(4)]
+        lanes = lax.broadcasted_iota(jnp.int32, (strip, LANES), 1)
+        for number in range(lag_count):
+            offset = lags[number]
+            away = lax.rem(LANES - offset, LANES)
+            s_re, s_im = pltpu.roll(planes[0], offset, 1), pltpu.roll(planes[1], offset, 1)
+            r_re, r_im = pltpu.roll(planes[2], away, 1), pltpu.roll(planes[3], away, 1)
+            inside = (lanes >= offset) & (lanes < LANES - offset)
+            image[index, number] = jnp.where(inside, s_re * r_re + s_im * r_im, 0.0)
+        return carry
+
+    lax.fori_loop(0, levels, level, 0)
+
+
+def run_levels(place, lags, surface, bins, stencil, step, shift, strip):
+    freqs, _, grid, _ = surface.shape
+    levels = bins.shape[0]
+    kernels = stencil.shape[1]
+    halo = HALF * levels
+    most = strip + 2 * halo
+    tiles = (most - 2 * HALF + TILE - 1) // TILE
+    rows = (tiles + 1) * TILE
+    padded = grid - strip + rows
+    padded = (padded + 7) // 8 * 8
+    padded = max(padded, halo + grid)
+    dims = (levels, kernels, strip, grid, lags.shape[0])
+    vm = pl.BlockSpec(memory_space=pltpu.VMEM)
+    sm = pl.BlockSpec(memory_space=pltpu.SMEM)
+    return pl.pallas_call(
+        functools.partial(levels_kernel, dims),
+        out_shape=jax.ShapeDtypeStruct((levels, lags.shape[0], strip, grid), F32),
+        in_specs=[sm, sm, vm, vm, vm, vm, vm],
+        out_specs=vm,
+        scratch_shapes=[
+            pltpu.VMEM((3, 2 * kernels * TILE, 512), BF),
+            pltpu.VMEM((4, kernels * TILE, LANES), F32),
+            pltpu.VMEM((4, padded, LANES), F32),
+            pltpu.VMEM((levels, padded, LANES), jnp.int32),
+            pltpu.VMEM((2, 3, TAPS, rows, 2 * LANES), BF),
+            pltpu.VMEM((2, 3, TAPS, rows, 2 * LANES), BF),
+            pltpu.VMEM((4, rows, LANES), F32),
+        ],
+        compiler_params=pltpu.CompilerParams(vmem_limit_bytes=60 * 1024 * 1024),
+    )(place, lags, surface, bins, stencil, step, shift)
 
 
 column_tile = 16
@@ -108,7 +291,7 @@
     return jnp.stack(lag_terms)
 
 
-def body(surface, bins, stencil, phase_step, phase_shift, lags):
+def pipeline_body(surface, bins, stencil, phase_step, phase_shift, lags):
     shot_count = surface.shape[0]
     freq_count = surface.shape[1]
     grid_width = surface.shape[3]
@@ -166,6 +349,85 @@
     final_sent, image_part = lax.fori_loop(0, depth_count + front_count - 1, advance_turn, start)
     image_part = image_part.reshape(slab_steps, LAGS, grid_width * grid_width)
     return lax.psum_scatter(image_part, "freq", scatter_dimension=2, tiled=True)
+
+
+def gather_bins(bins):
+    count, cores = lax.axis_size("depth"), lax.axis_size("freq")
+    core = lax.axis_index("freq")
+    rounds = -(-(count - 1) // cores)
+    received = []
+    for number in range(rounds):
+        pairs = []
+        for own in range(cores):
+            turn = 1 + number + own * rounds
+            if turn < count:
+                pairs += [(place * cores + own, (place + turn) % count * cores + own) for place in range(count)]
+        received.append(lax.ppermute(bins[0], ("depth", "freq"), pairs))
+    mine = jnp.stack(received)
+    theirs = lax.ppermute(mine, "freq", [(0, 1), (1, 0)])
+    first = jnp.where(core == 0, mine, theirs)
+    second = jnp.where(core == 0, theirs, mine)
+    return jnp.concatenate([bins, first, second])[:count]
+
+
+def spread_image(image, freqs):
+    count, cores = lax.axis_size("depth"), lax.axis_size("freq")
+    depth, core = lax.axis_index("depth"), lax.axis_index("freq")
+    strips = count // freqs
+    half = strips // cores
+    levels, lags, strip, grid = image.shape
+    block = image.reshape(half, cores, freqs, lags, strip, grid)
+    kept = lax.dynamic_index_in_dim(block, core, 1, keepdims=False)
+    given = lax.dynamic_index_in_dim(block, 1 - core, 1, keepdims=False)
+    block = kept + lax.ppermute(given, "freq", [(0, 1), (1, 0)])
+    place = depth % freqs
+    kept = lax.dynamic_index_in_dim(block, place, 1, keepdims=False)
+    given = lax.dynamic_index_in_dim(block, 1 - place, 1, keepdims=False)
+    block = kept + lax.ppermute(given, "depth", [(d, d ^ 1) for d in range(count)])
+    mine = depth // freqs
+    parts = []
+    for number in range(half):
+        pairs = []
+        for z in range(strips):
+            for y in range(freqs):
+                for c in range(cores):
+                    target = c + cores * ((z % half + number) % half)
+                    pairs.append(((z * freqs + y) * cores + c, (target * freqs + y) * cores + z // half))
+        chunk = lax.dynamic_index_in_dim(block, (mine % half + number) % half, 0, keepdims=False)
+        parts.append(lax.ppermute(chunk, ("depth", "freq"), pairs))
+    stacked = jnp.stack(parts)
+    row = mine // cores
+    ordered = jnp.stack([lax.dynamic_index_in_dim(stacked, (row - r) % half, 0, keepdims=False) for r in range(half)], 1)
+    return ordered.reshape(1, lags, half * strip * grid)
+
+
+def strip_body(surface, bins, stencil, phase_step, phase_shift, lags):
+    freqs, grid = surface.shape[1], surface.shape[3]
+    depth = lax.axis_index("depth")
+    strip = grid * freqs // lax.axis_size("depth")
+    place = jnp.stack([depth % freqs, depth // freqs * strip, depth]).astype(jnp.int32)
+    image = run_levels(place, lags, surface[0], gather_bins(bins), stencil, phase_step, phase_shift, strip)
+    return spread_image(image, freqs)
+
+
+def body(surface, bins, stencil, phase_step, phase_shift, lags):
+    count, cores = lax.axis_size("depth"), lax.axis_size("freq")
+    freqs, grid = surface.shape[1], surface.shape[3]
+    strips = count // freqs
+    fits = (
+        surface.shape[0] == 1
+        and bins.shape[0] == 1
+        and grid == LANES
+        and cores == 2
+        and freqs == 2
+        and count % freqs == 0
+        and strips % cores == 0
+        and grid % strips == 0
+        and (grid // strips) % 8 == 0
+        and HALF * count <= grid // 2
+    )
+    way = strip_body if fits else pipeline_body
+    return way(surface, bins, stencil, phase_step, phase_shift, lags)
 
 
 def solution(mesh):

time: 384 us -> 67.8 us (0.18)
  waiting for transfers between devices: 157 us -> 13.4 us
  starting transfers between devices: 112 us -> 16.4 us
  local copies, waits for them, and re-layouts: 56.1 us -> 3.96 us
  Pallas kernels: 0 us -> 31.3 us
  loops' own time: 21.4 us -> 0 us
  matrix products: 18.2 us -> 0 us
  between operations: 13.5 us -> 0.14 us
  other arithmetic: 5.48 us -> 1.6 us
    unnamed x2 -> x0, waiting for transfers between devices: 124 us -> none
    ppermute x9, starting transfers between devices: 112 us -> 16.4 us  [the longest x4 5.97 us: gather_bins(): received.append(lax.ppermute(bins[0], ('depth', 'freq'), pairs))]
    pallas_call x0 -> x1, Pallas kernels: none -> 31.3 us  [run_levels(): pl.pallas_call(functools.partial(levels_kernel, dims), out_shape=jax.Shap...]
    another operation x10 -> x0, loops' own time: 21.4 us -> none  [the longest x9 20.5 us: advance_turn(): return lax.cond(active, compute_front, keep_state, (incoming, image_now))]
    ppermute x9, waiting for transfers between devices: 32.8 us -> 13.4 us  [the longest x1 4.85 us: spread_image(): lax.ppermute(given, 'depth', [(d, d ^ 1) for d in range(count)])]
    dot_general x3 -> x0, matrix products: 18.2 us -> none  [the longest x2 12.6 us: advance_level(): jnp.dot(patches, weights, precision=lax.Precision.HIGHEST, preferred_elem...]
    unnamed x9 -> x7, local copies, waits for them, and re-layouts: 16.4 us -> 2.17 us
    another operation x4 -> x0, local copies, waits for them, and re-layouts: 11.8 us -> none  [advance_level(): jnp.stack([windows[:, row_tap:row_tap + grid_width] for row_tap in range(...]
  transfers between devices with their start and end apart: 10 -> 9, of which waited for: 10 -> 7; matrix products, arithmetic and copies ran while one was open for 0% -> 2% of each run, Pallas kernels for 0% -> 0%
where the time goes in v1:
time: 67.8 us; the launch traced here: 66.8 us
  Pallas kernels  31.3 us (46%)
  starting transfers between devices  16.4 us (24%)
  waiting for transfers between devices  13.4 us (20%)
  local copies, waits for them, and re-layouts  3.96 us (6%)
  other arithmetic  1.6 us (2%)
    pallas_call x1, Pallas kernels, run_levels(): pl.pallas_call(functools.partial(levels_kernel, dims), out_shape=jax.Shap...  31.3 us
    ppermute x4, starting transfers between devices, gather_bins(): received.append(lax.ppermute(bins[0], ('depth', 'freq'), pairs))  5.97 us
    ppermute x1, starting transfers between devices, gather_bins(): theirs = lax.ppermute(mine, 'freq', [(0, 1), (1, 0)])  5.61 us
    ppermute x1, waiting for transfers between devices, spread_image(): lax.ppermute(given, 'depth', [(d, d ^ 1) for d in range(count)])  4.85 us
    ppermute x2, starting transfers between devices, spread_image(): parts.append(lax.ppermute(chunk, ('depth', 'freq'), pairs))  4.6 us
    ppermute x4, waiting for transfers between devices, gather_bins(): received.append(lax.ppermute(bins[0], ('depth', 'freq'), pairs))  4.22 us
    ppermute x2, waiting for transfers between devices, spread_image(): parts.append(lax.ppermute(chunk, ('depth', 'freq'), pairs))  2.87 us
    unnamed x7, local copies, waits for them, and re-layouts  2.17 us
  transfers between devices with their start and end apart: 9, of which 7 were waited for; matrix products, arithmetic and copies ran while one was open for 2% of the time, Pallas kernels for 0%

profile of v1, /device:TPU:1, one launch (start us, length us, event | category | flops | bytes accessed | tf_op | source)
XLA Modules:
  0.0 66.8 jit_solution(9164471109946038675)
XLA Ops:
  0.0 0.7 collective-permute-start.3
  0.7 5.1 %collective-permute-start.2 = (s32[128,128]{1,0:T(8,128)}, s32[128,128]{1,0:T(8,128)S(1)}, u32[]{:S(2)}, u32[]{:S(2)}) collective-permute-start(s32[128,128]{1,0:T(8,128)} %bitcast.42), channel_id=1, source_target_pairs={{0,6},{2,8},{4,10},{6,12},{8,14},{10,0},{12,2},{14,4},{1,15},{3,1}... | collective-permute-start | bytes 196616 | tf_op jit(solution)/shard_map/ppermute | solution.py:365
  5.8 0.2 collective-permute-start.1
  6.0 0.0 collective-permute-start
  6.0 0.0 collective-permute-done.3
  6.0 1.7 %collective-permute-done.2 = s32[128,128]{1,0:T(8,128)S(1)} collective-permute-done((s32[128,128]{1,0:T(8,128)}, s32[128,128]{1,0:T(8,128)S(1)}, u32[]{:S(2)}, u32[]{:S(2)}) %collective-permute-start.2) | collective-permute-done | bytes 65568 | tf_op jit(solution)/shard_map/ppermute | solution.py:365
  7.7 1.4 %collective-permute-done.1 = s32[128,128]{1,0:T(8,128)S(1)} collective-permute-done((s32[128,128]{1,0:T(8,128)}, s32[128,128]{1,0:T(8,128)S(1)}, u32[]{:S(2)}, u32[]{:S(2)}) %collective-permute-start.1) | collective-permute-done | bytes 65568 | tf_op jit(solution)/shard_map/ppermute | solution.py:365
  9.1 1.1 %collective-permute-done = s32[128,128]{1,0:T(8,128)S(1)} collective-permute-done((s32[128,128]{1,0:T(8,128)}, s32[128,128]{1,0:T(8,128)S(1)}, u32[]{:S(2)}, u32[]{:S(2)}) %collective-permute-start) | collective-permute-done | bytes 65568 | tf_op jit(solution)/shard_map/ppermute | solution.py:365
  10.2 5.6 %collective-permute-start.4 = (s32[4,128,128]{2,1,0:T(8,128)S(1)}, s32[4,128,128]{2,1,0:T(8,128)S(1)}, u32[]{:S(2)}, u32[]{:S(2)}) collective-permute-start(s32[4,128,128]{2,1,0:T(8,128)S(1)} %pad_add_fusion.2), channel_id=1, source_target_pairs={{0,1},{1,0},{2,3},{3,2},{4,5},{5,4},{6,7},{7,6},{8,9},{9,8},{10,11... | collective-permute-start | bytes 786440 | tf_op jit(solution)/shard_map/ppermute | solution.py:367
  15.8 0.0 copy-start.2
  15.8 0.7 %copy-done.2 = f32[2,8,5]{1,0,2:T(2,128)S(1)} copy-done((f32[2,8,5]{1,0,2:T(2,128)S(1)}, f32[2,8,5]{1,0,2:T(2,128)}, u32[]{:S(2)}) %copy-start.2) | copy-done | bytes 344
  16.5 0.7 %copy.7.stencil = f32[2,8,5]{2,1,0:T(8,128)} copy(f32[2,8,5]{1,0,2:T(2,128)S(1)} %copy-done.2) | data formatting | bytes 640 | tf_op args[2]
  17.2 0.6 pad_add_fusion.3.place
  17.8 0.0 copy-start.1
  17.8 0.0 collective-permute-done.4
  17.9 0.8 %copy-done.1 = s32[1,128,128]{2,1,0:T(8,128)S(1)} copy-done((s32[1,128,128]{2,1,0:T(8,128)S(1)}, s32[1,128,128]{2,1,0:T(8,128)}, u32[]{:S(2)}) %copy-start.1) | copy-done | bytes 65560
  18.7 0.8 %pad_add_fusion.bins = s32[8,128,128]{2,1,0:T(8,128)} fusion(s32[4,128,128]{2,1,0:T(8,128)S(1)} %get-tuple-element.6, s32[4,128,128]{2,1,0:T(8,128)S(1)} %get-tuple-element.5, s32[1,128,128]{2,1,0:T(8,128)S(1)} %copy-done.1), kind=kLoop, calls=%fused_computation | loop fusion | flops 262144 | bytes 1114112 | tf_op jit(solution)/shard_map/concatenate | solution.py:370
  19.5 31.3 %shard_map.64 = f32[8,4,32,128]{3,2,1,0:T(8,128)} custom-call(s32[3]{0:T(128)} %pad_add_fusion.3.place, s32[4]{0:T(128)} %lags.1, f32[2,2,128,256]{3,2,1,0:T(8,128)} %bitcast.32, s32[8,128,128]{2,1,0:T(8,128)} %pad_add_fusion.bins, f32[2,8,5]{2,1,0:T(8,128)} %copy.7.stencil, f32[2,8]{1,0:T(2,128)} %step.1, f32[2,8]{1,0:T(2,128)} %shift.1), custom_call_target="tpu_custom_call" | custom-call | tf_op jit(solution)/shard_map/pallas_call | solution.py:180
  50.8 0.0 copy-start
  50.8 1.0 %dynamic-slice_bitcast_fusion = f32[2,2,4,32,128]{4,3,2,1,0:T(8,128)S(1)} fusion(f32[2,2,2,4,32,128]{5,4,3,2,1,0:T(8,128)} %bitcast.30, s32[]{:T(128)S(6)} %select_n.84), kind=kLoop, calls=%fused_computation.4 | loop fusion | bytes 524292 | tf_op jit(solution)/shard_map/jit(dynamic_index_in_dim)/squeeze | solution.py:381
  51.9 0.1 collective-permute-start.5
  52.0 1.5 %collective-permute-done.5 = f32[2,2,4,32,128]{4,3,2,1,0:T(8,128)S(1)} collective-permute-done((f32[2,2,4,32,128]{4,3,2,1,0:T(8,128)S(1)}, f32[2,2,4,32,128]{4,3,2,1,0:T(8,128)S(1)}, u32[]{:S(2)}, u32[]{:S(2)}) %collective-permute-start.5) | collective-permute-done | bytes 262176 | tf_op jit(solution)/shard_map/ppermute | solution.py:382
  53.5 0.0 copy-done
  53.5 0.1 collective-permute-start.6
  53.7 4.8 %collective-permute-done.6 = f32[2,4,32,128]{3,2,1,0:T(8,128)S(1)} collective-permute-done((f32[2,4,32,128]{3,2,1,0:T(8,128)S(1)}, f32[2,4,32,128]{3,2,1,0:T(8,128)S(1)}, u32[]{:S(2)}, u32[]{:S(2)}) %collective-permute-start.6) | collective-permute-done | bytes 131104 | tf_op jit(solution)/shard_map/ppermute | solution.py:386
  58.6 1.9 %collective-permute-start.7 = (f32[4,32,128]{2,1,0:T(8,128)S(1)}, f32[4,32,128]{2,1,0:T(8,128)S(1)}, u32[]{:S(2)}, u32[]{:S(2)}) collective-permute-start(f32[4,32,128]{2,1,0:T(8,128)S(1)} %get-tuple-element.10), channel_id=1, source_target_pairs={{0,0},{1,4},{2,2},{3,6},{4,8},{5,12},{6,10},{7,14},{8,1},{9,5},{10... | collective-permute-start | bytes 196616 | tf_op jit(solution)/shard_map/ppermute | solution.py:397
  60.5 2.7 %collective-permute-start.8 = (f32[4,32,128]{2,1,0:T(8,128)S(1)}, f32[4,32,128]{2,1,0:T(8,128)S(1)}, u32[]{:S(2)}, u32[]{:S(2)}) collective-permute-start(f32[4,32,128]{2,1,0:T(8,128)S(1)} %get-tuple-element.9), channel_id=1, source_target_pairs={{0,8},{1,12},{2,10},{3,14},{4,0},{5,4},{6,2},{7,6},{8,9},{9,13},{1... | collective-permute-start | bytes 196616 | tf_op jit(solution)/shard_map/ppermute | solution.py:397
  63.2 2.0 %collective-permute-done.7 = f32[4,32,128]{2,1,0:T(8,128)S(1)} collective-permute-done((f32[4,32,128]{2,1,0:T(8,128)S(1)}, f32[4,32,128]{2,1,0:T(8,128)S(1)}, u32[]{:S(2)}, u32[]{:S(2)}) %collective-permute-start.7) | collective-permute-done | bytes 65568 | tf_op jit(solution)/shard_map/ppermute | solution.py:397
  65.2 0.9 %collective-permute-done.8 = f32[4,32,128]{2,1,0:T(8,128)S(1)} collective-permute-done((f32[4,32,128]{2,1,0:T(8,128)S(1)}, f32[4,32,128]{2,1,0:T(8,128)S(1)}, u32[]{:S(2)}, u32[]{:S(2)}) %collective-permute-start.8) | collective-permute-done | bytes 65568 | tf_op jit(solution)/shard_map/ppermute | solution.py:397
  66.1 0.7 %reshape.9 = f32[1,4,8192]{2,1,0:T(4,128)} reshape(f32[4,2,32,128]{3,2,1,0:T(8,128)S(1)} %pad_maximum_fusion) | data formatting | bytes 262144 | tf_op jit(solution)/shard_map/reshape | solution.py:401
  (8 shorter events, 0.2 us)
Async XLA Ops:
  0.0 6.0 %collective-permute-start.3 = (s32[128,128]{1,0:T(8,128)}, s32[128,128]{1,0:T(8,128)S(1)}, u32[]{:S(2)}, u32[]{:S(2)}) collective-permute-start(s32[128,128]{1,0:T(8,128)} %bitcast.41), channel_id=1, source_target_pairs={{0,8},{2,10},{4,12},{6,14},{8,0},{10,2},{12,4},{14,6},{16,24},{18,... | collective-permute-start | bytes 196616 | tf_op jit(solution)/shard_map/ppermute | solution.py:365
  0.7 7.0 %collective-permute-start.2 = (s32[128,128]{1,0:T(8,128)}, s32[128,128]{1,0:T(8,128)S(1)}, u32[]{:S(2)}, u32[]{:S(2)}) collective-permute-start(s32[128,128]{1,0:T(8,128)} %bitcast.42), channel_id=1, source_target_pairs={{0,6},{2,8},{4,10},{6,12},{8,14},{10,0},{12,2},{14,4},{1,15},{3,1}... | collective-permute-start | bytes 196616 | tf_op jit(solution)/shard_map/ppermute | solution.py:365
  5.8 3.3 %collective-permute-start.1 = (s32[128,128]{1,0:T(8,128)}, s32[128,128]{1,0:T(8,128)S(1)}, u32[]{:S(2)}, u32[]{:S(2)}) collective-permute-start(s32[128,128]{1,0:T(8,128)} %bitcast.43), channel_id=1, source_target_pairs={{0,4},{2,6},{4,8},{6,10},{8,12},{10,14},{12,0},{14,2},{1,13},{3,15... | collective-permute-start | bytes 196616 | tf_op jit(solution)/shard_map/ppermute | solution.py:365
  6.0 4.2 %collective-permute-start = (s32[128,128]{1,0:T(8,128)}, s32[128,128]{1,0:T(8,128)S(1)}, u32[]{:S(2)}, u32[]{:S(2)}) collective-permute-start(s32[128,128]{1,0:T(8,128)} %bitcast.44), channel_id=1, source_target_pairs={{0,2},{2,4},{4,6},{6,8},{8,10},{10,12},{12,14},{14,0},{1,11},{3,13... | collective-permute-start | bytes 196616 | tf_op jit(solution)/shard_map/ppermute | solution.py:365
  10.2 7.6 %collective-permute-start.4 = (s32[4,128,128]{2,1,0:T(8,128)S(1)}, s32[4,128,128]{2,1,0:T(8,128)S(1)}, u32[]{:S(2)}, u32[]{:S(2)}) collective-permute-start(s32[4,128,128]{2,1,0:T(8,128)S(1)} %pad_add_fusion.2), channel_id=1, source_target_pairs={{0,1},{1,0},{2,3},{3,2},{4,5},{5,4},{6,7},{7,6},{8,9},{9,8},{10,11... | collective-permute-start | bytes 786440 | tf_op jit(solution)/shard_map/ppermute | solution.py:367
  15.8 0.7 %copy-start.2 = (f32[2,8,5]{1,0,2:T(2,128)S(1)}, f32[2,8,5]{1,0,2:T(2,128)}, u32[]{:S(2)}) copy-start(f32[2,8,5]{1,0,2:T(2,128)} %param.8) | copy-start | bytes 964
  17.8 0.8 %copy-start.1 = (s32[1,128,128]{2,1,0:T(8,128)S(1)}, s32[1,128,128]{2,1,0:T(8,128)}, u32[]{:S(2)}) copy-start(s32[1,128,128]{2,1,0:T(8,128)} %param.7) | copy-start | bytes 196612
  50.8 2.6 %copy-start = (f32[8,4,32,128]{3,2,1,0:T(8,128)S(1)}, f32[8,4,32,128]{3,2,1,0:T(8,128)}, u32[]{:S(2)}) copy-start(f32[8,4,32,128]{3,2,1,0:T(8,128)} %shard_map.64) | copy-start | bytes 1572868
  51.9 1.6 %collective-permute-start.5 = (f32[2,2,4,32,128]{4,3,2,1,0:T(8,128)S(1)}, f32[2,2,4,32,128]{4,3,2,1,0:T(8,128)S(1)}, u32[]{:S(2)}, u32[]{:S(2)}) collective-permute-start(f32[2,2,4,32,128]{4,3,2,1,0:T(8,128)S(1)} %dynamic-slice_bitcast_fusion), channel_id=1, source_target_pairs={{0,1},{1,0},{2,3},{3,2},{4,5},{5,4},{6,7},{7,6},{8,9},{9,8},{10,11... | collective-permute-start | bytes 786440 | tf_op jit(solution)/shard_map/ppermute | solution.py:382
  53.5 5.0 %collective-permute-start.6 = (f32[2,4,32,128]{3,2,1,0:T(8,128)S(1)}, f32[2,4,32,128]{3,2,1,0:T(8,128)S(1)}, u32[]{:S(2)}, u32[]{:S(2)}) collective-permute-start(f32[2,4,32,128]{3,2,1,0:T(8,128)S(1)} %dynamic-slice_bitcast_fusion.1), channel_id=1, source_target_pairs={{0,2},{2,0},{4,6},{6,4},{8,10},{10,8},{12,14},{14,12},{1,3},{3,1},... | collective-permute-start | bytes 393224 | tf_op jit(solution)/shard_map/ppermute | solution.py:386
  58.6 6.6 %collective-permute-start.7 = (f32[4,32,128]{2,1,0:T(8,128)S(1)}, f32[4,32,128]{2,1,0:T(8,128)S(1)}, u32[]{:S(2)}, u32[]{:S(2)}) collective-permute-start(f32[4,32,128]{2,1,0:T(8,128)S(1)} %get-tuple-element.10), channel_id=1, source_target_pairs={{0,0},{1,4},{2,2},{3,6},{4,8},{5,12},{6,10},{7,14},{8,1},{9,5},{10... | collective-permute-start | bytes 196616 | tf_op jit(solution)/shard_map/ppermute | solution.py:397
  60.5 5.5 %collective-permute-start.8 = (f32[4,32,128]{2,1,0:T(8,128)S(1)}, f32[4,32,128]{2,1,0:T(8,128)S(1)}, u32[]{:S(2)}, u32[]{:S(2)}) collective-permute-start(f32[4,32,128]{2,1,0:T(8,128)S(1)} %get-tuple-element.9), channel_id=1, source_target_pairs={{0,8},{1,12},{2,10},{3,14},{4,0},{5,4},{6,2},{7,6},{8,9},{9,13},{1... | collective-permute-start | bytes 196616 | tf_op jit(solution)/shard_map/ppermute | solution.py:397

commit v2 on v1

--- a/solution.py
+++ b/solution.py
@@ -11,7 +11,6 @@
 KERNELS = 8
 LAGS = 4
 HMAX = 7
-
 TAPS = 13
 HALF = 6
 TILE = 16
@@ -27,10 +26,9 @@
     return jnp.sum(jnp.where(eye, jnp.broadcast_to(row, (n, n)), 0.0), axis=1, keepdims=True)
 
 
-def lane_taps(stencil, step, shift):
-    kernels = stencil.shape[0]
+def lane_taps(weight, step, shift):
+    kernels = step.shape[0]
     lanes = 512
-    weight = [stencil[:, i : i + 1] for i in range(5)]
     total = weight[0] + 2.0 * (weight[1] + weight[2] + weight[3] + weight[4])
     scale = step / total
     weight = [w * scale for w in weight]
@@ -67,132 +65,162 @@
     return high, (value - high.astype(F32)).astype(BF)
 
 
-def levels_kernel(dims, place, lags, surface, bins, stencil, step, shift, image,
-                  weights, wide, grid_pad, bins_pad, high, low, state):
-    levels, kernels, strip, grid, lag_count = dims
+def tile_counts(levels, strip):
+    return [-(-(strip + 2 * HALF * (levels - 1 - level)) // TILE) for level in range(levels)]
+
+
+def levels_kernel(dims, lags, surface, own, mine, theirs, stencil, step, shift, image,
+                  weights, wide, grid_pad, bins_pad, high0, low0, high1, low1, state):
+    levels, kernels, freqs, strip, grid, lag_count = dims
     halo = HALF * levels
-    freq, first = place[0], place[1]
-    real, imag = lane_taps(stencil[freq], column(step[pl.ds(freq, 1), :]), column(shift[pl.ds(freq, 1), :]))
+    depth, core = lax.axis_index("depth"), lax.axis_index("freq")
+    freq, strip_index = lax.rem(depth, freqs), lax.div(depth, freqs)
+    base = strip_index * strip
+    rounds = mine.shape[0]
+    spots = kernels * TILE
+    span = TAPS * WIN
+    rows = [column(stencil[i, pl.ds(freq, 1), :]) for i in range(5)]
+    real, imag = lane_taps(rows, column(step[pl.ds(freq, 1), :]), column(shift[pl.ds(freq, 1), :]))
+    chunks = wide.shape[0]
     for which, taps in enumerate((real, real + imag, imag - real)):
+        taps_high = taps.astype(BF).astype(F32)
+        taps_low = taps - taps_high
+        rest = jnp.zeros((kernels, chunks * LANES - taps.shape[1]), F32)
+        long_high = jnp.concatenate([taps_high, rest], axis=1)
+        long_low = jnp.concatenate([taps_low, rest], axis=1)
+        line = long_high + pltpu.roll(long_low, span, 1) + pltpu.roll(long_high, 2 * span, 1)
         for row in range(TILE):
-            moved = pltpu.roll(taps, row, 1) if row else taps
-            for chunk in range(4):
+            moved = pltpu.roll(line, row, 1) if row else line
+            for chunk in range(chunks):
                 wide[chunk, pl.ds(row, kernels, stride=TILE), :] = moved[:, chunk * LANES : (chunk + 1) * LANES]
-        for chunk in range(4):
-            w_high, w_low = split(wide[chunk])
-            weights[which, : kernels * TILE, chunk * LANES : (chunk + 1) * LANES] = w_high
-            weights[which, kernels * TILE :, chunk * LANES : (chunk + 1) * LANES] = w_low
+        for chunk in range(chunks):
+            weights[which, :, chunk * LANES : (chunk + 1) * LANES] = wide[chunk].astype(BF)
     bins_pad[...] = jnp.full(bins_pad.shape, kernels, jnp.int32)
-    for slot in range(levels):
-        bins_pad[lax.rem(place[2] - slot + levels, levels), halo : halo + grid, :] = bins[slot]
+    for piece, other in ((mine, core), (theirs, 1 - core)):
+        for number in range(rounds):
+            turn = 1 + number + other * rounds
+            bins_pad[lax.rem(depth - turn + 2 * levels, levels), halo : halo + grid, :] = piece[number]
+    bins_pad[depth, halo : halo + grid, :] = own[0]
     grid_pad[...] = jnp.zeros(grid_pad.shape, F32)
     for field in range(2):
         for part in range(2):
             grid_pad[2 * field + part, halo : halo + grid, :] = surface[freq, field, :, part * LANES : (part + 1) * LANES]
     lane = lax.broadcasted_iota(jnp.int32, (TILE, LANES), 1)
 
-    def spread(slot, row, planes):
+    def spread(high, low, row, planes):
+        parts = []
+        for field in range(2):
+            re, im = planes[2 * field], planes[2 * field + 1]
+            for which, value in enumerate((re + im, im, re)):
+                for ref, piece in zip((high, low), split(value)):
+                    parts.append((ref, which, field, piece))
         for tap in range(TAPS):
             reach = tap - HALF
-            moved = []
-            for plane in planes:
+            for ref, which, field, piece in parts:
                 if reach:
-                    plane = pltpu.roll(plane, (-reach) % LANES, 1)
+                    piece = pltpu.roll(piece, (-reach) % LANES, 1)
                     inside = lane < LANES - reach if reach > 0 else lane >= -reach
-                    plane = jnp.where(inside, plane, 0.0)
-                moved.append(plane)
+                    piece = jnp.where(inside, piece, jnp.zeros_like(piece))
+                ref[which, tap, pl.ds(row, TILE), field * LANES : (field + 1) * LANES] = piece
+
+    def advance(high, low, level, row):
+        cell_bins = bins_pad[level, pl.ds(base + HALF * (level + 1) + row, TILE), :]
+        sums = []
+        for which in range(3):
+            rhs = high[which, :, pl.ds(row, WIN), :].reshape(span, 2 * LANES)
+            rhs_low = low[which, :, pl.ds(row, WIN), :].reshape(span, 2 * LANES)
+            out = jnp.dot(weights[which, :, : 3 * span], jnp.concatenate([rhs, rhs, rhs_low], axis=0), preferred_element_type=F32)
             for field in range(2):
-                re, im = moved[2 * field], moved[2 * field + 1]
-                for which, value in enumerate((re + im, im, re)):
-                    v_high, v_low = split(value)
-                    high[slot, which, tap, pl.ds(row, TILE), field * LANES : (field + 1) * LANES] = v_high
-                    low[slot, which, tap, pl.ds(row, TILE), field * LANES : (field + 1) * LANES] = v_low
-
-    base = first + halo - halo
-
-    def fill(index, carry):
-        row = pl.multiple_of(index * TILE, TILE)
-        spread(0, row, [grid_pad[plane, pl.ds(base + row, TILE), :] for plane in range(4)])
-        return carry
-
-    most = strip + 2 * halo
-    lax.fori_loop(0, (most - 2 * HALF + TILE - 1) // TILE + 1, fill, 0)
-
-    def level(index, carry):
-        slot = index % 2
-        needed = strip + 2 * HALF * (levels - 1 - index)
-        bins_base = base + HALF * (index + 1)
-
-        def tile(number, inner):
-            row = pl.multiple_of(number * TILE, TILE)
-            cell_bins = bins_pad[index, pl.ds(bins_base + row, TILE), :]
-            sums = []
-            for which in range(3):
-                rhs = high[slot, which, :, pl.ds(row, WIN), :].reshape(TAPS * WIN, 2 * LANES)
-                rhs_low = low[slot, which, :, pl.ds(row, WIN), :].reshape(TAPS * WIN, 2 * LANES)
-                out = jnp.dot(weights[which, :, : TAPS * WIN], rhs, preferred_element_type=F32)
-                out_low = jnp.dot(weights[which, : kernels * TILE, : TAPS * WIN], rhs_low, preferred_element_type=F32)
-                out = out[: kernels * TILE] + out[kernels * TILE :] + out_low
-                for field in range(2):
-                    chosen = jnp.zeros((TILE, LANES), F32)
-                    for k in range(kernels):
-                        chosen = jnp.where(cell_bins == k, out[k * TILE : (k + 1) * TILE, field * LANES : (field + 1) * LANES], chosen)
-                    sums.append(chosen)
-            planes = []
-            for field in range(2):
-                planes.append(sums[field] - sums[2 + field])
-                planes.append(sums[field] + sums[4 + field])
-            for plane in range(4):
-                state[plane, pl.ds(row, TILE), :] = planes[plane]
-            spread(1 - slot, row, planes)
-            return inner
-
-        lax.fori_loop(0, (needed + TILE - 1) // TILE, tile, 0)
-        start = halo - HALF * (index + 1)
-        planes = [state[plane, pl.ds(start, strip), :] for plane in range(4)]
+                chosen = jnp.zeros((TILE, LANES), F32)
+                for k in range(kernels):
+                    chosen = jnp.where(cell_bins == k, out[k * TILE : (k + 1) * TILE, field * LANES : (field + 1) * LANES], chosen)
+                sums.append(chosen)
+        planes = []
+        for field in range(2):
+            planes.append(sums[field] - sums[2 + field])
+            planes.append(sums[field] + sums[4 + field])
+        for plane in range(4):
+            state[level % 2, plane, pl.ds(row, TILE), :] = planes[plane]
+        return tuple(planes)
+
+    def correlate(level):
+        start = halo - HALF * (level + 1)
+        planes = [state[level % 2, plane, pl.ds(start, strip), :] for plane in range(4)]
         lanes = lax.broadcasted_iota(jnp.int32, (strip, LANES), 1)
+        z, y = level // freqs, level % freqs
+        half = image.shape[2]
+        place = (lax.rem(z % 2 + core, 2), lax.rem(y + freq, 2), lax.rem(z // 2 + strip_index * (half - 1), half))
         for number in range(lag_count):
             offset = lags[number]
             away = lax.rem(LANES - offset, LANES)
             s_re, s_im = pltpu.roll(planes[0], offset, 1), pltpu.roll(planes[1], offset, 1)
             r_re, r_im = pltpu.roll(planes[2], away, 1), pltpu.roll(planes[3], away, 1)
             inside = (lanes >= offset) & (lanes < LANES - offset)
-            image[index, number] = jnp.where(inside, s_re * r_re + s_im * r_im, 0.0)
+            image[place[0], place[1], place[2], number] = jnp.where(inside, s_re * r_re + s_im * r_im, 0.0)
+
+    def fill(index, carry):
+        row = pl.multiple_of(index * TILE, TILE)
+        spread(high0, low0, row, [grid_pad[plane, pl.ds(base + row, TILE), :] for plane in range(4)])
         return carry
 
-    lax.fori_loop(0, levels, level, 0)
-
-
-def run_levels(place, lags, surface, bins, stencil, step, shift, strip):
+    counts = tile_counts(levels, strip)
+    lax.fori_loop(0, counts[0] + 1, fill, 0)
+    slots = ((high0, low0), (high1, low1))
+    planes = None
+    for level in range(levels):
+        here, there = slots[level % 2], slots[1 - level % 2]
+        if planes is None:
+            planes = advance(*here, level, 0)
+        else:
+            last = (counts[level - 1] - 1) * TILE
+            if last < WIN:
+                spread(*here, last, planes)
+                first = advance(*here, level, 0)
+            else:
+                first = advance(*here, level, 0)
+                spread(*here, last, planes)
+            correlate(level - 1)
+            planes = first
+
+        def tile(number, carried, here=here, there=there, level=level):
+            row = number * TILE
+            fresh = advance(*here, level, row)
+            if level < levels - 1:
+                spread(*there, row - TILE, carried)
+            return fresh
+
+        for number in range(1, counts[level]):
+            planes = tile(number, planes)
+    correlate(levels - 1)
+
+
+def run_levels(lags, surface, own, mine, theirs, stencil, step, shift, strip, levels):
     freqs, _, grid, _ = surface.shape
-    levels = bins.shape[0]
-    kernels = stencil.shape[1]
+    kernels = step.shape[1]
     halo = HALF * levels
-    most = strip + 2 * halo
-    tiles = (most - 2 * HALF + TILE - 1) // TILE
-    rows = (tiles + 1) * TILE
-    padded = grid - strip + rows
-    padded = (padded + 7) // 8 * 8
-    padded = max(padded, halo + grid)
-    dims = (levels, kernels, strip, grid, lags.shape[0])
+    rows = (tile_counts(levels, strip)[0] + 1) * TILE
+    padded = max((grid - strip + rows + 7) // 8 * 8, halo + grid)
+    dims = (levels, kernels, freqs, strip, grid, lags.shape[0])
+    half = levels // freqs // 2
+    span = -(-3 * TAPS * WIN // LANES)
     vm = pl.BlockSpec(memory_space=pltpu.VMEM)
     sm = pl.BlockSpec(memory_space=pltpu.SMEM)
+    operand = pltpu.VMEM((3, TAPS, rows, 2 * LANES), BF)
     return pl.pallas_call(
         functools.partial(levels_kernel, dims),
-        out_shape=jax.ShapeDtypeStruct((levels, lags.shape[0], strip, grid), F32),
-        in_specs=[sm, sm, vm, vm, vm, vm, vm],
+        out_shape=jax.ShapeDtypeStruct((2, freqs, half, lags.shape[0], strip, grid), F32),
+        in_specs=[sm] + [vm] * 7,
         out_specs=vm,
         scratch_shapes=[
-            pltpu.VMEM((3, 2 * kernels * TILE, 512), BF),
-            pltpu.VMEM((4, kernels * TILE, LANES), F32),
+            pltpu.VMEM((3, kernels * TILE, span * LANES), BF),
+            pltpu.VMEM((span, kernels * TILE, LANES), F32),
             pltpu.VMEM((4, padded, LANES), F32),
             pltpu.VMEM((levels, padded, LANES), jnp.int32),
-            pltpu.VMEM((2, 3, TAPS, rows, 2 * LANES), BF),
-            pltpu.VMEM((2, 3, TAPS, rows, 2 * LANES), BF),
-            pltpu.VMEM((4, rows, LANES), F32),
+            operand, operand, operand, operand,
+            pltpu.VMEM((2, 4, rows, LANES), F32),
         ],
-        compiler_params=pltpu.CompilerParams(vmem_limit_bytes=60 * 1024 * 1024),
-    )(place, lags, surface, bins, stencil, step, shift)
+        compiler_params=pltpu.CompilerParams(vmem_limit_bytes=56 * 1024 * 1024),
+    )(lags, surface, own, mine, theirs, jnp.transpose(stencil, (2, 0, 1)), step, shift)
 
 
 column_tile = 16
@@ -353,7 +381,6 @@
 
 def gather_bins(bins):
     count, cores = lax.axis_size("depth"), lax.axis_size("freq")
-    core = lax.axis_index("freq")
     rounds = -(-(count - 1) // cores)
     received = []
     for number in range(rounds):
@@ -364,27 +391,16 @@
                 pairs += [(place * cores + own, (place + turn) % count * cores + own) for place in range(count)]
         received.append(lax.ppermute(bins[0], ("depth", "freq"), pairs))
     mine = jnp.stack(received)
-    theirs = lax.ppermute(mine, "freq", [(0, 1), (1, 0)])
-    first = jnp.where(core == 0, mine, theirs)
-    second = jnp.where(core == 0, theirs, mine)
-    return jnp.concatenate([bins, first, second])[:count]
+    return mine, lax.ppermute(mine, "freq", [(0, 1), (1, 0)])
 
 
 def spread_image(image, freqs):
     count, cores = lax.axis_size("depth"), lax.axis_size("freq")
-    depth, core = lax.axis_index("depth"), lax.axis_index("freq")
     strips = count // freqs
     half = strips // cores
-    levels, lags, strip, grid = image.shape
-    block = image.reshape(half, cores, freqs, lags, strip, grid)
-    kept = lax.dynamic_index_in_dim(block, core, 1, keepdims=False)
-    given = lax.dynamic_index_in_dim(block, 1 - core, 1, keepdims=False)
-    block = kept + lax.ppermute(given, "freq", [(0, 1), (1, 0)])
-    place = depth % freqs
-    kept = lax.dynamic_index_in_dim(block, place, 1, keepdims=False)
-    given = lax.dynamic_index_in_dim(block, 1 - place, 1, keepdims=False)
-    block = kept + lax.ppermute(given, "depth", [(d, d ^ 1) for d in range(count)])
-    mine = depth // freqs
+    lags, strip, grid = image.shape[3:]
+    block = image[0] + lax.ppermute(image[1], "freq", [(0, 1), (1, 0)])
+    block = block[0] + lax.ppermute(block[1], "depth", [(d, d ^ 1) for d in range(count)])
     parts = []
     for number in range(half):
         pairs = []
@@ -393,20 +409,19 @@
                 for c in range(cores):
                     target = c + cores * ((z % half + number) % half)
                     pairs.append(((z * freqs + y) * cores + c, (target * freqs + y) * cores + z // half))
-        chunk = lax.dynamic_index_in_dim(block, (mine % half + number) % half, 0, keepdims=False)
-        parts.append(lax.ppermute(chunk, ("depth", "freq"), pairs))
+        parts.append(lax.ppermute(block[number], ("depth", "freq"), pairs))
     stacked = jnp.stack(parts)
-    row = mine // cores
+    row = lax.axis_index("depth") // freqs // cores
     ordered = jnp.stack([lax.dynamic_index_in_dim(stacked, (row - r) % half, 0, keepdims=False) for r in range(half)], 1)
     return ordered.reshape(1, lags, half * strip * grid)
 
 
 def strip_body(surface, bins, stencil, phase_step, phase_shift, lags):
     freqs, grid = surface.shape[1], surface.shape[3]
-    depth = lax.axis_index("depth")
-    strip = grid * freqs // lax.axis_size("depth")
-    place = jnp.stack([depth % freqs, depth // freqs * strip, depth]).astype(jnp.int32)
-    image = run_levels(place, lags, surface[0], gather_bins(bins), stencil, phase_step, phase_shift, strip)
+    count = lax.axis_size("depth")
+    mine, theirs = gather_bins(bins)
+    strip = grid * freqs // count
+    image = run_levels(lags, surface[0], bins, mine, theirs, stencil, phase_step, phase_shift, strip, count)
     return spread_image(image, freqs)
 
 
@@ -423,8 +438,9 @@
         and count % freqs == 0
         and strips % cores == 0
         and grid % strips == 0
-        and (grid // strips) % 8 == 0
+        and grid // strips % 8 == 0
         and HALF * count <= grid // 2
+        and tile_counts(count, grid // strips)[1] < tile_counts(count, grid // strips)[0]
     )
     way = strip_body if fits else pipeline_body
     return way(surface, bins, stencil, phase_step, phase_shift, lags)

time: 67.8 us -> 52.3 us (0.77); the launches traced: 66.8 us -> 52.1 us
  Pallas kernels: 31.3 us -> 16.8 us
  waiting for transfers between devices: 13.4 us -> 15.7 us
  other arithmetic: 1.6 us -> 0.11 us
  local copies, waits for them, and re-layouts: 3.96 us -> 2.49 us
    pallas_call x1, Pallas kernels: 31.3 us -> 16.8 us  [run_levels(): pl.pallas_call(functools.partial(levels_kernel, dims), out_shape=jax.Shap...]
    ppermute x5, waiting for transfers between devices: 9.22 us -> 11.5 us  [the longest x1 4.67 us: spread_image(): lax.ppermute(block[1], 'depth', [(d, d ^ 1) for d in range(count)])]
    unnamed x7 -> x6, local copies, waits for them, and re-layouts: 2.17 us -> 0.72 us
    concatenate x1 -> x0, other arithmetic: 0.83 us -> none  [gather_bins(): return jnp.concatenate([bins, first, second])[:count]]
  transfers between devices with their start and end apart: 9 -> 9, of which waited for: 7 -> 8; matrix products, arithmetic and copies ran while one was open for 2% -> 0% of each run, Pallas kernels for 0% -> 0%
where the time goes in v2:
time: 52.3 us; the launch traced here: 52.1 us
  starting transfers between devices  16.9 us (32%)
  Pallas kernels  16.8 us (32%)
  waiting for transfers between devices  15.7 us (30%)
  local copies, waits for them, and re-layouts  2.49 us (5%)
    pallas_call x1, Pallas kernels, run_levels(): pl.pallas_call(functools.partial(levels_kernel, dims), out_shape=jax.Shap...  16.8 us
    ppermute x4, starting transfers between devices, gather_bins(): received.append(lax.ppermute(bins[0], ('depth', 'freq'), pairs))  5.97 us
    ppermute x1, starting transfers between devices, gather_bins(): return (mine, lax.ppermute(mine, 'freq', [(0, 1), (1, 0)]))  5.61 us
    ppermute x2, starting transfers between devices, spread_image(): parts.append(lax.ppermute(block[number], ('depth', 'freq'), pairs))  4.82 us
    ppermute x1, waiting for transfers between devices, spread_image(): lax.ppermute(block[1], 'depth', [(d, d ^ 1) for d in range(count)])  4.67 us
    ppermute x2, waiting for transfers between devices, spread_image(): parts.append(lax.ppermute(block[number], ('depth', 'freq'), pairs))  4.48 us
    ppermute x4, waiting for transfers between devices, gather_bins(): received.append(lax.ppermute(bins[0], ('depth', 'freq'), pairs))  4.22 us
    ppermute x1, waiting for transfers between devices, gather_bins(): return (mine, lax.ppermute(mine, 'freq', [(0, 1), (1, 0)]))  1.16 us
  transfers between devices with their start and end apart: 9, of which 8 were waited for; matrix products, arithmetic and copies ran while one was open for 0% of the time, Pallas kernels for 0%

profile of v2, /device:TPU:1, one launch (start us, length us, event | category | flops | bytes accessed | tf_op | source)
XLA Modules:
  0.0 52.1 jit_solution(16331252394539085295)
XLA Ops:
  0.0 0.7 %collective-permute-start.3 = (s32[128,128]{1,0:T(8,128)}, s32[128,128]{1,0:T(8,128)S(1)}, u32[]{:S(2)}, u32[]{:S(2)}) collective-permute-start(s32[128,128]{1,0:T(8,128)} %bitcast.38), channel_id=1, source_target_pairs={{0,8},{2,10},{4,12},{6,14},{8,0},{10,2},{12,4},{14,6},{16,24},{18,... | collective-permute-start | bytes 196616 | tf_op jit(solution)/shard_map/ppermute | solution.py:392
  0.7 5.1 %collective-permute-start.2 = (s32[128,128]{1,0:T(8,128)}, s32[128,128]{1,0:T(8,128)S(1)}, u32[]{:S(2)}, u32[]{:S(2)}) collective-permute-start(s32[128,128]{1,0:T(8,128)} %bitcast.39), channel_id=1, source_target_pairs={{0,6},{2,8},{4,10},{6,12},{8,14},{10,0},{12,2},{14,4},{1,15},{3,1}... | collective-permute-start | bytes 196616 | tf_op jit(solution)/shard_map/ppermute | solution.py:392
  5.8 0.2 collective-permute-start.1
  6.0 0.0 collective-permute-start
  6.0 0.0 collective-permute-done.3
  6.0 1.7 %collective-permute-done.2 = s32[128,128]{1,0:T(8,128)S(1)} collective-permute-done((s32[128,128]{1,0:T(8,128)}, s32[128,128]{1,0:T(8,128)S(1)}, u32[]{:S(2)}, u32[]{:S(2)}) %collective-permute-start.2) | collective-permute-done | bytes 65568 | tf_op jit(solution)/shard_map/ppermute | solution.py:392
  7.7 1.4 %collective-permute-done.1 = s32[128,128]{1,0:T(8,128)S(1)} collective-permute-done((s32[128,128]{1,0:T(8,128)}, s32[128,128]{1,0:T(8,128)S(1)}, u32[]{:S(2)}, u32[]{:S(2)}) %collective-permute-start.1) | collective-permute-done | bytes 65568 | tf_op jit(solution)/shard_map/ppermute | solution.py:392
  9.1 1.1 %collective-permute-done = s32[128,128]{1,0:T(8,128)S(1)} collective-permute-done((s32[128,128]{1,0:T(8,128)}, s32[128,128]{1,0:T(8,128)S(1)}, u32[]{:S(2)}, u32[]{:S(2)}) %collective-permute-start) | collective-permute-done | bytes 65568 | tf_op jit(solution)/shard_map/ppermute | solution.py:392
  10.2 0.0 copy-start.1
  10.2 5.6 %collective-permute-start.4 = (s32[4,128,128]{2,1,0:T(8,128)S(1)}, s32[4,128,128]{2,1,0:T(8,128)S(1)}, u32[]{:S(2)}, u32[]{:S(2)}) collective-permute-start(s32[4,128,128]{2,1,0:T(8,128)S(1)} %pad_add_fusion.mine), channel_id=1, source_target_pairs={{0,1},{1,0},{2,3},{3,2},{4,5},{5,4},{6,7},{7,6},{8,9},{9,8},{10,11... | collective-permute-start | bytes 786440 | tf_op jit(solution)/shard_map/ppermute | solution.py:394
  15.8 1.2 %collective-permute-done.4.theirs = s32[4,128,128]{2,1,0:T(8,128)S(1)} collective-permute-done((s32[4,128,128]{2,1,0:T(8,128)S(1)}, s32[4,128,128]{2,1,0:T(8,128)S(1)}, u32[]{:S(2)}, u32[]{:S(2)}) %collective-permute-start.4) | collective-permute-done | bytes 262176 | tf_op jit(solution)/shard_map/ppermute | solution.py:394
  17.0 0.0 copy-start.2
  17.0 0.0 copy-done.1
  17.0 0.7 %copy-done.2 = s32[4,128,128]{2,1,0:T(8,128)} copy-done((s32[4,128,128]{2,1,0:T(8,128)}, s32[4,128,128]{2,1,0:T(8,128)S(1)}, u32[]{:S(2)}) %copy-start.2) | copy-done | bytes 262168
  17.7 16.8 %shard_map.64 = f32[2,2,2,4,32,128]{5,4,3,2,1,0:T(8,128)} custom-call(s32[4]{0:T(128)} %lags.1, f32[2,2,128,256]{3,2,1,0:T(8,128)} %bitcast.31, s32[1,128,128]{2,1,0:T(8,128)} %own.1, s32[4,128,128]{2,1,0:T(8,128)} %copy-done.1, s32[4,128,128]{2,1,0:T(8,128)} %copy-done.2, f32[5,2,8]{2,1,0:T(2,128)} %bitcast.42, f32[2,8]{1,0:T(2,128)} %step.1, f32[2,8]{1,0:T(2,128)} %shift.1), custom_call_target="tpu_custom_call" | custom-call | tf_op jit(solution)/shard_map/pallas_call | solution.py:209
  34.5 0.0 copy-start
  34.5 1.0 %slice_bitcast_fusion = f32[2,2,4,32,128]{4,3,2,1,0:T(8,128)S(1)} fusion(f32[2,2,2,4,32,128]{5,4,3,2,1,0:T(8,128)} %shard_map.64), kind=kLoop, calls=%fused_computation | loop fusion | bytes 524288 | tf_op jit(solution)/shard_map/squeeze | solution.py:402
  35.5 0.4 collective-permute-start.5
  36.0 1.2 %collective-permute-done.5 = f32[2,2,4,32,128]{4,3,2,1,0:T(8,128)S(1)} collective-permute-done((f32[2,2,4,32,128]{4,3,2,1,0:T(8,128)S(1)}, f32[2,2,4,32,128]{4,3,2,1,0:T(8,128)S(1)}, u32[]{:S(2)}, u32[]{:S(2)}) %collective-permute-start.5) | collective-permute-done | bytes 262176 | tf_op jit(solution)/shard_map/ppermute | solution.py:402
  37.1 0.0 copy-done
  37.2 0.1 collective-permute-start.6
  37.3 4.7 %collective-permute-done.6 = f32[2,4,32,128]{3,2,1,0:T(8,128)S(1)} collective-permute-done((f32[2,4,32,128]{3,2,1,0:T(8,128)S(1)}, f32[2,4,32,128]{3,2,1,0:T(8,128)S(1)}, u32[]{:S(2)}, u32[]{:S(2)}) %collective-permute-start.6) | collective-permute-done | bytes 131104 | tf_op jit(solution)/shard_map/ppermute | solution.py:403
  42.0 2.9 %collective-permute-start.8 = (f32[4,32,128]{2,1,0:T(8,128)S(1)}, f32[4,32,128]{2,1,0:T(8,128)S(1)}, u32[]{:S(2)}, u32[]{:S(2)}) collective-permute-start(f32[4,32,128]{2,1,0:T(8,128)S(1)} %get-tuple-element.7), channel_id=1, source_target_pairs={{0,8},{1,12},{2,10},{3,14},{4,0},{5,4},{6,2},{7,6},{8,9},{9,13},{1... | collective-permute-start | bytes 196616 | tf_op jit(solution)/shard_map/ppermute | solution.py:412
  44.9 1.9 %collective-permute-start.7 = (f32[4,32,128]{2,1,0:T(8,128)S(1)}, f32[4,32,128]{2,1,0:T(8,128)S(1)}, u32[]{:S(2)}, u32[]{:S(2)}) collective-permute-start(f32[4,32,128]{2,1,0:T(8,128)S(1)} %get-tuple-element.8), channel_id=1, source_target_pairs={{0,0},{1,4},{2,2},{3,6},{4,8},{5,12},{6,10},{7,14},{8,1},{9,5},{10... | collective-permute-start | bytes 196616 | tf_op jit(solution)/shard_map/ppermute | solution.py:412
  46.9 0.7 %collective-permute-done.8 = f32[4,32,128]{2,1,0:T(8,128)S(1)} collective-permute-done((f32[4,32,128]{2,1,0:T(8,128)S(1)}, f32[4,32,128]{2,1,0:T(8,128)S(1)}, u32[]{:S(2)}, u32[]{:S(2)}) %collective-permute-start.8) | collective-permute-done | bytes 65568 | tf_op jit(solution)/shard_map/ppermute | solution.py:412
  47.6 3.8 %collective-permute-done.7 = f32[4,32,128]{2,1,0:T(8,128)S(1)} collective-permute-done((f32[4,32,128]{2,1,0:T(8,128)S(1)}, f32[4,32,128]{2,1,0:T(8,128)S(1)}, u32[]{:S(2)}, u32[]{:S(2)}) %collective-permute-start.7) | collective-permute-done | bytes 65568 | tf_op jit(solution)/shard_map/ppermute | solution.py:412
  51.4 0.7 %reshape.5 = f32[1,4,8192]{2,1,0:T(4,128)} reshape(f32[4,2,32,128]{3,2,1,0:T(8,128)S(1)} %pad_maximum_fusion) | data formatting | bytes 262144 | tf_op jit(solution)/shard_map/reshape | solution.py:416
  (7 shorter events, 0.1 us)
Async XLA Ops:
  0.0 6.0 %collective-permute-start.3 = (s32[128,128]{1,0:T(8,128)}, s32[128,128]{1,0:T(8,128)S(1)}, u32[]{:S(2)}, u32[]{:S(2)}) collective-permute-start(s32[128,128]{1,0:T(8,128)} %bitcast.38), channel_id=1, source_target_pairs={{0,8},{2,10},{4,12},{6,14},{8,0},{10,2},{12,4},{14,6},{16,24},{18,... | collective-permute-start | bytes 196616 | tf_op jit(solution)/shard_map/ppermute | solution.py:392
  0.7 7.0 %collective-permute-start.2 = (s32[128,128]{1,0:T(8,128)}, s32[128,128]{1,0:T(8,128)S(1)}, u32[]{:S(2)}, u32[]{:S(2)}) collective-permute-start(s32[128,128]{1,0:T(8,128)} %bitcast.39), channel_id=1, source_target_pairs={{0,6},{2,8},{4,10},{6,12},{8,14},{10,0},{12,2},{14,4},{1,15},{3,1}... | collective-permute-start | bytes 196616 | tf_op jit(solution)/shard_map/ppermute | solution.py:392
  5.8 3.3 %collective-permute-start.1 = (s32[128,128]{1,0:T(8,128)}, s32[128,128]{1,0:T(8,128)S(1)}, u32[]{:S(2)}, u32[]{:S(2)}) collective-permute-start(s32[128,128]{1,0:T(8,128)} %bitcast.40), channel_id=1, source_target_pairs={{0,4},{2,6},{4,8},{6,10},{8,12},{10,14},{12,0},{14,2},{1,13},{3,15... | collective-permute-start | bytes 196616 | tf_op jit(solution)/shard_map/ppermute | solution.py:392
  6.0 4.2 %collective-permute-start = (s32[128,128]{1,0:T(8,128)}, s32[128,128]{1,0:T(8,128)S(1)}, u32[]{:S(2)}, u32[]{:S(2)}) collective-permute-start(s32[128,128]{1,0:T(8,128)} %bitcast.41), channel_id=1, source_target_pairs={{0,2},{2,4},{4,6},{6,8},{8,10},{10,12},{12,14},{14,0},{1,11},{3,13... | collective-permute-start | bytes 196616 | tf_op jit(solution)/shard_map/ppermute | solution.py:392
  10.2 6.8 %copy-start.1 = (s32[4,128,128]{2,1,0:T(8,128)}, s32[4,128,128]{2,1,0:T(8,128)S(1)}, u32[]{:S(2)}) copy-start(s32[4,128,128]{2,1,0:T(8,128)S(1)} %pad_add_fusion.mine) | copy-start | bytes 786436
  10.2 6.8 %collective-permute-start.4 = (s32[4,128,128]{2,1,0:T(8,128)S(1)}, s32[4,128,128]{2,1,0:T(8,128)S(1)}, u32[]{:S(2)}, u32[]{:S(2)}) collective-permute-start(s32[4,128,128]{2,1,0:T(8,128)S(1)} %pad_add_fusion.mine), channel_id=1, source_target_pairs={{0,1},{1,0},{2,3},{3,2},{4,5},{5,4},{6,7},{7,6},{8,9},{9,8},{10,11... | collective-permute-start | bytes 786440 | tf_op jit(solution)/shard_map/ppermute | solution.py:394
  17.0 0.7 %copy-start.2 = (s32[4,128,128]{2,1,0:T(8,128)}, s32[4,128,128]{2,1,0:T(8,128)S(1)}, u32[]{:S(2)}) copy-start(s32[4,128,128]{2,1,0:T(8,128)S(1)} %collective-permute-done.4.theirs) | copy-start | bytes 786436
  34.5 2.6 %copy-start = (f32[2,2,2,4,32,128]{5,4,3,2,1,0:T(8,128)S(1)}, f32[2,2,2,4,32,128]{5,4,3,2,1,0:T(8,128)}, u32[]{:S(2)}) copy-start(f32[2,2,2,4,32,128]{5,4,3,2,1,0:T(8,128)} %shard_map.64) | copy-start | bytes 1572868
  35.5 1.6 %collective-permute-start.5 = (f32[2,2,4,32,128]{4,3,2,1,0:T(8,128)S(1)}, f32[2,2,4,32,128]{4,3,2,1,0:T(8,128)S(1)}, u32[]{:S(2)}, u32[]{:S(2)}) collective-permute-start(f32[2,2,4,32,128]{4,3,2,1,0:T(8,128)S(1)} %slice_bitcast_fusion), channel_id=1, source_target_pairs={{0,1},{1,0},{2,3},{3,2},{4,5},{5,4},{6,7},{7,6},{8,9},{9,8},{10,11... | collective-permute-start | bytes 786440 | tf_op jit(solution)/shard_map/ppermute | solution.py:402
  37.2 4.7 %collective-permute-start.6 = (f32[2,4,32,128]{3,2,1,0:T(8,128)S(1)}, f32[2,4,32,128]{3,2,1,0:T(8,128)S(1)}, u32[]{:S(2)}, u32[]{:S(2)}) collective-permute-start(f32[2,4,32,128]{3,2,1,0:T(8,128)S(1)} %slice_bitcast_fusion.2), channel_id=1, source_target_pairs={{0,2},{2,0},{4,6},{6,4},{8,10},{10,8},{12,14},{14,12},{1,3},{3,1},... | collective-permute-start | bytes 393224 | tf_op jit(solution)/shard_map/ppermute | solution.py:403
  42.0 5.6 %collective-permute-start.8 = (f32[4,32,128]{2,1,0:T(8,128)S(1)}, f32[4,32,128]{2,1,0:T(8,128)S(1)}, u32[]{:S(2)}, u32[]{:S(2)}) collective-permute-start(f32[4,32,128]{2,1,0:T(8,128)S(1)} %get-tuple-element.7), channel_id=1, source_target_pairs={{0,8},{1,12},{2,10},{3,14},{4,0},{5,4},{6,2},{7,6},{8,9},{9,13},{1... | collective-permute-start | bytes 196616 | tf_op jit(solution)/shard_map/ppermute | solution.py:412
  44.9 6.5 %collective-permute-start.7 = (f32[4,32,128]{2,1,0:T(8,128)S(1)}, f32[4,32,128]{2,1,0:T(8,128)S(1)}, u32[]{:S(2)}, u32[]{:S(2)}) collective-permute-start(f32[4,32,128]{2,1,0:T(8,128)S(1)} %get-tuple-element.8), channel_id=1, source_target_pairs={{0,0},{1,4},{2,2},{3,6},{4,8},{5,12},{6,10},{7,14},{8,1},{9,5},{10... | collective-permute-start | bytes 196616 | tf_op jit(solution)/shard_map/ppermute | solution.py:412

commit v3 on v2

--- a/solution.py
+++ b/solution.py
@@ -69,16 +69,41 @@
     return [-(-(strip + 2 * HALF * (levels - 1 - level)) // TILE) for level in range(levels)]
 
 
-def levels_kernel(dims, lags, surface, own, mine, theirs, stencil, step, shift, image,
-                  weights, wide, grid_pad, bins_pad, high0, low0, high1, low1, state):
+def spread(high, low, row, planes):
+    lane = lax.broadcasted_iota(jnp.int32, (TILE, LANES), 1)
+    parts = []
+    for field in range(2):
+        re, im = planes[2 * field], planes[2 * field + 1]
+        for which, value in enumerate((re + im, im, re)):
+            for ref, piece in zip((high, low), split(value)):
+                parts.append((ref, which, field, piece))
+    for tap in range(TAPS):
+        reach = tap - HALF
+        for ref, which, field, piece in parts:
+            if reach:
+                piece = pltpu.roll(piece, (-reach) % LANES, 1)
+                inside = lane < LANES - reach if reach > 0 else lane >= -reach
+                piece = jnp.where(inside, piece, jnp.zeros_like(piece))
+            ref[which, tap, pl.ds(row, TILE), field * LANES : (field + 1) * LANES] = piece
+
+
+def distant(value):
+    return pltpu.with_memory_space_constraint(value, pltpu.HBM)
+
+
+def fetch(pairs, sems):
+    copies = [pltpu.make_async_copy(source, target, sems.at[number]) for number, (source, target) in enumerate(pairs)]
+    for copy in copies:
+        copy.start()
+    for copy in copies:
+        copy.wait()
+
+
+def weights_kernel(dims, stencil_far, step_far, shift_far, weights, stencil, step, shift, wide, sems):
     levels, kernels, freqs, strip, grid, lag_count = dims
-    halo = HALF * levels
-    depth, core = lax.axis_index("depth"), lax.axis_index("freq")
-    freq, strip_index = lax.rem(depth, freqs), lax.div(depth, freqs)
-    base = strip_index * strip
-    rounds = mine.shape[0]
-    spots = kernels * TILE
+    freq = lax.rem(lax.axis_index("depth"), freqs)
     span = TAPS * WIN
+    fetch(((stencil_far, stencil), (step_far, step), (shift_far, shift)), sems)
     rows = [column(stencil[i, pl.ds(freq, 1), :]) for i in range(5)]
     real, imag = lane_taps(rows, column(step[pl.ds(freq, 1), :]), column(shift[pl.ds(freq, 1), :]))
     chunks = wide.shape[0]
@@ -95,34 +120,44 @@
                 wide[chunk, pl.ds(row, kernels, stride=TILE), :] = moved[:, chunk * LANES : (chunk + 1) * LANES]
         for chunk in range(chunks):
             weights[which, :, chunk * LANES : (chunk + 1) * LANES] = wide[chunk].astype(BF)
+
+
+def operands_kernel(dims, surface, high, low, fields, grid_pad, sems):
+    levels, kernels, freqs, strip, grid, lag_count = dims
+    halo = HALF * levels
+    depth = lax.axis_index("depth")
+    freq, strip_index = lax.rem(depth, freqs), lax.div(depth, freqs)
+    base = strip_index * strip
+    fetch(((surface.at[freq], fields),), sems)
+    grid_pad[...] = jnp.zeros(grid_pad.shape, F32)
+    for field in range(2):
+        for part in range(2):
+            grid_pad[2 * field + part, halo : halo + grid, :] = fields[field, :, part * LANES : (part + 1) * LANES]
+
+    def fill(index, carry):
+        row = pl.multiple_of(index * TILE, TILE)
+        spread(high, low, row, [grid_pad[plane, pl.ds(base + row, TILE), :] for plane in range(4)])
+        return carry
+
+    lax.fori_loop(0, tile_counts(levels, strip)[0] + 1, fill, 0)
+
+
+def levels_kernel(dims, lags_far, own, mine, theirs, weights, high, low, image,
+                  lags, bins_pad, high0, low0, high1, low1, state, sems):
+    levels, kernels, freqs, strip, grid, lag_count = dims
+    halo = HALF * levels
+    depth, core = lax.axis_index("depth"), lax.axis_index("freq")
+    freq, strip_index = lax.rem(depth, freqs), lax.div(depth, freqs)
+    base = strip_index * strip
+    rounds = mine.shape[0]
+    spots = kernels * TILE
+    span = TAPS * WIN
     bins_pad[...] = jnp.full(bins_pad.shape, kernels, jnp.int32)
     for piece, other in ((mine, core), (theirs, 1 - core)):
         for number in range(rounds):
             turn = 1 + number + other * rounds
             bins_pad[lax.rem(depth - turn + 2 * levels, levels), halo : halo + grid, :] = piece[number]
-    bins_pad[depth, halo : halo + grid, :] = own[0]
-    grid_pad[...] = jnp.zeros(grid_pad.shape, F32)
-    for field in range(2):
-        for part in range(2):
-            grid_pad[2 * field + part, halo : halo + grid, :] = surface[freq, field, :, part * LANES : (part + 1) * LANES]
-    lane = lax.broadcasted_iota(jnp.int32, (TILE, LANES), 1)
-
-    def spread(high, low, row, planes):
-        parts = []
-        for field in range(2):
-            re, im = planes[2 * field], planes[2 * field + 1]
-            for which, value in enumerate((re + im, im, re)):
-                for ref, piece in zip((high, low), split(value)):
-                    parts.append((ref, which, field, piece))
-        for tap in range(TAPS):
-            reach = tap - HALF
-            for ref, which, field, piece in parts:
-                if reach:
-                    piece = pltpu.roll(piece, (-reach) % LANES, 1)
-                    inside = lane < LANES - reach if reach > 0 else lane >= -reach
-                    piece = jnp.where(inside, piece, jnp.zeros_like(piece))
-                ref[which, tap, pl.ds(row, TILE), field * LANES : (field + 1) * LANES] = piece
-
+    fetch(((lags_far, lags), (own.at[0], bins_pad.at[depth, pl.ds(halo, grid), :])), sems)
     def advance(high, low, level, row):
         cell_bins = bins_pad[level, pl.ds(base + HALF * (level + 1) + row, TILE), :]
         sums = []
@@ -158,17 +193,11 @@
             inside = (lanes >= offset) & (lanes < LANES - offset)
             image[place[0], place[1], place[2], number] = jnp.where(inside, s_re * r_re + s_im * r_im, 0.0)
 
-    def fill(index, carry):
-        row = pl.multiple_of(index * TILE, TILE)
-        spread(high0, low0, row, [grid_pad[plane, pl.ds(base + row, TILE), :] for plane in range(4)])
-        return carry
-
     counts = tile_counts(levels, strip)
-    lax.fori_loop(0, counts[0] + 1, fill, 0)
-    slots = ((high0, low0), (high1, low1))
+    slots = [(high, low), (high1, low1)] + [(high0, low0), (high1, low1)] * levels
     planes = None
     for level in range(levels):
-        here, there = slots[level % 2], slots[1 - level % 2]
+        here, there = slots[level], slots[level + 1]
         if planes is None:
             planes = advance(*here, level, 0)
         else:
@@ -194,7 +223,7 @@
     correlate(levels - 1)
 
 
-def run_levels(lags, surface, own, mine, theirs, stencil, step, shift, strip, levels):
+def run_levels(lags, surface, bins, stencil, step, shift, strip, levels):
     freqs, _, grid, _ = surface.shape
     kernels = step.shape[1]
     halo = HALF * levels
@@ -205,22 +234,46 @@
     span = -(-3 * TAPS * WIN // LANES)
     vm = pl.BlockSpec(memory_space=pltpu.VMEM)
     sm = pl.BlockSpec(memory_space=pltpu.SMEM)
-    operand = pltpu.VMEM((3, TAPS, rows, 2 * LANES), BF)
+    operand = (3, TAPS, rows, 2 * LANES)
+    far = pl.BlockSpec(memory_space=pltpu.HBM)
+    weights = pl.pallas_call(
+        functools.partial(weights_kernel, dims),
+        out_shape=jax.ShapeDtypeStruct((3, kernels * TILE, span * LANES), BF),
+        in_specs=[far] * 3,
+        out_specs=vm,
+        scratch_shapes=[
+            pltpu.VMEM((5, freqs, kernels), F32),
+            pltpu.VMEM((freqs, kernels), F32),
+            pltpu.VMEM((freqs, kernels), F32),
+            pltpu.VMEM((span, kernels * TILE, LANES), F32),
+            pltpu.SemaphoreType.DMA((3,)),
+        ],
+        compiler_params=pltpu.CompilerParams(vmem_limit_bytes=8 * 1024 * 1024),
+    )(*map(distant, (jnp.transpose(stencil, (2, 0, 1)), step, shift)))
+    received, weights = lax.optimization_barrier((fetch_bins(bins), weights))
+    mine, theirs = swap_bins(received)
+    high, low = pl.pallas_call(
+        functools.partial(operands_kernel, dims),
+        out_shape=[jax.ShapeDtypeStruct(operand, BF)] * 2,
+        in_specs=[far],
+        out_specs=[vm] * 2,
+        scratch_shapes=[
+            pltpu.VMEM((2, grid, 2 * grid), F32),
+            pltpu.VMEM((4, padded, LANES), F32),
+            pltpu.SemaphoreType.DMA((1,)),
+        ],
+        compiler_params=pltpu.CompilerParams(vmem_limit_bytes=12 * 1024 * 1024),
+    )(distant(surface))
     return pl.pallas_call(
         functools.partial(levels_kernel, dims),
         out_shape=jax.ShapeDtypeStruct((2, freqs, half, lags.shape[0], strip, grid), F32),
-        in_specs=[sm] + [vm] * 7,
+        in_specs=[far, far] + [vm] * 5,
         out_specs=vm,
-        scratch_shapes=[
-            pltpu.VMEM((3, kernels * TILE, span * LANES), BF),
-            pltpu.VMEM((span, kernels * TILE, LANES), F32),
-            pltpu.VMEM((4, padded, LANES), F32),
-            pltpu.VMEM((levels, padded, LANES), jnp.int32),
-            operand, operand, operand, operand,
-            pltpu.VMEM((2, 4, rows, LANES), F32),
-        ],
-        compiler_params=pltpu.CompilerParams(vmem_limit_bytes=56 * 1024 * 1024),
-    )(lags, surface, own, mine, theirs, jnp.transpose(stencil, (2, 0, 1)), step, shift)
+        scratch_shapes=[pltpu.SMEM(lags.shape, jnp.int32), pltpu.VMEM((levels, padded, LANES), jnp.int32)]
+        + [pltpu.VMEM(operand, BF)] * 4
+        + [pltpu.VMEM((2, 4, rows, LANES), F32), pltpu.SemaphoreType.DMA((2,))],
+        compiler_params=pltpu.CompilerParams(vmem_limit_bytes=32 * 1024 * 1024),
+    )(distant(lags), distant(bins), mine, theirs, weights, high, low)
 
 
 column_tile = 16
@@ -379,7 +432,7 @@
     return lax.psum_scatter(image_part, "freq", scatter_dimension=2, tiled=True)
 
 
-def gather_bins(bins):
+def fetch_bins(bins):
     count, cores = lax.axis_size("depth"), lax.axis_size("freq")
     rounds = -(-(count - 1) // cores)
     received = []
@@ -390,6 +443,10 @@
             if turn < count:
                 pairs += [(place * cores + own, (place + turn) % count * cores + own) for place in range(count)]
         received.append(lax.ppermute(bins[0], ("depth", "freq"), pairs))
+    return received
+
+
+def swap_bins(received):
     mine = jnp.stack(received)
     return mine, lax.ppermute(mine, "freq", [(0, 1), (1, 0)])
 
@@ -400,16 +457,19 @@
     half = strips // cores
     lags, strip, grid = image.shape[3:]
     block = image[0] + lax.ppermute(image[1], "freq", [(0, 1), (1, 0)])
-    block = block[0] + lax.ppermute(block[1], "depth", [(d, d ^ 1) for d in range(count)])
     parts = []
     for number in range(half):
-        pairs = []
-        for z in range(strips):
-            for y in range(freqs):
-                for c in range(cores):
-                    target = c + cores * ((z % half + number) % half)
-                    pairs.append(((z * freqs + y) * cores + c, (target * freqs + y) * cores + z // half))
-        parts.append(lax.ppermute(block[number], ("depth", "freq"), pairs))
+        total = None
+        for turn in range(freqs):
+            pairs = []
+            for z in range(strips):
+                for y in range(freqs):
+                    for c in range(cores):
+                        target = c + cores * ((z % half + number) % half)
+                        pairs.append(((z * freqs + y) * cores + c, (target * freqs + (y ^ turn)) * cores + z // half))
+            part = lax.ppermute(block[turn, number], ("depth", "freq"), pairs)
+            total = part if total is None else total + part
+        parts.append(total)
     stacked = jnp.stack(parts)
     row = lax.axis_index("depth") // freqs // cores
     ordered = jnp.stack([lax.dynamic_index_in_dim(stacked, (row - r) % half, 0, keepdims=False) for r in range(half)], 1)
@@ -419,9 +479,8 @@
 def strip_body(surface, bins, stencil, phase_step, phase_shift, lags):
     freqs, grid = surface.shape[1], surface.shape[3]
     count = lax.axis_size("depth")
-    mine, theirs = gather_bins(bins)
     strip = grid * freqs // count
-    image = run_levels(lags, surface[0], bins, mine, theirs, stencil, phase_step, phase_shift, strip, count)
+    image = run_levels(lags, surface[0], bins, stencil, phase_step, phase_shift, strip, count)
     return spread_image(image, freqs)
 
 

time: 52.3 us -> 45.1 us (0.86)
  waiting for transfers between devices: 15.7 us -> 8.16 us
  local copies, waits for them, and re-layouts: 2.49 us -> 0.75 us
  starting transfers between devices: 16.9 us -> 18.3 us
    ppermute x8 -> x9, waiting for transfers between devices: 14.5 us -> 6.65 us  [the longest x4 5.98 us: spread_image(): part = lax.ppermute(block[turn, number], ('depth', 'freq'), pairs)]
    pallas_call x0 -> x2, Pallas kernels: none -> 5.4 us  [the longest x1 2.98 us: run_levels(): pl.pallas_call(functools.partial(operands_kernel, dims), out_shape=[jax.S...]
    pallas_call x1, Pallas kernels: 16.8 us -> 11.9 us  [run_levels(): pl.pallas_call(functools.partial(levels_kernel, dims), out_shape=jax.Shap...]
    ppermute x8 -> x9, starting transfers between devices: 16.5 us -> 18.2 us  [the longest x4 6.69 us: spread_image(): part = lax.ppermute(block[turn, number], ('depth', 'freq'), pairs)]
    squeeze x1, local copies, waits for them, and re-layouts: 1.04 us -> 0.02 us  [spread_image(): block = image[0] + lax.ppermute(image[1], 'freq', [(0, 1), (1, 0)])]
    unnamed x6 -> x0, local copies, waits for them, and re-layouts: 0.72 us -> none
  transfers between devices with their start and end apart: 9 -> 10, of which waited for: 8 -> 5; matrix products, arithmetic and copies ran while one was open for 0% -> 0% of each run, Pallas kernels for 0% -> 12%
where the time goes in v3:
time: 45.1 us; the launch traced here: 44.8 us
  starting transfers between devices  18.3 us (41%)
  Pallas kernels  17.3 us (38%)
  waiting for transfers between devices  8.16 us (18%)
  local copies, waits for them, and re-layouts  0.75 us (2%)
    pallas_call x1, Pallas kernels, run_levels(): pl.pallas_call(functools.partial(levels_kernel, dims), out_shape=jax.Shap...  11.9 us
    ppermute x4, starting transfers between devices, spread_image(): part = lax.ppermute(block[turn, number], ('depth', 'freq'), pairs)  6.69 us
    ppermute x4, starting transfers between devices, fetch_bins(): received.append(lax.ppermute(bins[0], ('depth', 'freq'), pairs))  6.03 us
    ppermute x4, waiting for transfers between devices, spread_image(): part = lax.ppermute(block[turn, number], ('depth', 'freq'), pairs)  5.98 us
    ppermute x1, starting transfers between devices, swap_bins(): return (mine, lax.ppermute(mine, 'freq', [(0, 1), (1, 0)]))  5.5 us
    pallas_call x1, Pallas kernels, run_levels(): pl.pallas_call(functools.partial(operands_kernel, dims), out_shape=[jax.S...  2.98 us
    pallas_call x1, Pallas kernels, run_levels(): pl.pallas_call(functools.partial(weights_kernel, dims), out_shape=jax.Sha...  2.41 us
    ppermute x1, waiting for transfers between devices, spread_image(): block = image[0] + lax.ppermute(image[1], 'freq', [(0, 1), (1, 0)])  1.51 us
  transfers between devices with their start and end apart: 10, of which 5 were waited for; matrix products, arithmetic and copies ran while one was open for 0% of the time, Pallas kernels for 12%

profile of v3, /device:TPU:1, one launch (start us, length us, event | category | flops | bytes accessed | tf_op | source)
XLA Modules:
  0.0 44.8 jit_solution(3529683857851566428)
XLA Ops:
  0.0 4.1 %collective-permute-start = (s32[128,128]{1,0:T(8,128)}, s32[128,128]{1,0:T(8,128)S(1)}, u32[]{:S(2)}, u32[]{:S(2)}) collective-permute-start(s32[128,128]{1,0:T(8,128)} %bitcast.32), channel_id=1, source_target_pairs={{0,2},{2,4},{4,6},{6,8},{8,10},{10,12},{12,14},{14,0},{1,11},{3,13... | collective-permute-start | bytes 196616 | tf_op jit(solution)/shard_map/ppermute | solution.py:445
  4.1 1.1 %collective-permute-start.1 = (s32[128,128]{1,0:T(8,128)}, s32[128,128]{1,0:T(8,128)S(1)}, u32[]{:S(2)}, u32[]{:S(2)}) collective-permute-start(s32[128,128]{1,0:T(8,128)} %bitcast.33), channel_id=1, source_target_pairs={{0,4},{2,6},{4,8},{6,10},{8,12},{10,14},{12,0},{14,2},{1,13},{3,15... | collective-permute-start | bytes 196616 | tf_op jit(solution)/shard_map/ppermute | solution.py:445
  5.2 0.2 collective-permute-start.2
  5.4 0.7 %collective-permute-start.3 = (s32[128,128]{1,0:T(8,128)}, s32[128,128]{1,0:T(8,128)S(1)}, u32[]{:S(2)}, u32[]{:S(2)}) collective-permute-start(s32[128,128]{1,0:T(8,128)} %bitcast.35), channel_id=1, source_target_pairs={{0,8},{2,10},{4,12},{6,14},{8,0},{10,2},{12,4},{14,6},{16,24},{18,... | collective-permute-start | bytes 196616 | tf_op jit(solution)/shard_map/ppermute | solution.py:445
  6.0 2.4 %shard_map.64.weights = bf16[3,128,1280]{2,1,0:T(8,128)(2,1)S(1)} custom-call(f32[5,2,8]{2,1,0:T(2,128)} %bitcast.40, f32[2,8]{1,0:T(2,128)} %step_far.1, f32[2,8]{1,0:T(2,128)} %shift_far.1), custom_call_target="tpu_custom_call" | custom-call | tf_op jit(solution)/shard_map/pallas_call | solution.py:239
  8.5 0.0 collective-permute-done
  8.5 0.0 collective-permute-done.1
  8.5 0.7 %collective-permute-done.2 = s32[128,128]{1,0:T(8,128)S(1)} collective-permute-done((s32[128,128]{1,0:T(8,128)}, s32[128,128]{1,0:T(8,128)S(1)}, u32[]{:S(2)}, u32[]{:S(2)}) %collective-permute-start.2) | collective-permute-done | bytes 65568 | tf_op jit(solution)/shard_map/ppermute | solution.py:445
  9.1 0.0 collective-permute-done.3
  9.2 5.5 %collective-permute-start.4 = (s32[4,128,128]{2,1,0:T(8,128)S(1)}, s32[4,128,128]{2,1,0:T(8,128)S(1)}, u32[]{:S(2)}, u32[]{:S(2)}) collective-permute-start(s32[4,128,128]{2,1,0:T(8,128)S(1)} %pad_add_fusion.mine), channel_id=1, source_target_pairs={{0,1},{1,0},{2,3},{3,2},{4,5},{5,4},{6,7},{7,6},{8,9},{9,8},{10,11... | collective-permute-start | bytes 786440 | tf_op jit(solution)/shard_map/ppermute | solution.py:451
  14.7 3.0 %shard_map.65 = (bf16[3,13,144,256]{3,2,1,0:T(8,128)(2,1)S(1)}, bf16[3,13,144,256]{3,2,1,0:T(8,128)(2,1)S(1)}) custom-call(f32[2,2,128,256]{3,2,1,0:T(8,128)} %bitcast.31), custom_call_target="tpu_custom_call" | custom-call | tf_op jit(solution)/shard_map/pallas_call | solution.py:255
  17.7 0.0 collective-permute-done.4.theirs
  17.7 11.9 %shard_map.66 = f32[2,2,2,4,32,128]{5,4,3,2,1,0:T(8,128)S(1)} custom-call(s32[4]{0:T(128)} %lags_far.1, s32[1,128,128]{2,1,0:T(8,128)} %own.1, s32[4,128,128]{2,1,0:T(8,128)S(1)} %pad_add_fusion.mine, s32[4,128,128]{2,1,0:T(8,128)S(1)} %collective-permute-done.4.theirs, bf16[3,128,1280]{2,1,0:T(8,128)(2,1)S(1)} %shard_map.64.weights, ...), custom_call_target="tpu_custom_call" | custom-call | tf_op jit(solution)/shard_map/pallas_call | solution.py:267
  29.6 0.1 collective-permute-start.5
  29.7 1.5 %collective-permute-done.5 = f32[2,2,4,32,128]{4,3,2,1,0:T(8,128)S(1)} collective-permute-done((f32[2,2,4,32,128]{4,3,2,1,0:T(8,128)S(1)}, f32[2,2,4,32,128]{4,3,2,1,0:T(8,128)S(1)}, u32[]{:S(2)}, u32[]{:S(2)}) %collective-permute-start.5) | collective-permute-done | bytes 262176 | tf_op jit(solution)/shard_map/ppermute | solution.py:459
  31.3 2.4 %collective-permute-start.8 = (f32[4,32,128]{2,1,0:T(8,128)S(1)}, f32[4,32,128]{2,1,0:T(8,128)S(1)}, u32[]{:S(2)}, u32[]{:S(2)}) collective-permute-start(f32[4,32,128]{2,1,0:T(8,128)S(1)} %get-tuple-element.20), channel_id=1, source_target_pairs={{0,8},{1,12},{2,10},{3,14},{4,0},{5,4},{6,2},{7,6},{8,9},{9,13},{1... | collective-permute-start | bytes 196616 | tf_op jit(solution)/shard_map/ppermute | solution.py:470
  33.7 2.3 %collective-permute-start.9 = (f32[4,32,128]{2,1,0:T(8,128)S(1)}, f32[4,32,128]{2,1,0:T(8,128)S(1)}, u32[]{:S(2)}, u32[]{:S(2)}) collective-permute-start(f32[4,32,128]{2,1,0:T(8,128)S(1)} %get-tuple-element.19), channel_id=1, source_target_pairs={{0,10},{1,14},{2,8},{3,12},{4,2},{5,6},{6,0},{7,4},{8,11},{9,15},{... | collective-permute-start | bytes 196616 | tf_op jit(solution)/shard_map/ppermute | solution.py:470
  36.0 1.9 %collective-permute-start.6 = (f32[4,32,128]{2,1,0:T(8,128)S(1)}, f32[4,32,128]{2,1,0:T(8,128)S(1)}, u32[]{:S(2)}, u32[]{:S(2)}) collective-permute-start(f32[4,32,128]{2,1,0:T(8,128)S(1)} %get-tuple-element.22), channel_id=1, source_target_pairs={{0,0},{1,4},{2,2},{3,6},{4,8},{5,12},{6,10},{7,14},{8,1},{9,5},{10... | collective-permute-start | bytes 196616 | tf_op jit(solution)/shard_map/ppermute | solution.py:470
  37.9 0.1 collective-permute-start.7
  38.0 0.0 collective-permute-done.8
  38.0 2.1 %collective-permute-done.9 = f32[4,32,128]{2,1,0:T(8,128)S(1)} collective-permute-done((f32[4,32,128]{2,1,0:T(8,128)S(1)}, f32[4,32,128]{2,1,0:T(8,128)S(1)}, u32[]{:S(2)}, u32[]{:S(2)}) %collective-permute-start.9) | collective-permute-done | bytes 65568 | tf_op jit(solution)/shard_map/ppermute | solution.py:470
  40.1 2.4 %collective-permute-done.6 = f32[4,32,128]{2,1,0:T(8,128)S(1)} collective-permute-done((f32[4,32,128]{2,1,0:T(8,128)S(1)}, f32[4,32,128]{2,1,0:T(8,128)S(1)}, u32[]{:S(2)}, u32[]{:S(2)}) %collective-permute-start.6) | collective-permute-done | bytes 65568 | tf_op jit(solution)/shard_map/ppermute | solution.py:470
  42.5 1.5 %collective-permute-done.7 = f32[4,32,128]{2,1,0:T(8,128)S(1)} collective-permute-done((f32[4,32,128]{2,1,0:T(8,128)S(1)}, f32[4,32,128]{2,1,0:T(8,128)S(1)}, u32[]{:S(2)}, u32[]{:S(2)}) %collective-permute-start.7) | collective-permute-done | bytes 65568 | tf_op jit(solution)/shard_map/ppermute | solution.py:470
  44.1 0.7 %reshape.5 = f32[1,4,8192]{2,1,0:T(4,128)} reshape(f32[4,2,32,128]{3,2,1,0:T(8,128)S(1)} %pad_maximum_fusion) | data formatting | bytes 262144 | tf_op jit(solution)/shard_map/reshape | solution.py:476
  (8 shorter events, 0.2 us)
Async XLA Ops:
  0.0 8.5 %collective-permute-start = (s32[128,128]{1,0:T(8,128)}, s32[128,128]{1,0:T(8,128)S(1)}, u32[]{:S(2)}, u32[]{:S(2)}) collective-permute-start(s32[128,128]{1,0:T(8,128)} %bitcast.32), channel_id=1, source_target_pairs={{0,2},{2,4},{4,6},{6,8},{8,10},{10,12},{12,14},{14,0},{1,11},{3,13... | collective-permute-start | bytes 196616 | tf_op jit(solution)/shard_map/ppermute | solution.py:445
  4.1 4.4 %collective-permute-start.1 = (s32[128,128]{1,0:T(8,128)}, s32[128,128]{1,0:T(8,128)S(1)}, u32[]{:S(2)}, u32[]{:S(2)}) collective-permute-start(s32[128,128]{1,0:T(8,128)} %bitcast.33), channel_id=1, source_target_pairs={{0,4},{2,6},{4,8},{6,10},{8,12},{10,14},{12,0},{14,2},{1,13},{3,15... | collective-permute-start | bytes 196616 | tf_op jit(solution)/shard_map/ppermute | solution.py:445
  5.2 4.0 %collective-permute-start.2 = (s32[128,128]{1,0:T(8,128)}, s32[128,128]{1,0:T(8,128)S(1)}, u32[]{:S(2)}, u32[]{:S(2)}) collective-permute-start(s32[128,128]{1,0:T(8,128)} %bitcast.34), channel_id=1, source_target_pairs={{0,6},{2,8},{4,10},{6,12},{8,14},{10,0},{12,2},{14,4},{1,15},{3,1}... | collective-permute-start | bytes 196616 | tf_op jit(solution)/shard_map/ppermute | solution.py:445
  5.4 3.8 %collective-permute-start.3 = (s32[128,128]{1,0:T(8,128)}, s32[128,128]{1,0:T(8,128)S(1)}, u32[]{:S(2)}, u32[]{:S(2)}) collective-permute-start(s32[128,128]{1,0:T(8,128)} %bitcast.35), channel_id=1, source_target_pairs={{0,8},{2,10},{4,12},{6,14},{8,0},{10,2},{12,4},{14,6},{16,24},{18,... | collective-permute-start | bytes 196616 | tf_op jit(solution)/shard_map/ppermute | solution.py:445
  9.2 8.5 %collective-permute-start.4 = (s32[4,128,128]{2,1,0:T(8,128)S(1)}, s32[4,128,128]{2,1,0:T(8,128)S(1)}, u32[]{:S(2)}, u32[]{:S(2)}) collective-permute-start(s32[4,128,128]{2,1,0:T(8,128)S(1)} %pad_add_fusion.mine), channel_id=1, source_target_pairs={{0,1},{1,0},{2,3},{3,2},{4,5},{5,4},{6,7},{7,6},{8,9},{9,8},{10,11... | collective-permute-start | bytes 786440 | tf_op jit(solution)/shard_map/ppermute | solution.py:451
  29.6 1.6 %collective-permute-start.5 = (f32[2,2,4,32,128]{4,3,2,1,0:T(8,128)S(1)}, f32[2,2,4,32,128]{4,3,2,1,0:T(8,128)S(1)}, u32[]{:S(2)}, u32[]{:S(2)}) collective-permute-start(f32[2,2,4,32,128]{4,3,2,1,0:T(8,128)S(1)} %slice_bitcast_fusion), channel_id=1, source_target_pairs={{0,1},{1,0},{2,3},{3,2},{4,5},{5,4},{6,7},{7,6},{8,9},{9,8},{10,11... | collective-permute-start | bytes 786440 | tf_op jit(solution)/shard_map/ppermute | solution.py:459
  31.3 6.7 %collective-permute-start.8 = (f32[4,32,128]{2,1,0:T(8,128)S(1)}, f32[4,32,128]{2,1,0:T(8,128)S(1)}, u32[]{:S(2)}, u32[]{:S(2)}) collective-permute-start(f32[4,32,128]{2,1,0:T(8,128)S(1)} %get-tuple-element.20), channel_id=1, source_target_pairs={{0,8},{1,12},{2,10},{3,14},{4,0},{5,4},{6,2},{7,6},{8,9},{9,13},{1... | collective-permute-start | bytes 196616 | tf_op jit(solution)/shard_map/ppermute | solution.py:470
  33.7 6.4 %collective-permute-start.9 = (f32[4,32,128]{2,1,0:T(8,128)S(1)}, f32[4,32,128]{2,1,0:T(8,128)S(1)}, u32[]{:S(2)}, u32[]{:S(2)}) collective-permute-start(f32[4,32,128]{2,1,0:T(8,128)S(1)} %get-tuple-element.19), channel_id=1, source_target_pairs={{0,10},{1,14},{2,8},{3,12},{4,2},{5,6},{6,0},{7,4},{8,11},{9,15},{... | collective-permute-start | bytes 196616 | tf_op jit(solution)/shard_map/ppermute | solution.py:470
  36.0 6.5 %collective-permute-start.6 = (f32[4,32,128]{2,1,0:T(8,128)S(1)}, f32[4,32,128]{2,1,0:T(8,128)S(1)}, u32[]{:S(2)}, u32[]{:S(2)}) collective-permute-start(f32[4,32,128]{2,1,0:T(8,128)S(1)} %get-tuple-element.22), channel_id=1, source_target_pairs={{0,0},{1,4},{2,2},{3,6},{4,8},{5,12},{6,10},{7,14},{8,1},{9,5},{10... | collective-permute-start | bytes 196616 | tf_op jit(solution)/shard_map/ppermute | solution.py:470
  37.9 6.1 %collective-permute-start.7 = (f32[4,32,128]{2,1,0:T(8,128)S(1)}, f32[4,32,128]{2,1,0:T(8,128)S(1)}, u32[]{:S(2)}, u32[]{:S(2)}) collective-permute-start(f32[4,32,128]{2,1,0:T(8,128)S(1)} %get-tuple-element.21), channel_id=1, source_target_pairs={{0,2},{1,6},{2,0},{3,4},{4,10},{5,14},{6,8},{7,12},{8,3},{9,7},{10... | collective-permute-start | bytes 196616 | tf_op jit(solution)/shard_map/ppermute | solution.py:470

commit v4 on v3

--- a/solution.py
+++ b/solution.py
@@ -14,6 +14,8 @@
 TAPS = 13
 HALF = 6
 TILE = 16
+STRIPS = 2
+EDGE = 8
 WIN = 32
 LANES = 128
 BF = jnp.bfloat16
@@ -65,8 +67,9 @@
     return high, (value - high.astype(F32)).astype(BF)
 
 
-def tile_counts(levels, strip):
-    return [-(-(strip + 2 * HALF * (levels - 1 - level)) // TILE) for level in range(levels)]
+def tile_counts(levels, grid):
+    reaches = [grid // STRIPS + HALF * (levels - 1 - level) for level in range(levels)]
+    return [min(-(-reach // TILE), grid // TILE) for reach in reaches]
 
 
 def spread(high, low, row, planes):
@@ -100,7 +103,7 @@
 
 
 def weights_kernel(dims, stencil_far, step_far, shift_far, weights, stencil, step, shift, wide, sems):
-    levels, kernels, freqs, strip, grid, lag_count = dims
+    levels, kernels, freqs, grid, lag_count = dims
     freq = lax.rem(lax.axis_index("depth"), freqs)
     span = TAPS * WIN
     fetch(((stencil_far, stencil), (step_far, step), (shift_far, shift)), sems)
@@ -115,122 +118,124 @@
         long_low = jnp.concatenate([taps_low, rest], axis=1)
         line = long_high + pltpu.roll(long_low, span, 1) + pltpu.roll(long_high, 2 * span, 1)
         for row in range(TILE):
-            moved = pltpu.roll(line, row, 1) if row else line
+            moved = pltpu.roll(line, row + EDGE - HALF, 1)
             for chunk in range(chunks):
                 wide[chunk, pl.ds(row, kernels, stride=TILE), :] = moved[:, chunk * LANES : (chunk + 1) * LANES]
         for chunk in range(chunks):
             weights[which, :, chunk * LANES : (chunk + 1) * LANES] = wide[chunk].astype(BF)
 
 
-def operands_kernel(dims, surface, high, low, fields, grid_pad, sems):
-    levels, kernels, freqs, strip, grid, lag_count = dims
-    halo = HALF * levels
-    depth = lax.axis_index("depth")
-    freq, strip_index = lax.rem(depth, freqs), lax.div(depth, freqs)
-    base = strip_index * strip
+def operands_kernel(dims, surface, high, low, fields, padded, sems):
+    levels, kernels, freqs, grid, lag_count = dims
+    freq = lax.rem(lax.axis_index("depth"), freqs)
     fetch(((surface.at[freq], fields),), sems)
-    grid_pad[...] = jnp.zeros(grid_pad.shape, F32)
     for field in range(2):
         for part in range(2):
-            grid_pad[2 * field + part, halo : halo + grid, :] = fields[field, :, part * LANES : (part + 1) * LANES]
+            plane = 2 * field + part
+            padded[plane, :EDGE, :] = jnp.zeros((EDGE, LANES), F32)
+            padded[plane, EDGE : EDGE + grid, :] = fields[field, :, part * LANES : (part + 1) * LANES]
+            padded[plane, EDGE + grid :, :] = jnp.zeros((EDGE, LANES), F32)
 
     def fill(index, carry):
         row = pl.multiple_of(index * TILE, TILE)
-        spread(high, low, row, [grid_pad[plane, pl.ds(base + row, TILE), :] for plane in range(4)])
+        spread(high, low, row, [padded[plane, pl.ds(row, TILE), :] for plane in range(4)])
         return carry
 
-    lax.fori_loop(0, tile_counts(levels, strip)[0] + 1, fill, 0)
+    lax.fori_loop(0, grid // TILE + 1, fill, 0)
 
 
 def levels_kernel(dims, lags_far, own, mine, theirs, weights, high, low, image,
-                  lags, bins_pad, high0, low0, high1, low1, state, sems):
-    levels, kernels, freqs, strip, grid, lag_count = dims
-    halo = HALF * levels
+                  lags, bins, high0, low0, high1, low1, state, sems):
+    levels, kernels, freqs, grid, lag_count = dims
     depth, core = lax.axis_index("depth"), lax.axis_index("freq")
-    freq, strip_index = lax.rem(depth, freqs), lax.div(depth, freqs)
-    base = strip_index * strip
-    rounds = mine.shape[0]
-    spots = kernels * TILE
+    freq, layer = lax.rem(depth, freqs), lax.div(depth, freqs)
+    strip_index, group = lax.rem(layer, STRIPS), lax.div(layer, STRIPS)
+    strip = grid // STRIPS
     span = TAPS * WIN
-    bins_pad[...] = jnp.full(bins_pad.shape, kernels, jnp.int32)
+    counts = tile_counts(levels, grid)
     for piece, other in ((mine, core), (theirs, 1 - core)):
-        for number in range(rounds):
-            turn = 1 + number + other * rounds
-            bins_pad[lax.rem(depth - turn + 2 * levels, levels), halo : halo + grid, :] = piece[number]
-    fetch(((lags_far, lags), (own.at[0], bins_pad.at[depth, pl.ds(halo, grid), :])), sems)
-    def advance(high, low, level, row):
-        cell_bins = bins_pad[level, pl.ds(base + HALF * (level + 1) + row, TILE), :]
-        sums = []
-        for which in range(3):
-            rhs = high[which, :, pl.ds(row, WIN), :].reshape(span, 2 * LANES)
-            rhs_low = low[which, :, pl.ds(row, WIN), :].reshape(span, 2 * LANES)
-            out = jnp.dot(weights[which, :, : 3 * span], jnp.concatenate([rhs, rhs, rhs_low], axis=0), preferred_element_type=F32)
+        for number in range(mine.shape[0]):
+            turn = 1 + number + other * mine.shape[0]
+            bins[lax.rem(depth - turn + 2 * levels, levels)] = piece[number]
+    fetch(((lags_far, lags), (own.at[0], bins.at[depth])), sems)
+
+    def descend(forward):
+        def row_of(tile):
+            return (tile if forward else grid // TILE - 1 - tile) * TILE
+
+        def spread_between(there, number, before, after):
+            planes = []
+            for old, new in zip(before, after):
+                halves = [old[EDGE:], new[:EDGE]] if forward else [new[EDGE:], old[:EDGE]]
+                planes.append(jnp.concatenate(halves, axis=0))
+            spread(*there, (number if forward else grid // TILE - number) * TILE, planes)
+
+        def advance(high, low, level, row):
+            cell_bins = bins[level, pl.ds(row, TILE), :]
+            sums = []
+            for which in range(3):
+                rhs = high[which, :, pl.ds(row, WIN), :].reshape(span, 2 * LANES)
+                rhs_low = low[which, :, pl.ds(row, WIN), :].reshape(span, 2 * LANES)
+                out = jnp.dot(weights[which, :, : 3 * span], jnp.concatenate([rhs, rhs, rhs_low], axis=0), preferred_element_type=F32)
+                for field in range(2):
+                    chosen = jnp.zeros((TILE, LANES), F32)
+                    for k in range(kernels):
+                        chosen = jnp.where(cell_bins == k, out[k * TILE : (k + 1) * TILE, field * LANES : (field + 1) * LANES], chosen)
+                    sums.append(chosen)
+            planes = []
             for field in range(2):
-                chosen = jnp.zeros((TILE, LANES), F32)
-                for k in range(kernels):
-                    chosen = jnp.where(cell_bins == k, out[k * TILE : (k + 1) * TILE, field * LANES : (field + 1) * LANES], chosen)
-                sums.append(chosen)
-        planes = []
-        for field in range(2):
-            planes.append(sums[field] - sums[2 + field])
-            planes.append(sums[field] + sums[4 + field])
-        for plane in range(4):
-            state[level % 2, plane, pl.ds(row, TILE), :] = planes[plane]
-        return tuple(planes)
-
-    def correlate(level):
-        start = halo - HALF * (level + 1)
-        planes = [state[level % 2, plane, pl.ds(start, strip), :] for plane in range(4)]
-        lanes = lax.broadcasted_iota(jnp.int32, (strip, LANES), 1)
-        z, y = level // freqs, level % freqs
-        half = image.shape[2]
-        place = (lax.rem(z % 2 + core, 2), lax.rem(y + freq, 2), lax.rem(z // 2 + strip_index * (half - 1), half))
-        for number in range(lag_count):
-            offset = lags[number]
-            away = lax.rem(LANES - offset, LANES)
-            s_re, s_im = pltpu.roll(planes[0], offset, 1), pltpu.roll(planes[1], offset, 1)
-            r_re, r_im = pltpu.roll(planes[2], away, 1), pltpu.roll(planes[3], away, 1)
-            inside = (lanes >= offset) & (lanes < LANES - offset)
-            image[place[0], place[1], place[2], number] = jnp.where(inside, s_re * r_re + s_im * r_im, 0.0)
-
-    counts = tile_counts(levels, strip)
-    slots = [(high, low), (high1, low1)] + [(high0, low0), (high1, low1)] * levels
-    planes = None
-    for level in range(levels):
-        here, there = slots[level], slots[level + 1]
-        if planes is None:
-            planes = advance(*here, level, 0)
-        else:
-            last = (counts[level - 1] - 1) * TILE
-            if last < WIN:
-                spread(*here, last, planes)
-                first = advance(*here, level, 0)
-            else:
-                first = advance(*here, level, 0)
-                spread(*here, last, planes)
-            correlate(level - 1)
-            planes = first
-
-        def tile(number, carried, here=here, there=there, level=level):
-            row = number * TILE
-            fresh = advance(*here, level, row)
-            if level < levels - 1:
-                spread(*there, row - TILE, carried)
-            return fresh
-
-        for number in range(1, counts[level]):
-            planes = tile(number, planes)
-    correlate(levels - 1)
-
-
-def run_levels(lags, surface, bins, stencil, step, shift, strip, levels):
+                planes.append(sums[field] - sums[2 + field])
+                planes.append(sums[field] + sums[4 + field])
+            for plane in range(4):
+                state[level % 2, plane, pl.ds(row, TILE), :] = planes[plane]
+            return tuple(planes)
+
+        def correlate(level):
+            start = 0 if forward else grid - strip
+            planes = [state[level % 2, plane, pl.ds(start, strip), :] for plane in range(4)]
+            lanes = lax.broadcasted_iota(jnp.int32, (strip, LANES), 1)
+            z, y = level // freqs, level % freqs
+            place = (z % STRIPS ^ core) * freqs + (y ^ freq)
+            place = jnp.where(group == z // STRIPS, place, STRIPS * freqs)
+            for number in range(lag_count):
+                offset = lags[number]
+                away = lax.rem(LANES - offset, LANES)
+                s_re, s_im = pltpu.roll(planes[0], offset, 1), pltpu.roll(planes[1], offset, 1)
+                r_re, r_im = pltpu.roll(planes[2], away, 1), pltpu.roll(planes[3], away, 1)
+                inside = (lanes >= offset) & (lanes < LANES - offset)
+                image[place, number] = jnp.where(inside, s_re * r_re + s_im * r_im, 0.0)
+
+        slots = [(high, low), (high1, low1)] + [(high0, low0), (high1, low1)] * levels
+        zeros = tuple(jnp.zeros((TILE, LANES), F32) for _ in range(4))
+        before = after = zeros
+        for level in range(levels):
+            here, there = slots[level], slots[level + 1]
+            first = advance(*here, level, row_of(0))
+            if level:
+                spread_between(here, counts[level - 1] - 1, before, after)
+                if counts[level] == counts[level - 1]:
+                    spread_between(here, counts[level], after, zeros)
+                correlate(level - 1)
+            before, after = zeros, first
+            for number in range(1, counts[level]):
+                fresh = advance(*here, level, row_of(number))
+                if level < levels - 1:
+                    spread_between(there, number - 1, before, after)
+                before, after = after, fresh
+        correlate(levels - 1)
+
+    for number in range(STRIPS):
+
+        @pl.when(strip_index == number)
+        def _(number=number):
+            descend(number == 0)
+
+
+def run_levels(lags, surface, bins, stencil, step, shift, levels):
     freqs, _, grid, _ = surface.shape
     kernels = step.shape[1]
-    halo = HALF * levels
-    rows = (tile_counts(levels, strip)[0] + 1) * TILE
-    padded = max((grid - strip + rows + 7) // 8 * 8, halo + grid)
-    dims = (levels, kernels, freqs, strip, grid, lags.shape[0])
-    half = levels // freqs // 2
+    rows = grid + 2 * EDGE
+    dims = (levels, kernels, freqs, grid, lags.shape[0])
     span = -(-3 * TAPS * WIN // LANES)
     vm = pl.BlockSpec(memory_space=pltpu.VMEM)
     sm = pl.BlockSpec(memory_space=pltpu.SMEM)
@@ -259,19 +264,19 @@
         out_specs=[vm] * 2,
         scratch_shapes=[
             pltpu.VMEM((2, grid, 2 * grid), F32),
-            pltpu.VMEM((4, padded, LANES), F32),
+            pltpu.VMEM((4, rows, LANES), F32),
             pltpu.SemaphoreType.DMA((1,)),
         ],
         compiler_params=pltpu.CompilerParams(vmem_limit_bytes=12 * 1024 * 1024),
     )(distant(surface))
     return pl.pallas_call(
         functools.partial(levels_kernel, dims),
-        out_shape=jax.ShapeDtypeStruct((2, freqs, half, lags.shape[0], strip, grid), F32),
+        out_shape=jax.ShapeDtypeStruct((STRIPS * freqs + 1, lags.shape[0], grid // STRIPS, grid), F32),
         in_specs=[far, far] + [vm] * 5,
         out_specs=vm,
-        scratch_shapes=[pltpu.SMEM(lags.shape, jnp.int32), pltpu.VMEM((levels, padded, LANES), jnp.int32)]
+        scratch_shapes=[pltpu.SMEM(lags.shape, jnp.int32), pltpu.VMEM((levels, grid, LANES), jnp.int32)]
         + [pltpu.VMEM(operand, BF)] * 4
-        + [pltpu.VMEM((2, 4, rows, LANES), F32), pltpu.SemaphoreType.DMA((2,))],
+        + [pltpu.VMEM((2, 4, grid, LANES), F32), pltpu.SemaphoreType.DMA((2,))],
         compiler_params=pltpu.CompilerParams(vmem_limit_bytes=32 * 1024 * 1024),
     )(distant(lags), distant(bins), mine, theirs, weights, high, low)
 
@@ -453,53 +458,38 @@
 
 def spread_image(image, freqs):
     count, cores = lax.axis_size("depth"), lax.axis_size("freq")
-    strips = count // freqs
-    half = strips // cores
-    lags, strip, grid = image.shape[3:]
-    block = image[0] + lax.ppermute(image[1], "freq", [(0, 1), (1, 0)])
-    parts = []
-    for number in range(half):
-        total = None
-        for turn in range(freqs):
-            pairs = []
-            for z in range(strips):
-                for y in range(freqs):
-                    for c in range(cores):
-                        target = c + cores * ((z % half + number) % half)
-                        pairs.append(((z * freqs + y) * cores + c, (target * freqs + (y ^ turn)) * cores + z // half))
-            part = lax.ppermute(block[turn, number], ("depth", "freq"), pairs)
-            total = part if total is None else total + part
-        parts.append(total)
-    stacked = jnp.stack(parts)
-    row = lax.axis_index("depth") // freqs // cores
-    ordered = jnp.stack([lax.dynamic_index_in_dim(stacked, (row - r) % half, 0, keepdims=False) for r in range(half)], 1)
-    return ordered.reshape(1, lags, half * strip * grid)
+    lags, strip, grid = image.shape[1:]
+    block = image[:freqs] + lax.ppermute(image[freqs : 2 * freqs], "freq", [(0, 1), (1, 0)])
+    total = None
+    for turn in reversed(range(freqs)):
+        pairs = []
+        for depth in range(count):
+            z, y = depth // freqs, depth % freqs
+            for c in range(cores):
+                target = (z // STRIPS * STRIPS + c) * freqs + (y ^ turn)
+                pairs.append((depth * cores + c, target * cores + z % STRIPS))
+        part = lax.ppermute(block[turn], ("depth", "freq"), pairs)
+        total = part if total is None else total + part
+    return total.reshape(1, lags, strip * grid)
 
 
 def strip_body(surface, bins, stencil, phase_step, phase_shift, lags):
-    freqs, grid = surface.shape[1], surface.shape[3]
-    count = lax.axis_size("depth")
-    strip = grid * freqs // count
-    image = run_levels(lags, surface[0], bins, stencil, phase_step, phase_shift, strip, count)
-    return spread_image(image, freqs)
+    image = run_levels(lags, surface[0], bins, stencil, phase_step, phase_shift, lax.axis_size("depth"))
+    return spread_image(image, surface.shape[1])
 
 
 def body(surface, bins, stencil, phase_step, phase_shift, lags):
     count, cores = lax.axis_size("depth"), lax.axis_size("freq")
     freqs, grid = surface.shape[1], surface.shape[3]
-    strips = count // freqs
     fits = (
         surface.shape[0] == 1
         and bins.shape[0] == 1
         and grid == LANES
         and cores == 2
         and freqs == 2
-        and count % freqs == 0
-        and strips % cores == 0
-        and grid % strips == 0
-        and grid // strips % 8 == 0
-        and HALF * count <= grid // 2
-        and tile_counts(count, grid // strips)[1] < tile_counts(count, grid // strips)[0]
+        and count % (STRIPS * freqs) == 0
+        and count & (count - 1) == 0
+        and HALF * (count - 1) <= grid // 2
     )
     way = strip_body if fits else pipeline_body
     return way(surface, bins, stencil, phase_step, phase_shift, lags)

time: 45.1 us -> 42.5 us (0.942)
  starting transfers between devices: 18.3 us -> 13.8 us
  Pallas kernels: 17.3 us -> 19.2 us
    ppermute x5 -> x3, starting transfers between devices: 6.78 us -> 2.24 us  [the longest x2 2.15 us: spread_image(): part = lax.ppermute(block[turn], ('depth', 'freq'), pairs)]
    pallas_call x1, Pallas kernels: 11.9 us -> 13.7 us  [run_levels(): pl.pallas_call(functools.partial(levels_kernel, dims), out_shape=jax.Shap...]
    ppermute x4, waiting for transfers between devices: 0.67 us -> 1.72 us  [fetch_bins(): received.append(lax.ppermute(bins[0], ('depth', 'freq'), pairs))]
    ppermute x5 -> x3, waiting for transfers between devices: 7.49 us -> 6.64 us  [the longest x2 5.13 us: spread_image(): part = lax.ppermute(block[turn], ('depth', 'freq'), pairs)]
  transfers between devices with their start and end apart: 10 -> 8, of which waited for: 5 -> 5; matrix products, arithmetic and copies ran while one was open for 0% -> 0% of each run, Pallas kernels for 12% -> 13%
where the time goes in v4:
time: 42.5 us; the launch traced here: 42.3 us
  Pallas kernels  19.2 us (45%)
  starting transfers between devices  13.8 us (32%)
  waiting for transfers between devices  8.36 us (20%)
  local copies, waits for them, and re-layouts  0.75 us (2%)
    pallas_call x1, Pallas kernels, run_levels(): pl.pallas_call(functools.partial(levels_kernel, dims), out_shape=jax.Shap...  13.7 us
    ppermute x4, starting transfers between devices, fetch_bins(): received.append(lax.ppermute(bins[0], ('depth', 'freq'), pairs))  5.97 us
    ppermute x1, starting transfers between devices, swap_bins(): return (mine, lax.ppermute(mine, 'freq', [(0, 1), (1, 0)]))  5.61 us
    ppermute x2, waiting for transfers between devices, spread_image(): part = lax.ppermute(block[turn], ('depth', 'freq'), pairs)  5.13 us
    pallas_call x1, Pallas kernels, run_levels(): pl.pallas_call(functools.partial(operands_kernel, dims), out_shape=[jax.S...  2.98 us
    pallas_call x1, Pallas kernels, run_levels(): pl.pallas_call(functools.partial(weights_kernel, dims), out_shape=jax.Sha...  2.48 us
    ppermute x2, starting transfers between devices, spread_image(): part = lax.ppermute(block[turn], ('depth', 'freq'), pairs)  2.15 us
    ppermute x4, waiting for transfers between devices, fetch_bins(): received.append(lax.ppermute(bins[0], ('depth', 'freq'), pairs))  1.72 us
  transfers between devices with their start and end apart: 8, of which 5 were waited for; matrix products, arithmetic and copies ran while one was open for 0% of the time, Pallas kernels for 13%

profile of v4, /device:TPU:1, one launch (start us, length us, event | category | flops | bytes accessed | tf_op | source)
XLA Modules:
  0.0 42.3 jit_solution(4047944062242587656)
XLA Ops:
  0.0 0.7 %collective-permute-start.3 = (s32[128,128]{1,0:T(8,128)}, s32[128,128]{1,0:T(8,128)S(1)}, u32[]{:S(2)}, u32[]{:S(2)}) collective-permute-start(s32[128,128]{1,0:T(8,128)} %bitcast.12), channel_id=1, source_target_pairs={{0,8},{2,10},{4,12},{6,14},{8,0},{10,2},{12,4},{14,6},{16,24},{18,... | collective-permute-start | bytes 196616 | tf_op jit(solution)/shard_map/ppermute | solution.py:450
  0.7 5.1 %collective-permute-start.2 = (s32[128,128]{1,0:T(8,128)}, s32[128,128]{1,0:T(8,128)S(1)}, u32[]{:S(2)}, u32[]{:S(2)}) collective-permute-start(s32[128,128]{1,0:T(8,128)} %bitcast.13), channel_id=1, source_target_pairs={{0,6},{2,8},{4,10},{6,12},{8,14},{10,0},{12,2},{14,4},{1,15},{3,1}... | collective-permute-start | bytes 196616 | tf_op jit(solution)/shard_map/ppermute | solution.py:450
  5.8 0.2 collective-permute-start.1
  6.0 0.0 collective-permute-start
  6.0 2.5 %shard_map.64.weights = bf16[3,128,1280]{2,1,0:T(8,128)(2,1)S(1)} custom-call(f32[5,2,8]{2,1,0:T(2,128)} %bitcast.20, f32[2,8]{1,0:T(2,128)} %step_far.1, f32[2,8]{1,0:T(2,128)} %shift_far.1), custom_call_target="tpu_custom_call" | custom-call | tf_op jit(solution)/shard_map/pallas_call | solution.py:244
  8.5 0.0 collective-permute-done.3
  8.5 0.0 collective-permute-done.2
  8.5 0.6 %collective-permute-done.1 = s32[128,128]{1,0:T(8,128)S(1)} collective-permute-done((s32[128,128]{1,0:T(8,128)}, s32[128,128]{1,0:T(8,128)S(1)}, u32[]{:S(2)}, u32[]{:S(2)}) %collective-permute-start.1) | collective-permute-done | bytes 65568 | tf_op jit(solution)/shard_map/ppermute | solution.py:450
  9.1 1.1 %collective-permute-done = s32[128,128]{1,0:T(8,128)S(1)} collective-permute-done((s32[128,128]{1,0:T(8,128)}, s32[128,128]{1,0:T(8,128)S(1)}, u32[]{:S(2)}, u32[]{:S(2)}) %collective-permute-start) | collective-permute-done | bytes 65568 | tf_op jit(solution)/shard_map/ppermute | solution.py:450
  10.2 5.6 %collective-permute-start.4 = (s32[4,128,128]{2,1,0:T(8,128)S(1)}, s32[4,128,128]{2,1,0:T(8,128)S(1)}, u32[]{:S(2)}, u32[]{:S(2)}) collective-permute-start(s32[4,128,128]{2,1,0:T(8,128)S(1)} %pad_add_fusion.mine), channel_id=1, source_target_pairs={{0,1},{1,0},{2,3},{3,2},{4,5},{5,4},{6,7},{7,6},{8,9},{9,8},{10,11... | collective-permute-start | bytes 786440 | tf_op jit(solution)/shard_map/ppermute | solution.py:456
  15.8 3.0 %shard_map.65 = (bf16[3,13,144,256]{3,2,1,0:T(8,128)(2,1)S(1)}, bf16[3,13,144,256]{3,2,1,0:T(8,128)(2,1)S(1)}) custom-call(f32[2,2,128,256]{3,2,1,0:T(8,128)} %bitcast.11), custom_call_target="tpu_custom_call" | custom-call | tf_op jit(solution)/shard_map/pallas_call | solution.py:260
  18.8 0.0 collective-permute-done.4.theirs
  18.8 13.7 %shard_map.66 = f32[5,4,64,128]{3,2,1,0:T(8,128)S(1)} custom-call(s32[4]{0:T(128)} %lags_far.1, s32[1,128,128]{2,1,0:T(8,128)} %own.1, s32[4,128,128]{2,1,0:T(8,128)S(1)} %pad_add_fusion.mine, s32[4,128,128]{2,1,0:T(8,128)S(1)} %collective-permute-done.4.theirs, bf16[3,128,1280]{2,1,0:T(8,128)(2,1)S(1)} %shard_map.64.weights, ...), custom_call_target="tpu_custom_call" | custom-call | tf_op jit(solution)/shard_map/pallas_call | solution.py:272
  32.6 0.1 collective-permute-start.5
  32.7 1.5 %collective-permute-done.5 = f32[2,4,64,128]{3,2,1,0:T(8,128)S(1)} collective-permute-done((f32[2,4,64,128]{3,2,1,0:T(8,128)S(1)}, f32[2,4,64,128]{3,2,1,0:T(8,128)S(1)}, u32[]{:S(2)}, u32[]{:S(2)}) %collective-permute-start.5) | collective-permute-done | bytes 262176 | tf_op jit(solution)/shard_map/ppermute | solution.py:462
  34.2 1.9 %collective-permute-start.7 = (f32[4,64,128]{2,1,0:T(8,128)S(1)}, f32[4,64,128]{2,1,0:T(8,128)S(1)}, u32[]{:S(2)}, u32[]{:S(2)}) collective-permute-start(f32[4,64,128]{2,1,0:T(8,128)S(1)} %get-tuple-element.19), channel_id=1, source_target_pairs={{0,0},{1,4},{2,2},{3,6},{4,1},{5,5},{6,3},{7,7},{8,8},{9,12},{10,1... | collective-permute-start | bytes 393224 | tf_op jit(solution)/shard_map/ppermute | solution.py:471
  36.2 0.2 collective-permute-start.6
  36.4 4.1 %collective-permute-done.7 = f32[4,64,128]{2,1,0:T(8,128)S(1)} collective-permute-done((f32[4,64,128]{2,1,0:T(8,128)S(1)}, f32[4,64,128]{2,1,0:T(8,128)S(1)}, u32[]{:S(2)}, u32[]{:S(2)}) %collective-permute-start.7) | collective-permute-done | bytes 131104 | tf_op jit(solution)/shard_map/ppermute | solution.py:471
  40.5 1.0 %collective-permute-done.6 = f32[4,64,128]{2,1,0:T(8,128)S(1)} collective-permute-done((f32[4,64,128]{2,1,0:T(8,128)S(1)}, f32[4,64,128]{2,1,0:T(8,128)S(1)}, u32[]{:S(2)}, u32[]{:S(2)}) %collective-permute-start.6) | collective-permute-done | bytes 131104 | tf_op jit(solution)/shard_map/ppermute | solution.py:471
  41.5 0.7 %reshape.3 = f32[1,4,8192]{2,1,0:T(4,128)} reshape(f32[4,64,128]{2,1,0:T(8,128)S(1)} %add.7) | data formatting | bytes 262144 | tf_op jit(solution)/shard_map/reshape | solution.py:473
  (5 shorter events, 0.1 us)
Async XLA Ops:
  0.0 8.5 %collective-permute-start.3 = (s32[128,128]{1,0:T(8,128)}, s32[128,128]{1,0:T(8,128)S(1)}, u32[]{:S(2)}, u32[]{:S(2)}) collective-permute-start(s32[128,128]{1,0:T(8,128)} %bitcast.12), channel_id=1, source_target_pairs={{0,8},{2,10},{4,12},{6,14},{8,0},{10,2},{12,4},{14,6},{16,24},{18,... | collective-permute-start | bytes 196616 | tf_op jit(solution)/shard_map/ppermute | solution.py:450
  0.7 7.8 %collective-permute-start.2 = (s32[128,128]{1,0:T(8,128)}, s32[128,128]{1,0:T(8,128)S(1)}, u32[]{:S(2)}, u32[]{:S(2)}) collective-permute-start(s32[128,128]{1,0:T(8,128)} %bitcast.13), channel_id=1, source_target_pairs={{0,6},{2,8},{4,10},{6,12},{8,14},{10,0},{12,2},{14,4},{1,15},{3,1}... | collective-permute-start | bytes 196616 | tf_op jit(solution)/shard_map/ppermute | solution.py:450
  5.8 3.3 %collective-permute-start.1 = (s32[128,128]{1,0:T(8,128)}, s32[128,128]{1,0:T(8,128)S(1)}, u32[]{:S(2)}, u32[]{:S(2)}) collective-permute-start(s32[128,128]{1,0:T(8,128)} %bitcast.14), channel_id=1, source_target_pairs={{0,4},{2,6},{4,8},{6,10},{8,12},{10,14},{12,0},{14,2},{1,13},{3,15... | collective-permute-start | bytes 196616 | tf_op jit(solution)/shard_map/ppermute | solution.py:450
  6.0 4.2 %collective-permute-start = (s32[128,128]{1,0:T(8,128)}, s32[128,128]{1,0:T(8,128)S(1)}, u32[]{:S(2)}, u32[]{:S(2)}) collective-permute-start(s32[128,128]{1,0:T(8,128)} %bitcast.15), channel_id=1, source_target_pairs={{0,2},{2,4},{4,6},{6,8},{8,10},{10,12},{12,14},{14,0},{1,11},{3,13... | collective-permute-start | bytes 196616 | tf_op jit(solution)/shard_map/ppermute | solution.py:450
  10.2 8.6 %collective-permute-start.4 = (s32[4,128,128]{2,1,0:T(8,128)S(1)}, s32[4,128,128]{2,1,0:T(8,128)S(1)}, u32[]{:S(2)}, u32[]{:S(2)}) collective-permute-start(s32[4,128,128]{2,1,0:T(8,128)S(1)} %pad_add_fusion.mine), channel_id=1, source_target_pairs={{0,1},{1,0},{2,3},{3,2},{4,5},{5,4},{6,7},{7,6},{8,9},{9,8},{10,11... | collective-permute-start | bytes 786440 | tf_op jit(solution)/shard_map/ppermute | solution.py:456
  32.6 1.6 %collective-permute-start.5 = (f32[2,4,64,128]{3,2,1,0:T(8,128)S(1)}, f32[2,4,64,128]{3,2,1,0:T(8,128)S(1)}, u32[]{:S(2)}, u32[]{:S(2)}) collective-permute-start(f32[2,4,64,128]{3,2,1,0:T(8,128)S(1)} %slice.17), channel_id=1, source_target_pairs={{0,1},{1,0},{2,3},{3,2},{4,5},{5,4},{6,7},{7,6},{8,9},{9,8},{10,11... | collective-permute-start | bytes 786440 | tf_op jit(solution)/shard_map/ppermute | solution.py:462
  34.2 6.3 %collective-permute-start.7 = (f32[4,64,128]{2,1,0:T(8,128)S(1)}, f32[4,64,128]{2,1,0:T(8,128)S(1)}, u32[]{:S(2)}, u32[]{:S(2)}) collective-permute-start(f32[4,64,128]{2,1,0:T(8,128)S(1)} %get-tuple-element.19), channel_id=1, source_target_pairs={{0,0},{1,4},{2,2},{3,6},{4,1},{5,5},{6,3},{7,7},{8,8},{9,12},{10,1... | collective-permute-start | bytes 393224 | tf_op jit(solution)/shard_map/ppermute | solution.py:471
  36.2 5.4 %collective-permute-start.6 = (f32[4,64,128]{2,1,0:T(8,128)S(1)}, f32[4,64,128]{2,1,0:T(8,128)S(1)}, u32[]{:S(2)}, u32[]{:S(2)}) collective-permute-start(f32[4,64,128]{2,1,0:T(8,128)S(1)} %get-tuple-element.20), channel_id=1, source_target_pairs={{0,2},{1,6},{2,0},{3,4},{4,3},{5,7},{6,1},{7,5},{8,10},{9,14},{10,... | collective-permute-start | bytes 393224 | tf_op jit(solution)/shard_map/ppermute | solution.py:471

commit v5 on v4

--- a/solution.py
+++ b/solution.py
@@ -136,12 +136,8 @@
             padded[plane, EDGE : EDGE + grid, :] = fields[field, :, part * LANES : (part + 1) * LANES]
             padded[plane, EDGE + grid :, :] = jnp.zeros((EDGE, LANES), F32)
 
-    def fill(index, carry):
-        row = pl.multiple_of(index * TILE, TILE)
+    for row in range(0, grid + 1, TILE):
         spread(high, low, row, [padded[plane, pl.ds(row, TILE), :] for plane in range(4)])
-        return carry
-
-    lax.fori_loop(0, grid // TILE + 1, fill, 0)
 
 
 def levels_kernel(dims, lags_far, own, mine, theirs, weights, high, low, image,
@@ -203,7 +199,7 @@
                 s_re, s_im = pltpu.roll(planes[0], offset, 1), pltpu.roll(planes[1], offset, 1)
                 r_re, r_im = pltpu.roll(planes[2], away, 1), pltpu.roll(planes[3], away, 1)
                 inside = (lanes >= offset) & (lanes < LANES - offset)
-                image[place, number] = jnp.where(inside, s_re * r_re + s_im * r_im, 0.0)
+                image[place, pl.ds(number, strip, stride=lag_count), :] = jnp.where(inside, s_re * r_re + s_im * r_im, 0.0)
 
         slots = [(high, low), (high1, low1)] + [(high0, low0), (high1, low1)] * levels
         zeros = tuple(jnp.zeros((TILE, LANES), F32) for _ in range(4))
@@ -255,8 +251,6 @@
         ],
         compiler_params=pltpu.CompilerParams(vmem_limit_bytes=8 * 1024 * 1024),
     )(*map(distant, (jnp.transpose(stencil, (2, 0, 1)), step, shift)))
-    received, weights = lax.optimization_barrier((fetch_bins(bins), weights))
-    mine, theirs = swap_bins(received)
     high, low = pl.pallas_call(
         functools.partial(operands_kernel, dims),
         out_shape=[jax.ShapeDtypeStruct(operand, BF)] * 2,
@@ -269,9 +263,11 @@
         ],
         compiler_params=pltpu.CompilerParams(vmem_limit_bytes=12 * 1024 * 1024),
     )(distant(surface))
+    received, weights, high, low = lax.optimization_barrier((fetch_bins(bins), weights, high, low))
+    mine, theirs = swap_bins(received)
     return pl.pallas_call(
         functools.partial(levels_kernel, dims),
-        out_shape=jax.ShapeDtypeStruct((STRIPS * freqs + 1, lags.shape[0], grid // STRIPS, grid), F32),
+        out_shape=jax.ShapeDtypeStruct((STRIPS * freqs + 1, grid // STRIPS * lags.shape[0], grid), F32),
         in_specs=[far, far] + [vm] * 5,
         out_specs=vm,
         scratch_shapes=[pltpu.SMEM(lags.shape, jnp.int32), pltpu.VMEM((levels, grid, LANES), jnp.int32)]
@@ -456,9 +452,9 @@
     return mine, lax.ppermute(mine, "freq", [(0, 1), (1, 0)])
 
 
-def spread_image(image, freqs):
+def spread_image(image, freqs, lags):
     count, cores = lax.axis_size("depth"), lax.axis_size("freq")
-    lags, strip, grid = image.shape[1:]
+    grid = image.shape[2]
     block = image[:freqs] + lax.ppermute(image[freqs : 2 * freqs], "freq", [(0, 1), (1, 0)])
     total = None
     for turn in reversed(range(freqs)):
@@ -470,12 +466,13 @@
                 pairs.append((depth * cores + c, target * cores + z % STRIPS))
         part = lax.ppermute(block[turn], ("depth", "freq"), pairs)
         total = part if total is None else total + part
-    return total.reshape(1, lags, strip * grid)
+    total = jnp.transpose(total.reshape(-1, lags, grid), (1, 0, 2))
+    return total.reshape(1, lags, -1)
 
 
 def strip_body(surface, bins, stencil, phase_step, phase_shift, lags):
     image = run_levels(lags, surface[0], bins, stencil, phase_step, phase_shift, lax.axis_size("depth"))
-    return spread_image(image, surface.shape[1])
+    return spread_image(image, surface.shape[1], lags.shape[0])
 
 
 def body(surface, bins, stencil, phase_step, phase_shift, lags):

time: 42.5 us -> 41.1 us (0.967)
  waiting for transfers between devices: 8.36 us -> 6.3 us
  starting transfers between devices: 13.8 us -> 15 us
  local copies, waits for them, and re-layouts: 0.75 us -> 0.04 us
  other arithmetic: 0.08 us -> 0.73 us
  Pallas kernels: 19.2 us -> 18.6 us
    ppermute x4, waiting for transfers between devices: 1.72 us -> 0.01 us  [fetch_bins(): received.append(lax.ppermute(bins[0], ('depth', 'freq'), pairs))]
    ppermute x2, starting transfers between devices: 2.15 us -> 3.73 us  [spread_image(): part = lax.ppermute(block[turn], ('depth', 'freq'), pairs)]
    ppermute x2, waiting for transfers between devices: 5.13 us -> 3.96 us  [spread_image(): part = lax.ppermute(block[turn], ('depth', 'freq'), pairs)]
    ppermute x1, waiting for transfers between devices: 0.01 us -> 1.16 us  [swap_bins(): return (mine, lax.ppermute(mine, 'freq', [(0, 1), (1, 0)]))]
    ppermute x1, starting transfers between devices: 5.61 us -> 4.9 us  [swap_bins(): return (mine, lax.ppermute(mine, 'freq', [(0, 1), (1, 0)]))]
    reshape x1 -> x0, local copies, waits for them, and re-layouts: 0.71 us -> none  [spread_image(): return total.reshape(1, lags, strip * grid)]
    add x1, other arithmetic: 0.02 us -> 0.67 us  [spread_image(): total = part if total is None else total + part]
    pallas_call x1, Pallas kernels: 2.98 us -> 2.39 us  [run_levels(): pl.pallas_call(functools.partial(operands_kernel, dims), out_shape=[jax.S...]
  transfers between devices with their start and end apart: 8 -> 8, of which waited for: 5 -> 4; matrix products, arithmetic and copies ran while one was open for 0% -> 0% of each run, Pallas kernels for 13% -> 12%
where the time goes in v5:
time: 41.1 us; the launch traced here: 40.8 us
  Pallas kernels  18.6 us (45%)
  starting transfers between devices  15 us (36%)
  waiting for transfers between devices  6.3 us (15%)
  other arithmetic  0.73 us (2%)
    pallas_call x1, Pallas kernels, run_levels(): pl.pallas_call(functools.partial(levels_kernel, dims), out_shape=jax.Shap...  13.7 us
    ppermute x4, starting transfers between devices, fetch_bins(): received.append(lax.ppermute(bins[0], ('depth', 'freq'), pairs))  5.97 us
    ppermute x1, starting transfers between devices, swap_bins(): return (mine, lax.ppermute(mine, 'freq', [(0, 1), (1, 0)]))  4.9 us
    ppermute x2, waiting for transfers between devices, spread_image(): part = lax.ppermute(block[turn], ('depth', 'freq'), pairs)  3.96 us
    ppermute x2, starting transfers between devices, spread_image(): part = lax.ppermute(block[turn], ('depth', 'freq'), pairs)  3.73 us
    pallas_call x1, Pallas kernels, run_levels(): pl.pallas_call(functools.partial(weights_kernel, dims), out_shape=jax.Sha...  2.48 us
    pallas_call x1, Pallas kernels, run_levels(): pl.pallas_call(functools.partial(operands_kernel, dims), out_shape=[jax.S...  2.39 us
    ppermute x1, waiting for transfers between devices, swap_bins(): return (mine, lax.ppermute(mine, 'freq', [(0, 1), (1, 0)]))  1.16 us
  transfers between devices with their start and end apart: 8, of which 4 were waited for; matrix products, arithmetic and copies ran while one was open for 0% of the time, Pallas kernels for 12%

profile of v5, /device:TPU:1, one launch (start us, length us, event | category | flops | bytes accessed | tf_op | source)
XLA Modules:
  0.0 40.8 jit_solution(13753774247522791320)
XLA Ops:
  0.0 0.7 %collective-permute-start.3 = (s32[128,128]{1,0:T(8,128)}, s32[128,128]{1,0:T(8,128)S(1)}, u32[]{:S(2)}, u32[]{:S(2)}) collective-permute-start(s32[128,128]{1,0:T(8,128)} %bitcast.17), channel_id=1, source_target_pairs={{0,8},{2,10},{4,12},{6,14},{8,0},{10,2},{12,4},{14,6},{16,24},{18,... | collective-permute-start | bytes 196616 | tf_op jit(solution)/shard_map/ppermute | solution.py:446
  0.7 5.1 %collective-permute-start.2 = (s32[128,128]{1,0:T(8,128)}, s32[128,128]{1,0:T(8,128)S(1)}, u32[]{:S(2)}, u32[]{:S(2)}) collective-permute-start(s32[128,128]{1,0:T(8,128)} %bitcast.18), channel_id=1, source_target_pairs={{0,6},{2,8},{4,10},{6,12},{8,14},{10,0},{12,2},{14,4},{1,15},{3,1}... | collective-permute-start | bytes 196616 | tf_op jit(solution)/shard_map/ppermute | solution.py:446
  5.8 0.2 collective-permute-start.1
  6.0 0.0 collective-permute-start
  6.0 2.4 %shard_map.65 = (bf16[3,13,144,256]{3,2,1,0:T(8,128)(2,1)S(1)}, bf16[3,13,144,256]{3,2,1,0:T(8,128)(2,1)S(1)}) custom-call(f32[2,2,128,256]{3,2,1,0:T(8,128)} %bitcast.16), custom_call_target="tpu_custom_call" | custom-call | tf_op jit(solution)/shard_map/pallas_call | solution.py:254
  8.4 2.5 %shard_map.64.weights = bf16[3,128,1280]{2,1,0:T(8,128)(2,1)S(1)} custom-call(f32[5,2,8]{2,1,0:T(2,128)} %bitcast.25, f32[2,8]{1,0:T(2,128)} %step_far.1, f32[2,8]{1,0:T(2,128)} %shift_far.1), custom_call_target="tpu_custom_call" | custom-call | tf_op jit(solution)/shard_map/pallas_call | solution.py:240
  10.9 0.0 collective-permute-done.3
  10.9 0.0 collective-permute-done.2
  10.9 0.0 collective-permute-done.1
  10.9 0.0 collective-permute-done
  10.9 4.9 %collective-permute-start.4 = (s32[4,128,128]{2,1,0:T(8,128)S(1)}, s32[4,128,128]{2,1,0:T(8,128)S(1)}, u32[]{:S(2)}, u32[]{:S(2)}) collective-permute-start(s32[4,128,128]{2,1,0:T(8,128)S(1)} %pad_add_fusion.mine), channel_id=1, source_target_pairs={{0,1},{1,0},{2,3},{3,2},{4,5},{5,4},{6,7},{7,6},{8,9},{9,8},{10,11... | collective-permute-start | bytes 786440 | tf_op jit(solution)/shard_map/ppermute | solution.py:452
  15.8 1.2 %collective-permute-done.4.theirs = s32[4,128,128]{2,1,0:T(8,128)S(1)} collective-permute-done((s32[4,128,128]{2,1,0:T(8,128)S(1)}, s32[4,128,128]{2,1,0:T(8,128)S(1)}, u32[]{:S(2)}, u32[]{:S(2)}) %collective-permute-start.4) | collective-permute-done | bytes 262176 | tf_op jit(solution)/shard_map/ppermute | solution.py:452
  17.0 13.7 %shard_map.66 = f32[5,256,128]{2,1,0:T(8,128)S(1)} custom-call(s32[4]{0:T(128)} %lags_far.1, s32[1,128,128]{2,1,0:T(8,128)} %own.1, s32[4,128,128]{2,1,0:T(8,128)S(1)} %pad_add_fusion.mine, s32[4,128,128]{2,1,0:T(8,128)S(1)} %collective-permute-done.4.theirs, bf16[3,128,1280]{2,1,0:T(8,128)(2,1)S(1)} %shard_map.64.weights, ...), custom_call_target="tpu_custom_call" | custom-call | tf_op jit(solution)/shard_map/pallas_call | solution.py:268
  30.8 0.4 %collective-permute-start.5 = (f32[2,256,128]{2,1,0:T(8,128)S(1)}, f32[2,256,128]{2,1,0:T(8,128)S(1)}, u32[]{:S(2)}, u32[]{:S(2)}) collective-permute-start(f32[2,256,128]{2,1,0:T(8,128)S(1)} %slice.17), channel_id=1, source_target_pairs={{0,1},{1,0},{2,3},{3,2},{4,5},{5,4},{6,7},{7,6},{8,9},{9,8},{10,11... | collective-permute-start | bytes 786440 | tf_op jit(solution)/shard_map/ppermute | solution.py:458
  31.2 1.2 %collective-permute-done.5 = f32[2,256,128]{2,1,0:T(8,128)S(1)} collective-permute-done((f32[2,256,128]{2,1,0:T(8,128)S(1)}, f32[2,256,128]{2,1,0:T(8,128)S(1)}, u32[]{:S(2)}, u32[]{:S(2)}) %collective-permute-start.5) | collective-permute-done | bytes 262176 | tf_op jit(solution)/shard_map/ppermute | solution.py:458
  32.4 1.9 %collective-permute-start.7 = (f32[256,128]{1,0:T(8,128)S(1)}, f32[256,128]{1,0:T(8,128)S(1)}, u32[]{:S(2)}, u32[]{:S(2)}) collective-permute-start(f32[256,128]{1,0:T(8,128)S(1)} %get-tuple-element.23), channel_id=1, source_target_pairs={{0,0},{1,4},{2,2},{3,6},{4,1},{5,5},{6,3},{7,7},{8,8},{9,12},{10,1... | collective-permute-start | bytes 393224 | tf_op jit(solution)/shard_map/ppermute | solution.py:467
  34.4 1.8 %collective-permute-start.6 = (f32[256,128]{1,0:T(8,128)S(1)}, f32[256,128]{1,0:T(8,128)S(1)}, u32[]{:S(2)}, u32[]{:S(2)}) collective-permute-start(f32[256,128]{1,0:T(8,128)S(1)} %get-tuple-element.24), channel_id=1, source_target_pairs={{0,2},{1,6},{2,0},{3,4},{4,3},{5,7},{6,1},{7,5},{8,10},{9,14},{10,... | collective-permute-start | bytes 393224 | tf_op jit(solution)/shard_map/ppermute | solution.py:467
  36.2 2.5 %collective-permute-done.7 = f32[256,128]{1,0:T(8,128)S(1)} collective-permute-done((f32[256,128]{1,0:T(8,128)S(1)}, f32[256,128]{1,0:T(8,128)S(1)}, u32[]{:S(2)}, u32[]{:S(2)}) %collective-permute-start.7) | collective-permute-done | bytes 131104 | tf_op jit(solution)/shard_map/ppermute | solution.py:467
  38.7 1.4 %collective-permute-done.6 = f32[256,128]{1,0:T(8,128)S(1)} collective-permute-done((f32[256,128]{1,0:T(8,128)S(1)}, f32[256,128]{1,0:T(8,128)S(1)}, u32[]{:S(2)}, u32[]{:S(2)}) %collective-permute-start.6) | collective-permute-done | bytes 131104 | tf_op jit(solution)/shard_map/ppermute | solution.py:467
  40.1 0.7 %add.7 = f32[256,128]{1,0:T(8,128)} add(f32[256,128]{1,0:T(8,128)S(1)} %collective-permute-done.6, f32[256,128]{1,0:T(8,128)S(1)} %collective-permute-done.7) | non-fusion elementwise | flops 32768 | bytes 393216 | tf_op jit(solution)/shard_map/add | solution.py:468
  (4 shorter events, 0.1 us)
Async XLA Ops:
  0.0 10.9 %collective-permute-start.3 = (s32[128,128]{1,0:T(8,128)}, s32[128,128]{1,0:T(8,128)S(1)}, u32[]{:S(2)}, u32[]{:S(2)}) collective-permute-start(s32[128,128]{1,0:T(8,128)} %bitcast.17), channel_id=1, source_target_pairs={{0,8},{2,10},{4,12},{6,14},{8,0},{10,2},{12,4},{14,6},{16,24},{18,... | collective-permute-start | bytes 196616 | tf_op jit(solution)/shard_map/ppermute | solution.py:446
  0.7 10.2 %collective-permute-start.2 = (s32[128,128]{1,0:T(8,128)}, s32[128,128]{1,0:T(8,128)S(1)}, u32[]{:S(2)}, u32[]{:S(2)}) collective-permute-start(s32[128,128]{1,0:T(8,128)} %bitcast.18), channel_id=1, source_target_pairs={{0,6},{2,8},{4,10},{6,12},{8,14},{10,0},{12,2},{14,4},{1,15},{3,1}... | collective-permute-start | bytes 196616 | tf_op jit(solution)/shard_map/ppermute | solution.py:446
  5.8 5.1 %collective-permute-start.1 = (s32[128,128]{1,0:T(8,128)}, s32[128,128]{1,0:T(8,128)S(1)}, u32[]{:S(2)}, u32[]{:S(2)}) collective-permute-start(s32[128,128]{1,0:T(8,128)} %bitcast.19), channel_id=1, source_target_pairs={{0,4},{2,6},{4,8},{6,10},{8,12},{10,14},{12,0},{14,2},{1,13},{3,15... | collective-permute-start | bytes 196616 | tf_op jit(solution)/shard_map/ppermute | solution.py:446
  6.0 4.9 %collective-permute-start = (s32[128,128]{1,0:T(8,128)}, s32[128,128]{1,0:T(8,128)S(1)}, u32[]{:S(2)}, u32[]{:S(2)}) collective-permute-start(s32[128,128]{1,0:T(8,128)} %bitcast.20), channel_id=1, source_target_pairs={{0,2},{2,4},{4,6},{6,8},{8,10},{10,12},{12,14},{14,0},{1,11},{3,13... | collective-permute-start | bytes 196616 | tf_op jit(solution)/shard_map/ppermute | solution.py:446
  10.9 6.1 %collective-permute-start.4 = (s32[4,128,128]{2,1,0:T(8,128)S(1)}, s32[4,128,128]{2,1,0:T(8,128)S(1)}, u32[]{:S(2)}, u32[]{:S(2)}) collective-permute-start(s32[4,128,128]{2,1,0:T(8,128)S(1)} %pad_add_fusion.mine), channel_id=1, source_target_pairs={{0,1},{1,0},{2,3},{3,2},{4,5},{5,4},{6,7},{7,6},{8,9},{9,8},{10,11... | collective-permute-start | bytes 786440 | tf_op jit(solution)/shard_map/ppermute | solution.py:452
  30.8 1.6 %collective-permute-start.5 = (f32[2,256,128]{2,1,0:T(8,128)S(1)}, f32[2,256,128]{2,1,0:T(8,128)S(1)}, u32[]{:S(2)}, u32[]{:S(2)}) collective-permute-start(f32[2,256,128]{2,1,0:T(8,128)S(1)} %slice.17), channel_id=1, source_target_pairs={{0,1},{1,0},{2,3},{3,2},{4,5},{5,4},{6,7},{7,6},{8,9},{9,8},{10,11... | collective-permute-start | bytes 786440 | tf_op jit(solution)/shard_map/ppermute | solution.py:458
  32.4 6.3 %collective-permute-start.7 = (f32[256,128]{1,0:T(8,128)S(1)}, f32[256,128]{1,0:T(8,128)S(1)}, u32[]{:S(2)}, u32[]{:S(2)}) collective-permute-start(f32[256,128]{1,0:T(8,128)S(1)} %get-tuple-element.23), channel_id=1, source_target_pairs={{0,0},{1,4},{2,2},{3,6},{4,1},{5,5},{6,3},{7,7},{8,8},{9,12},{10,1... | collective-permute-start | bytes 393224 | tf_op jit(solution)/shard_map/ppermute | solution.py:467
  34.4 5.8 %collective-permute-start.6 = (f32[256,128]{1,0:T(8,128)S(1)}, f32[256,128]{1,0:T(8,128)S(1)}, u32[]{:S(2)}, u32[]{:S(2)}) collective-permute-start(f32[256,128]{1,0:T(8,128)S(1)} %get-tuple-element.24), channel_id=1, source_target_pairs={{0,2},{1,6},{2,0},{3,4},{4,3},{5,7},{6,1},{7,5},{8,10},{9,14},{10,... | collective-permute-start | bytes 393224 | tf_op jit(solution)/shard_map/ppermute | solution.py:467

commit v6 on v5

--- a/solution.py
+++ b/solution.py
@@ -263,7 +263,7 @@
         ],
         compiler_params=pltpu.CompilerParams(vmem_limit_bytes=12 * 1024 * 1024),
     )(distant(surface))
-    received, weights, high, low = lax.optimization_barrier((fetch_bins(bins), weights, high, low))
+    received, weights, high, low = lax.optimization_barrier((fetch_bins(bins, STRIPS * freqs), weights, high, low))
     mine, theirs = swap_bins(received)
     return pl.pallas_call(
         functools.partial(levels_kernel, dims),
@@ -433,7 +433,7 @@
     return lax.psum_scatter(image_part, "freq", scatter_dimension=2, tiled=True)
 
 
-def fetch_bins(bins):
+def fetch_bins(bins, group):
     count, cores = lax.axis_size("depth"), lax.axis_size("freq")
     rounds = -(-(count - 1) // cores)
     received = []
@@ -441,8 +441,10 @@
         pairs = []
         for own in range(cores):
             turn = 1 + number + own * rounds
-            if turn < count:
-                pairs += [(place * cores + own, (place + turn) % count * cores + own) for place in range(count)]
+            for place in range(count if turn < count else 0):
+                target = (place + turn) % count
+                if target // group >= place // group:
+                    pairs.append((place * cores + own, target * cores + own))
         received.append(lax.ppermute(bins[0], ("depth", "freq"), pairs))
     return received
 

time: 41.1 us -> 45.4 us (1.10)
  starting transfers between devices: 15 us -> 19.3 us
    ppermute x4, starting transfers between devices: 5.97 us -> 11.7 us  [fetch_bins(): received.append(lax.ppermute(bins[0], ('depth', 'freq'), pairs))]
    ppermute x1, starting transfers between devices: 4.9 us -> 3.22 us  [swap_bins(): return (mine, lax.ppermute(mine, 'freq', [(0, 1), (1, 0)]))]
  transfers between devices with their start and end apart: 8 -> 8, of which waited for: 4 -> 4; matrix products, arithmetic and copies ran while one was open for 0% -> 0% of each run, Pallas kernels for 12% -> 11%
where the time goes in v6:
time: 45.4 us; the launch traced here: 45.1 us
  starting transfers between devices  19.3 us (43%)
  Pallas kernels  18.6 us (41%)
  waiting for transfers between devices  6.3 us (14%)
  other arithmetic  0.73 us (2%)
    pallas_call x1, Pallas kernels, run_levels(): pl.pallas_call(functools.partial(levels_kernel, dims), out_shape=jax.Shap...  13.7 us
    ppermute x4, starting transfers between devices, fetch_bins(): received.append(lax.ppermute(bins[0], ('depth', 'freq'), pairs))  11.7 us
    ppermute x2, starting transfers between devices, spread_image(): part = lax.ppermute(block[turn], ('depth', 'freq'), pairs)  3.99 us
    ppermute x2, waiting for transfers between devices, spread_image(): part = lax.ppermute(block[turn], ('depth', 'freq'), pairs)  3.96 us
    ppermute x1, starting transfers between devices, swap_bins(): return (mine, lax.ppermute(mine, 'freq', [(0, 1), (1, 0)]))  3.22 us
    pallas_call x1, Pallas kernels, run_levels(): pl.pallas_call(functools.partial(weights_kernel, dims), out_shape=jax.Sha...  2.48 us
    pallas_call x1, Pallas kernels, run_levels(): pl.pallas_call(functools.partial(operands_kernel, dims), out_shape=[jax.S...  2.41 us
    ppermute x1, waiting for transfers between devices, spread_image(): lax.ppermute(image[freqs:2 * freqs], 'freq', [(0, 1), (1, 0)])  1.16 us
  transfers between devices with their start and end apart: 8, of which 4 were waited for; matrix products, arithmetic and copies ran while one was open for 0% of the time, Pallas kernels for 11%

profile of v6, /device:TPU:1, one launch (start us, length us, event | category | flops | bytes accessed | tf_op | source)
XLA Modules:
  0.0 45.1 jit_solution(10403692790001054970)
XLA Ops:
  0.0 0.7 %collective-permute-start.3 = (s32[128,128]{1,0:T(8,128)}, s32[128,128]{1,0:T(8,128)S(1)}, u32[]{:S(2)}, u32[]{:S(2)}) collective-permute-start(s32[128,128]{1,0:T(8,128)} %bitcast.17), channel_id=1, source_target_pairs={{0,8},{2,10},{4,12},{6,14},{16,24},{18,26},{20,28},{22,30}} | collective-permute-start | bytes 196616 | tf_op jit(solution)/shard_map/ppermute | solution.py:448
  0.7 7.0 %collective-permute-start.2 = (s32[128,128]{1,0:T(8,128)}, s32[128,128]{1,0:T(8,128)S(1)}, u32[]{:S(2)}, u32[]{:S(2)}) collective-permute-start(s32[128,128]{1,0:T(8,128)} %bitcast.18), channel_id=1, source_target_pairs={{0,6},{2,8},{4,10},{6,12},{8,14},{1,15},{3,1},{5,3},{7,5},{11,9},{... | collective-permute-start | bytes 196616 | tf_op jit(solution)/shard_map/ppermute | solution.py:448
  7.7 2.1 %collective-permute-start.1 = (s32[128,128]{1,0:T(8,128)}, s32[128,128]{1,0:T(8,128)S(1)}, u32[]{:S(2)}, u32[]{:S(2)}) collective-permute-start(s32[128,128]{1,0:T(8,128)} %bitcast.19), channel_id=1, source_target_pairs={{0,4},{2,6},{4,8},{6,10},{8,12},{10,14},{1,13},{3,15},{5,1},{7,3},... | collective-permute-start | bytes 196616 | tf_op jit(solution)/shard_map/ppermute | solution.py:448
  9.8 1.9 %collective-permute-start = (s32[128,128]{1,0:T(8,128)}, s32[128,128]{1,0:T(8,128)S(1)}, u32[]{:S(2)}, u32[]{:S(2)}) collective-permute-start(s32[128,128]{1,0:T(8,128)} %bitcast.20), channel_id=1, source_target_pairs={{0,2},{2,4},{4,6},{6,8},{8,10},{10,12},{12,14},{1,11},{3,13},{5,15... | collective-permute-start | bytes 196616 | tf_op jit(solution)/shard_map/ppermute | solution.py:448
  11.7 2.4 %shard_map.65 = (bf16[3,13,144,256]{3,2,1,0:T(8,128)(2,1)S(1)}, bf16[3,13,144,256]{3,2,1,0:T(8,128)(2,1)S(1)}) custom-call(f32[2,2,128,256]{3,2,1,0:T(8,128)} %bitcast.16), custom_call_target="tpu_custom_call" | custom-call | tf_op jit(solution)/shard_map/pallas_call | solution.py:254
  14.1 2.5 %shard_map.64.weights = bf16[3,128,1280]{2,1,0:T(8,128)(2,1)S(1)} custom-call(f32[5,2,8]{2,1,0:T(2,128)} %bitcast.25, f32[2,8]{1,0:T(2,128)} %step_far.1, f32[2,8]{1,0:T(2,128)} %shift_far.1), custom_call_target="tpu_custom_call" | custom-call | tf_op jit(solution)/shard_map/pallas_call | solution.py:240
  16.6 0.0 collective-permute-done.3
  16.6 0.0 collective-permute-done.2
  16.6 0.0 collective-permute-done.1
  16.6 0.0 collective-permute-done
  16.7 3.2 %collective-permute-start.4 = (s32[4,128,128]{2,1,0:T(8,128)S(1)}, s32[4,128,128]{2,1,0:T(8,128)S(1)}, u32[]{:S(2)}, u32[]{:S(2)}) collective-permute-start(s32[4,128,128]{2,1,0:T(8,128)S(1)} %pad_add_fusion.mine), channel_id=1, source_target_pairs={{0,1},{1,0},{2,3},{3,2},{4,5},{5,4},{6,7},{7,6},{8,9},{9,8},{10,11... | collective-permute-start | bytes 786440 | tf_op jit(solution)/shard_map/ppermute | solution.py:454
  19.9 1.2 %collective-permute-done.4.theirs = s32[4,128,128]{2,1,0:T(8,128)S(1)} collective-permute-done((s32[4,128,128]{2,1,0:T(8,128)S(1)}, s32[4,128,128]{2,1,0:T(8,128)S(1)}, u32[]{:S(2)}, u32[]{:S(2)}) %collective-permute-start.4) | collective-permute-done | bytes 262176 | tf_op jit(solution)/shard_map/ppermute | solution.py:454
  21.0 13.7 %shard_map.66 = f32[5,256,128]{2,1,0:T(8,128)S(1)} custom-call(s32[4]{0:T(128)} %lags_far.1, s32[1,128,128]{2,1,0:T(8,128)} %own.1, s32[4,128,128]{2,1,0:T(8,128)S(1)} %pad_add_fusion.mine, s32[4,128,128]{2,1,0:T(8,128)S(1)} %collective-permute-done.4.theirs, bf16[3,128,1280]{2,1,0:T(8,128)(2,1)S(1)} %shard_map.64.weights, ...), custom_call_target="tpu_custom_call" | custom-call | tf_op jit(solution)/shard_map/pallas_call | solution.py:268
  34.8 0.4 collective-permute-start.5
  35.3 1.2 %collective-permute-done.5 = f32[2,256,128]{2,1,0:T(8,128)S(1)} collective-permute-done((f32[2,256,128]{2,1,0:T(8,128)S(1)}, f32[2,256,128]{2,1,0:T(8,128)S(1)}, u32[]{:S(2)}, u32[]{:S(2)}) %collective-permute-start.5) | collective-permute-done | bytes 262176 | tf_op jit(solution)/shard_map/ppermute | solution.py:460
  36.5 1.9 %collective-permute-start.7 = (f32[256,128]{1,0:T(8,128)S(1)}, f32[256,128]{1,0:T(8,128)S(1)}, u32[]{:S(2)}, u32[]{:S(2)}) collective-permute-start(f32[256,128]{1,0:T(8,128)S(1)} %get-tuple-element.23), channel_id=1, source_target_pairs={{0,0},{1,4},{2,2},{3,6},{4,1},{5,5},{6,3},{7,7},{8,8},{9,12},{10,1... | collective-permute-start | bytes 393224 | tf_op jit(solution)/shard_map/ppermute | solution.py:469
  38.4 2.1 %collective-permute-start.6 = (f32[256,128]{1,0:T(8,128)S(1)}, f32[256,128]{1,0:T(8,128)S(1)}, u32[]{:S(2)}, u32[]{:S(2)}) collective-permute-start(f32[256,128]{1,0:T(8,128)S(1)} %get-tuple-element.24), channel_id=1, source_target_pairs={{0,2},{1,6},{2,0},{3,4},{4,3},{5,7},{6,1},{7,5},{8,10},{9,14},{10,... | collective-permute-start | bytes 393224 | tf_op jit(solution)/shard_map/ppermute | solution.py:469
  40.5 2.3 %collective-permute-done.7 = f32[256,128]{1,0:T(8,128)S(1)} collective-permute-done((f32[256,128]{1,0:T(8,128)S(1)}, f32[256,128]{1,0:T(8,128)S(1)}, u32[]{:S(2)}, u32[]{:S(2)}) %collective-permute-start.7) | collective-permute-done | bytes 131104 | tf_op jit(solution)/shard_map/ppermute | solution.py:469
  42.8 1.7 %collective-permute-done.6 = f32[256,128]{1,0:T(8,128)S(1)} collective-permute-done((f32[256,128]{1,0:T(8,128)S(1)}, f32[256,128]{1,0:T(8,128)S(1)}, u32[]{:S(2)}, u32[]{:S(2)}) %collective-permute-start.6) | collective-permute-done | bytes 131104 | tf_op jit(solution)/shard_map/ppermute | solution.py:469
  44.5 0.7 %add.7 = f32[256,128]{1,0:T(8,128)} add(f32[256,128]{1,0:T(8,128)S(1)} %collective-permute-done.6, f32[256,128]{1,0:T(8,128)S(1)} %collective-permute-done.7) | non-fusion elementwise | flops 32768 | bytes 393216 | tf_op jit(solution)/shard_map/add | solution.py:470
  (4 shorter events, 0.1 us)
Async XLA Ops:
  0.0 16.6 %collective-permute-start.3 = (s32[128,128]{1,0:T(8,128)}, s32[128,128]{1,0:T(8,128)S(1)}, u32[]{:S(2)}, u32[]{:S(2)}) collective-permute-start(s32[128,128]{1,0:T(8,128)} %bitcast.17), channel_id=1, source_target_pairs={{0,8},{2,10},{4,12},{6,14},{16,24},{18,26},{20,28},{22,30}} | collective-permute-start | bytes 196616 | tf_op jit(solution)/shard_map/ppermute | solution.py:448
  0.7 15.9 %collective-permute-start.2 = (s32[128,128]{1,0:T(8,128)}, s32[128,128]{1,0:T(8,128)S(1)}, u32[]{:S(2)}, u32[]{:S(2)}) collective-permute-start(s32[128,128]{1,0:T(8,128)} %bitcast.18), channel_id=1, source_target_pairs={{0,6},{2,8},{4,10},{6,12},{8,14},{1,15},{3,1},{5,3},{7,5},{11,9},{... | collective-permute-start | bytes 196616 | tf_op jit(solution)/shard_map/ppermute | solution.py:448
  7.7 8.9 %collective-permute-start.1 = (s32[128,128]{1,0:T(8,128)}, s32[128,128]{1,0:T(8,128)S(1)}, u32[]{:S(2)}, u32[]{:S(2)}) collective-permute-start(s32[128,128]{1,0:T(8,128)} %bitcast.19), channel_id=1, source_target_pairs={{0,4},{2,6},{4,8},{6,10},{8,12},{10,14},{1,13},{3,15},{5,1},{7,3},... | collective-permute-start | bytes 196616 | tf_op jit(solution)/shard_map/ppermute | solution.py:448
  9.8 6.9 %collective-permute-start = (s32[128,128]{1,0:T(8,128)}, s32[128,128]{1,0:T(8,128)S(1)}, u32[]{:S(2)}, u32[]{:S(2)}) collective-permute-start(s32[128,128]{1,0:T(8,128)} %bitcast.20), channel_id=1, source_target_pairs={{0,2},{2,4},{4,6},{6,8},{8,10},{10,12},{12,14},{1,11},{3,13},{5,15... | collective-permute-start | bytes 196616 | tf_op jit(solution)/shard_map/ppermute | solution.py:448
  16.7 4.4 %collective-permute-start.4 = (s32[4,128,128]{2,1,0:T(8,128)S(1)}, s32[4,128,128]{2,1,0:T(8,128)S(1)}, u32[]{:S(2)}, u32[]{:S(2)}) collective-permute-start(s32[4,128,128]{2,1,0:T(8,128)S(1)} %pad_add_fusion.mine), channel_id=1, source_target_pairs={{0,1},{1,0},{2,3},{3,2},{4,5},{5,4},{6,7},{7,6},{8,9},{9,8},{10,11... | collective-permute-start | bytes 786440 | tf_op jit(solution)/shard_map/ppermute | solution.py:454
  34.8 1.6 %collective-permute-start.5 = (f32[2,256,128]{2,1,0:T(8,128)S(1)}, f32[2,256,128]{2,1,0:T(8,128)S(1)}, u32[]{:S(2)}, u32[]{:S(2)}) collective-permute-start(f32[2,256,128]{2,1,0:T(8,128)S(1)} %slice.17), channel_id=1, source_target_pairs={{0,1},{1,0},{2,3},{3,2},{4,5},{5,4},{6,7},{7,6},{8,9},{9,8},{10,11... | collective-permute-start | bytes 786440 | tf_op jit(solution)/shard_map/ppermute | solution.py:460
  36.5 6.3 %collective-permute-start.7 = (f32[256,128]{1,0:T(8,128)S(1)}, f32[256,128]{1,0:T(8,128)S(1)}, u32[]{:S(2)}, u32[]{:S(2)}) collective-permute-start(f32[256,128]{1,0:T(8,128)S(1)} %get-tuple-element.23), channel_id=1, source_target_pairs={{0,0},{1,4},{2,2},{3,6},{4,1},{5,5},{6,3},{7,7},{8,8},{9,12},{10,1... | collective-permute-start | bytes 393224 | tf_op jit(solution)/shard_map/ppermute | solution.py:469
  38.4 6.0 %collective-permute-start.6 = (f32[256,128]{1,0:T(8,128)S(1)}, f32[256,128]{1,0:T(8,128)S(1)}, u32[]{:S(2)}, u32[]{:S(2)}) collective-permute-start(f32[256,128]{1,0:T(8,128)S(1)} %get-tuple-element.24), channel_id=1, source_target_pairs={{0,2},{1,6},{2,0},{3,4},{4,3},{5,7},{6,1},{7,5},{8,10},{9,14},{10,... | collective-permute-start | bytes 393224 | tf_op jit(solution)/shard_map/ppermute | solution.py:469
